TPU v7x, 32 devices: a whole 2x2x4 slice. The times are simulated.
32 devices in a mesh: fsdp: 8 (over z, x), ctx: 2 (over y), tp: 2 (over core).
Axes of the slice: x: 2, y: 2, z: 4, core: 2. Of those that a mesh axis runs over, the one named last changes fastest.
Arguments:
- tokens: bfloat16 [16, 1024, 1024], P('fsdp', 'ctx'), may hold values from -6 to 6
- out_grad: bfloat16 [16, 1024, 1024], P('fsdp', 'ctx'), may hold values from -6 to 6
- norm_gains: bfloat16 [2, 1024], P(None, ('fsdp', 'ctx')), may hold values from 0.5 to 1.5
- query_weight: bfloat16 [1024, 512], P(('fsdp', 'ctx'), 'tp'), may hold values from -0.25 to 0.25
- key_value_matrix: bfloat16 [1024, 2, 128], P(('fsdp', 'ctx'), 'tp'), may hold values from -0.1875 to 0.1875
- output_weight: bfloat16 [512, 1024], P('tp', ('fsdp', 'ctx')), may hold values from -0.75 to 0.75
- mixer_weight: bfloat16 [1024, 24, 128], P(('fsdp', 'ctx'), 'tp'), may hold values from -0.1875 to 0.1875
- state_weight: bfloat16 [1024, 256], P(('fsdp', 'ctx')), may hold values from -0.1875 to 0.1875
- step_weight: bfloat16 [1024, 24], P(('fsdp', 'ctx'), 'tp'), may hold values from -0.1875 to 0.1875
- conv_inner: bfloat16 [5, 1536], P(None, 'tp'), may hold values from -2.5 to 2.5
- conv_state: bfloat16 [5, 256], replicated, may hold values from -2.5 to 2.5
- step_bias: bfloat16 [24], P('tp'), may hold values from -4.5 to -3
- decay_log: bfloat16 [24], P('tp'), may hold values from -2.5 to 1
- skip_scale: bfloat16 [24], P('tp'), may hold values from 0.5 to 1.5
- gated_gain: bfloat16 [1536], P('tp'), may hold values from 0.5 to 1.5
- mamba_weight: bfloat16 [1536, 1024], P('tp', ('fsdp', 'ctx')), may hold values from -0.15625 to 0.15625
- gateup_weight: bfloat16 [1024, 2, 2048], P(('fsdp', 'ctx'), None, 'tp'), may hold values from -0.1875 to 0.1875
- down_weight: bfloat16 [2048, 1024], P('tp', ('fsdp', 'ctx')), may hold values from -0.125 to 0.125
Outputs:
- layer_out: bfloat16 [16, 1024, 1024], P('fsdp', 'ctx', 'tp')
- tokens_grad: float32 [16, 1024, 1024], P('fsdp', 'ctx')
- norm_gains_grad: float32 [2, 1024], P(None, ('fsdp', 'ctx'))
- query_weight_grad: float32 [1024, 512], P(('fsdp', 'ctx'), 'tp')
- keyvalue_weight_grad: float32 [1024, 2, 128], P(('fsdp', 'ctx'), 'tp')
- output_weight_grad: float32 [512, 1024], P('tp', ('fsdp', 'ctx'))
- mixer_weight_grad: float32 [1024, 24, 128], P(('fsdp', 'ctx'), 'tp')
- state_weight_grad: float32 [1024, 256], P(('fsdp', 'ctx'))
- step_weight_grad: float32 [1024, 24], P(('fsdp', 'ctx'), 'tp')
- conv_inner_grad: float32 [5, 1536], P(None, 'tp')
- conv_state_grad: float32 [5, 256], replicated
- step_bias_grad: float32 [24], P('tp')
- decay_log_grad: float32 [24], P('tp')
- skip_scale_grad: float32 [24], P('tp')
- gated_gain_grad: float32 [1536], P('tp')
- mamba_weight_grad: float32 [1536, 1024], P('tp', ('fsdp', 'ctx'))
- gateup_weight_grad: float32 [1024, 2, 2048], P(('fsdp', 'ctx'), None, 'tp')
- down_weight_grad: float32 [2048, 1024], P('tp', ('fsdp', 'ctx'))
All inputs are finite; a program needn't handle non-finite values.
Results may differ from a plain program's by a relative error of at most 0.017.
Values may be sent and summed in bfloat16 or wider, within the bound.
No kernel may reach another device: no remote copies, remote signals or barrier semaphores. Data moves between devices by JAX's collectives and lax.ppermute only.
A program may use at most 320 MiB of HBM per device.

v0:
```python
import jax
import jax.numpy as jnp
from jax import lax
from jax.sharding import PartitionSpec as P

HEAD_DIMENSION = 64
MP = 64
NS = 128
SPAN = 128


EPSILON = 1e-05
HIGHEST = lax.Precision.HIGHEST
MASKED = -1e30
ROPE_BASE = 10000.0


def from_behind(block, axis, distance):
    devices = range(lax.axis_size(axis))
    route = [(i - distance, i) for i in devices if i - distance in devices]
    return lax.ppermute(block, axis, route)


def prefix(value, axis, combine, identity):
    length, position = (lax.axis_size(axis), lax.axis_index(axis))
    everything = jax.tree.map(
        lambda part, kind: lax.all_gather(part.astype(kind), axis),
        value,
        (jnp.bfloat16, jnp.bfloat16),
    )
    start = jax.tree.map(
        lambda part, zero: jnp.broadcast_to(jnp.asarray(zero, part.dtype), part.shape),
        value,
        identity,
    )

    def lap(k, before):
        reached = k < position
        new = combine(
            before, jax.tree.map(lambda part, own: part[k].astype(own.dtype), everything, value)
        )
        return jax.tree.map(lambda a, b: jnp.where(reached, a, b), new, before)

    return lax.fori_loop(0, length, lap, start)


def prefix_2(value, axis, join, neutral):
    count = lax.axis_size(axis)
    place = lax.axis_index(axis)
    ahead = count - 1 - place
    gathered = jax.tree.map(
        lambda a, kind: lax.all_gather(a.astype(kind), axis),
        value,
        jax.tree.map(lambda a: jnp.bfloat16 if a.dtype == jnp.float32 else a.dtype, value),
    )
    state = jax.tree.map(lambda a, e: jnp.zeros_like(a) + jnp.asarray(e, a.dtype), value, neutral)

    def one(lap, state):
        source = count - 1 - lap
        return join(
            state,
            jax.tree.map(
                lambda a, own: lax.dynamic_index_in_dim(a, source, 0, False).astype(own.dtype),
                gathered,
                value,
            ),
        )

    return lax.fori_loop(0, ahead, one, state)


def rms_inverse(values):
    return lax.rsqrt(jnp.mean(values * values, axis=-1, keepdims=True) + EPSILON)


def norm_back(values, inverse, gain_values, gradient):
    weighted = gradient * gain_values
    inner_sum = jnp.sum(weighted * values, axis=-1, keepdims=True) / values.shape[-1]
    return (
        inverse * weighted - values * inverse**3 * inner_sum,
        jnp.sum(gradient * values * inverse, axis=0),
    )


def rope_tables(first_place, place_count, head_width):
    position = (first_place + jnp.arange(place_count)).astype(jnp.float32)
    frequency = ROPE_BASE ** (-(jnp.arange(head_width // 2).astype(jnp.float32) * 2.0 / head_width))
    angles = position[:, None] * frequency[None, :]
    return (jnp.cos(angles), jnp.sin(angles))


def rotate(values, cosines, sines):
    half_width = values.shape[-1] // 2
    front = values[..., :half_width]
    behind = values[..., half_width:]
    return jnp.concatenate(
        [front * cosines - behind * sines, behind * cosines + front * sines], axis=-1
    )


def conv_silu(padded, conv_table):
    tap_count = conv_table.shape[0] - 1
    length_out = padded.shape[1] - tap_count + 1
    summed = conv_table[tap_count]
    for tap_index in range(tap_count):
        summed = summed + conv_table[tap_index] * padded[:, tap_index : tap_index + length_out]
    return jax.nn.silu(summed)


def block_step(carry_state, pieces):
    block_x, block_write, block_read, block_size, block_rate = pieces
    block_len = block_x.shape[1]
    cumulative = jnp.cumsum(block_rate, axis=1)
    lower_mask = jnp.arange(block_len)[:, None] >= jnp.arange(block_len)[None, :]
    log_decay = jnp.where(
        lower_mask[None, :, :, None], cumulative[:, :, None, :] - cumulative[:, None, :, :], MASKED
    )
    intersection = jnp.einsum("gtn,gsn->gts", block_read, block_write, precision=HIGHEST)
    mixing = intersection[..., None] * jnp.exp(log_decay) * block_size[:, None, :, :]
    inside = jnp.einsum("gtsh,gshp->gthp", mixing, block_x, precision=HIGHEST)
    carried = (
        jnp.einsum("gtn,ghpn->gthp", block_read, carry_state, precision=HIGHEST)
        * jnp.exp(cumulative)[..., None]
    )
    tail_decay = jnp.exp(cumulative[:, -1:, :] - cumulative) * block_size
    fresh_state = jnp.einsum(
        "gsh,gshp,gsn->ghpn", tail_decay, block_x, block_write, precision=HIGHEST
    )
    updated = carry_state * jnp.exp(cumulative[:, -1])[:, :, None, None] + fresh_state
    return (updated, inside + carried, cumulative)


def mamba_local(padded, conv_table, step_raw, bias_values, decay_values):
    conv_output = conv_silu(padded, conv_table)
    seq_count, row_count, channels = conv_output.shape
    head_count = step_raw.shape[-1]
    inner_width = channels - 2 * NS
    head_inputs = conv_output[..., :inner_width].reshape(
        seq_count, row_count, head_count, inner_width // head_count
    )
    write_vectors = conv_output[..., inner_width : inner_width + NS]
    read_vectors = conv_output[..., inner_width + NS :]
    step_size = jax.nn.softplus(step_raw + bias_values)
    decay_rate = step_size * -jnp.exp(decay_values)
    block_count = row_count // SPAN

    def to_blocks(values):
        return jnp.moveaxis(values.reshape((seq_count, block_count, SPAN) + values.shape[2:]), 1, 0)

    def from_blocks(values):
        return jnp.moveaxis(values, 0, 1).reshape((seq_count, row_count) + values.shape[3:])

    def advance(carry, pieces):
        carry_state, offset = carry
        updated, output, cumulative = block_step(carry_state, pieces)
        return ((updated, offset + cumulative[:, -1]), (output, cumulative + offset[:, None, :]))

    initial = (
        jnp.zeros((seq_count, head_count, inner_width // head_count, NS), jnp.float32),
        jnp.zeros((seq_count, head_count), jnp.float32),
    )
    (final_state, total_rate), (outputs, cumulatives) = lax.scan(
        advance,
        initial,
        (
            to_blocks(head_inputs),
            to_blocks(write_vectors),
            to_blocks(read_vectors),
            to_blocks(step_size),
            to_blocks(decay_rate),
        ),
    )
    return (
        from_blocks(outputs),
        head_inputs,
        read_vectors,
        from_blocks(cumulatives),
        final_state,
        jnp.exp(total_rate),
    )


def mamba_finish(local_out, head_inputs, read_vectors, cumulative, incoming, skip_values, gate_z):
    carried = (
        jnp.einsum("gtn,ghpn->gthp", read_vectors, incoming, precision=HIGHEST)
        * jnp.exp(cumulative)[..., None]
    )
    values = local_out + carried + skip_values[:, None] * head_inputs
    return values.reshape(gate_z.shape) * jax.nn.silu(gate_z)


def chain_join(earlier, later):
    return (earlier[0] * later[0], later[0][:, :, None, None] * earlier[1] + later[1])


def channel_total(values):
    return lax.psum(jnp.sum(values, axis=-1), "tp")


def fetch_weights(
    norm_gains,
    query_weight,
    key_value_matrix,
    output_weight,
    mixer_weight,
    state_weight,
    step_weight,
    mamba_weight,
    gateup_weight,
    down_weight,
):
    return (
        lax.all_gather(norm_gains, ("fsdp", "ctx"), axis=1, tiled=True),
        lax.all_gather(query_weight, ("fsdp", "ctx"), axis=0, tiled=True),
        lax.all_gather(key_value_matrix, ("fsdp", "ctx"), axis=0, tiled=True),
        lax.all_gather(output_weight, ("fsdp", "ctx"), axis=1, tiled=True),
        lax.all_gather(mixer_weight, ("fsdp", "ctx"), axis=0, tiled=True),
        lax.all_gather(state_weight, ("fsdp", "ctx"), axis=0, tiled=True),
        lax.all_gather(step_weight, ("fsdp", "ctx"), axis=0, tiled=True),
        lax.all_gather(mamba_weight, ("fsdp", "ctx"), axis=1, tiled=True),
        lax.all_gather(gateup_weight, ("fsdp", "ctx"), axis=0, tiled=True),
        lax.all_gather(down_weight, ("fsdp", "ctx"), axis=1, tiled=True),
    )


def shards(
    tokens,
    out_grad,
    norm_gains,
    query_weight,
    key_value_matrix,
    output_weight,
    mixer_weight,
    state_weight,
    step_weight,
    conv_inner,
    conv_state,
    step_bias,
    decay_log,
    skip_scale,
    gated_gain,
    mamba_weight,
    gateup_weight,
    down_weight,
):
    gathered = fetch_weights(
        norm_gains,
        query_weight,
        key_value_matrix,
        output_weight,
        mixer_weight,
        state_weight,
        step_weight,
        mamba_weight,
        gateup_weight,
        down_weight,
    )
    (
        gain_pair,
        query_full,
        keyvalue_full,
        output_full,
        mixer_full,
        state_full,
        step_full,
        mamba_full,
        gateup_full,
        down_full,
    ) = gathered
    seq_count, row_count, model_width = tokens.shape
    total_rows = seq_count * row_count
    context_index = lax.axis_index("ctx")
    tensor_index = lax.axis_index("tp")
    tensor_count = lax.axis_size("tp")
    key_length = row_count * lax.axis_size("ctx")
    query_heads = query_full.shape[1] // HEAD_DIMENSION
    state_heads = step_bias.shape[0]
    inner_width = state_heads * MP
    score_scale = HEAD_DIMENSION ** (-0.5)
    residual = tokens.astype(jnp.float32).reshape(total_rows, model_width)
    first_inverse = rms_inverse(residual)
    first_gain = gain_pair[0].astype(jnp.float32)
    normed_one = (residual * first_inverse * first_gain).astype(jnp.bfloat16)
    cosines, sines = rope_tables(context_index * row_count, row_count, HEAD_DIMENSION)
    cos_grid = cosines[None, :, None, :]
    sin_grid = sines[None, :, None, :]
    query_lin = jnp.dot(normed_one, query_full, preferred_element_type=jnp.float32).reshape(
        seq_count, row_count, query_heads, HEAD_DIMENSION
    )
    rotated_query = rotate(query_lin, cos_grid, sin_grid).astype(jnp.bfloat16)
    keyvalue_flat = keyvalue_full.reshape(model_width, 2 * HEAD_DIMENSION)
    pair_lin = jnp.dot(normed_one, keyvalue_flat, preferred_element_type=jnp.float32).reshape(
        seq_count, row_count, 2 * HEAD_DIMENSION
    )
    key_rot = rotate(pair_lin[:, :, None, :HEAD_DIMENSION], cos_grid, sin_grid)[:, :, 0, :].astype(
        jnp.bfloat16
    )
    local_pairs = jnp.concatenate(
        [key_rot, pair_lin[..., HEAD_DIMENSION:].astype(jnp.bfloat16)], axis=-1
    )
    all_pairs = lax.all_gather(local_pairs, "ctx", axis=1, tiled=True)
    query_rows = jnp.transpose(rotated_query, (0, 2, 1, 3)).reshape(
        seq_count, query_heads * row_count, HEAD_DIMENSION
    )
    query_place = context_index * row_count + jnp.tile(jnp.arange(row_count), query_heads)
    visible = jnp.arange(key_length)[None, :] <= query_place[:, None]

    def attend(pieces):
        query_one, pair_one = pieces
        logits = (
            jnp.einsum(
                "qd,kd->qk",
                query_one,
                pair_one[:, :HEAD_DIMENSION],
                preferred_element_type=jnp.float32,
            )
            * score_scale
        )
        logits = jnp.where(visible, logits, MASKED)
        largest = jnp.max(logits, axis=-1, keepdims=True)
        log_total = largest + jnp.log(jnp.sum(jnp.exp(logits - largest), axis=-1, keepdims=True))
        prob_low = jnp.exp(logits - log_total).astype(jnp.bfloat16)
        return (
            jnp.dot(prob_low, pair_one[:, HEAD_DIMENSION:], preferred_element_type=jnp.float32),
            log_total[:, 0],
        )

    attended_rows, log_totals = lax.map(attend, (query_rows, all_pairs))
    attended = (
        jnp.transpose(
            attended_rows.reshape(seq_count, query_heads, row_count, HEAD_DIMENSION), (0, 2, 1, 3)
        )
        .reshape(total_rows, query_heads * HEAD_DIMENSION)
        .astype(jnp.bfloat16)
    )
    mixer_lin = jnp.einsum(
        "td,dhe->the", normed_one, mixer_full, preferred_element_type=jnp.float32
    )
    gate_z = mixer_lin[..., :MP].reshape(seq_count, row_count, inner_width)
    inner_in = mixer_lin[..., MP:].reshape(seq_count, row_count, inner_width).astype(jnp.bfloat16)
    state_in = (
        jnp.dot(normed_one, state_full, preferred_element_type=jnp.float32)
        .reshape(seq_count, row_count, 2 * NS)
        .astype(jnp.bfloat16)
    )
    step_raw = jnp.dot(normed_one, step_full, preferred_element_type=jnp.float32).reshape(
        seq_count, row_count, state_heads
    )
    conv_in = jnp.concatenate([inner_in, state_in], axis=-1)
    rim_width = conv_inner.shape[0] - 2
    rim_rows = from_behind(conv_in[:, row_count - rim_width :], "ctx", 1)
    padded = jnp.concatenate([rim_rows, conv_in], axis=1).astype(jnp.float32)
    conv_table = jnp.concatenate([conv_inner, conv_state], axis=1).astype(jnp.float32)
    local_values, local_back = jax.vjp(
        mamba_local,
        padded,
        conv_table,
        step_raw,
        step_bias.astype(jnp.float32),
        decay_log.astype(jnp.float32),
    )
    local_out, head_inputs, read_vectors, cumulative, final_state, block_decay = local_values
    identity = (jnp.ones_like(block_decay), jnp.zeros_like(final_state))
    carried_in = prefix((block_decay, final_state), "ctx", chain_join, identity)
    incoming = carried_in[1]
    gated_values, finish_back = jax.vjp(
        mamba_finish,
        local_out,
        head_inputs,
        read_vectors,
        cumulative,
        incoming,
        skip_scale.astype(jnp.float32),
        gate_z,
    )
    gated = gated_values.reshape(total_rows, inner_width)
    gate_gain = gated_gain.astype(jnp.float32)
    square_sum = channel_total(gated * gated)
    gate_inverse = lax.rsqrt(square_sum / (inner_width * tensor_count) + EPSILON)[:, None]
    gated_low = (gated * gate_inverse * gate_gain).astype(jnp.bfloat16)
    branch_part = jnp.dot(attended, output_full, preferred_element_type=jnp.float32) + jnp.dot(
        gated_low, mamba_full, preferred_element_type=jnp.float32
    )
    branch = lax.psum(branch_part, "tp")
    middle = residual + branch
    second_inverse = rms_inverse(middle)
    second_gain = gain_pair[1].astype(jnp.float32)
    normed_two = (middle * second_inverse * second_gain).astype(jnp.bfloat16)
    gate_up = jnp.einsum("td,dkf->tkf", normed_two, gateup_full, preferred_element_type=jnp.float32)
    gate_val = gate_up[:, 0]
    up_val = gate_up[:, 1]
    sigmoid_gate = jax.nn.sigmoid(gate_val)
    silu_gate = gate_val * sigmoid_gate
    act_low = (silu_gate * up_val).astype(jnp.bfloat16)
    feed_share = lax.psum_scatter(
        jnp.dot(act_low, down_full, preferred_element_type=jnp.float32).astype(jnp.bfloat16),
        "tp",
        scatter_dimension=1,
        tiled=True,
    ).astype(jnp.float32)
    share_width = model_width // tensor_count
    middle_share = lax.dynamic_slice_in_dim(middle, tensor_index * share_width, share_width, 1)
    out_block = (
        (middle_share + feed_share).astype(jnp.bfloat16).reshape(seq_count, row_count, share_width)
    )
    (
        gain_pair,
        query_full,
        keyvalue_full,
        output_full,
        mixer_full,
        state_full,
        step_full,
        mamba_full,
        gateup_full,
        down_full,
    ) = gathered
    keyvalue_flat = keyvalue_full.reshape(model_width, 2 * HEAD_DIMENSION)
    cotangent = out_grad.reshape(total_rows, model_width)
    act_grad = jnp.einsum("td,fd->tf", cotangent, down_full, preferred_element_type=jnp.float32)
    down_grad = jnp.einsum("tf,td->fd", act_low, cotangent, preferred_element_type=jnp.float32)
    gate_grad = (act_grad * up_val * sigmoid_gate * (1.0 + gate_val * (1.0 - sigmoid_gate))).astype(
        jnp.bfloat16
    )
    up_grad = (act_grad * silu_gate).astype(jnp.bfloat16)
    both_grads = jnp.stack([gate_grad, up_grad], axis=1)
    gateup_grad = jnp.einsum(
        "td,tkf->dkf", normed_two, both_grads, preferred_element_type=jnp.float32
    )
    normed_two_part = jnp.einsum(
        "tkf,dkf->td", both_grads, gateup_full, preferred_element_type=jnp.float32
    )
    normed_two_grad = lax.psum(normed_two_part.astype(jnp.bfloat16), "tp").astype(jnp.float32)
    second_back, second_gain_grad = norm_back(middle, second_inverse, second_gain, normed_two_grad)
    middle_grad = cotangent.astype(jnp.float32) + second_back
    branch_grad = middle_grad.astype(jnp.bfloat16)
    output_grad = jnp.einsum("te,td->ed", attended, branch_grad, preferred_element_type=jnp.float32)
    attended_grad = jnp.einsum(
        "td,ed->te", branch_grad, output_full, preferred_element_type=jnp.float32
    ).astype(jnp.bfloat16)
    attended_grad_rows = jnp.transpose(
        attended_grad.reshape(seq_count, row_count, query_heads, HEAD_DIMENSION), (0, 2, 1, 3)
    ).reshape(seq_count, query_heads * row_count, HEAD_DIMENSION)

    def attend_back(pieces):
        query_one, pair_one, total_one, grad_one = pieces
        key_one = pair_one[:, :HEAD_DIMENSION]
        value_one = pair_one[:, HEAD_DIMENSION:]
        logits = (
            jnp.einsum("qd,kd->qk", query_one, key_one, preferred_element_type=jnp.float32)
            * score_scale
        )
        logits = jnp.where(visible, logits, MASKED)
        prob_full = jnp.exp(logits - total_one[:, None])
        prob_grad = jnp.einsum("qd,kd->qk", grad_one, value_one, preferred_element_type=jnp.float32)
        row_inner = jnp.sum(prob_full * prob_grad, axis=-1, keepdims=True)
        logit_grad = (prob_full * (prob_grad - row_inner)).astype(jnp.bfloat16)
        query_part = jnp.dot(logit_grad, key_one, preferred_element_type=jnp.float32) * score_scale
        key_part = (
            jnp.einsum("qk,qd->kd", logit_grad, query_one, preferred_element_type=jnp.float32)
            * score_scale
        )
        value_part = jnp.einsum(
            "qk,qd->kd",
            prob_full.astype(jnp.bfloat16),
            grad_one,
            preferred_element_type=jnp.float32,
        )
        return (query_part, jnp.concatenate([key_part, value_part], axis=-1))

    query_grad_rows, pair_grad_all = lax.map(
        attend_back, (query_rows, all_pairs, log_totals, attended_grad_rows)
    )
    pair_grad = lax.psum_scatter(
        pair_grad_all.astype(jnp.bfloat16), "ctx", scatter_dimension=1, tiled=True
    ).astype(jnp.float32)
    query_grad = jnp.transpose(
        query_grad_rows.reshape(seq_count, query_heads, row_count, HEAD_DIMENSION), (0, 2, 1, 3)
    )
    query_lin_grad = (
        rotate(query_grad, cos_grid, -sin_grid)
        .reshape(total_rows, query_heads * HEAD_DIMENSION)
        .astype(jnp.bfloat16)
    )
    key_lin_grad = rotate(pair_grad[:, :, None, :HEAD_DIMENSION], cos_grid, -sin_grid)[:, :, 0, :]
    pair_lin_grad = (
        jnp.concatenate([key_lin_grad, pair_grad[..., HEAD_DIMENSION:]], axis=-1)
        .reshape(total_rows, 2 * HEAD_DIMENSION)
        .astype(jnp.bfloat16)
    )
    query_weight_grad = jnp.einsum(
        "td,te->de", normed_one, query_lin_grad, preferred_element_type=jnp.float32
    )
    keyvalue_grad = jnp.einsum(
        "td,te->de", normed_one, pair_lin_grad, preferred_element_type=jnp.float32
    ).reshape(keyvalue_full.shape)
    normed_one_part = jnp.einsum(
        "te,de->td", query_lin_grad, query_full, preferred_element_type=jnp.float32
    )
    normed_one_part = normed_one_part + jnp.einsum(
        "te,de->td", pair_lin_grad, keyvalue_flat, preferred_element_type=jnp.float32
    )
    mamba_grad = jnp.einsum("te,td->ed", gated_low, branch_grad, preferred_element_type=jnp.float32)
    gated_low_grad = jnp.einsum(
        "td,ed->te", branch_grad, mamba_full, preferred_element_type=jnp.float32
    )
    coupling = channel_total(gated_low_grad * gate_gain * gated)[:, None]
    gated_gain_grad = jnp.sum(gated_low_grad * gated * gate_inverse, axis=0)
    gated_grad = gate_inverse * gate_gain * gated_low_grad - gated * gate_inverse**3 * coupling / (
        inner_width * tensor_count
    )
    local_grad, inputs_grad, read_grad, cumulative_grad, incoming_grad, skip_grad, gate_z_grad = (
        finish_back(gated_grad.reshape(seq_count, row_count, inner_width))
    )
    later_values = prefix_2((block_decay, incoming_grad), "ctx", chain_join, identity)
    later_grad = later_values[1]
    decay_grad = jnp.sum(later_grad * incoming, axis=(2, 3))
    padded_grad, table_grad, step_raw_grad, bias_grad, decay_log_grad = local_back(
        (local_grad, inputs_grad, read_grad, cumulative_grad, later_grad, decay_grad)
    )
    rim_grad = from_behind(padded_grad[:, :rim_width].astype(jnp.bfloat16), "ctx", -1).astype(
        jnp.float32
    )
    conv_grad = padded_grad[:, rim_width:] + jnp.pad(
        rim_grad, ((0, 0), (row_count - rim_width, 0), (0, 0))
    )
    mixer_lin_grad = jnp.concatenate(
        [
            gate_z_grad.reshape(total_rows, state_heads, MP),
            conv_grad[..., :inner_width].reshape(total_rows, state_heads, MP),
        ],
        axis=-1,
    ).astype(jnp.bfloat16)
    step_low = step_raw_grad.reshape(total_rows, state_heads).astype(jnp.bfloat16)
    mixer_grad = jnp.einsum(
        "td,the->dhe", normed_one, mixer_lin_grad, preferred_element_type=jnp.float32
    )
    step_grad = jnp.einsum("td,th->dh", normed_one, step_low, preferred_element_type=jnp.float32)
    normed_one_part = normed_one_part + jnp.einsum(
        "the,dhe->td", mixer_lin_grad, mixer_full, preferred_element_type=jnp.float32
    )
    normed_one_part = normed_one_part + jnp.einsum(
        "th,dh->td", step_low, step_full, preferred_element_type=jnp.float32
    )
    normed_one_grad, state_total, conv_state_grad = (
        lax.psum(normed_one_part.astype(jnp.bfloat16), "tp").astype(jnp.float32),
        lax.psum(conv_grad[..., inner_width:].astype(jnp.bfloat16), "tp").astype(jnp.float32),
        lax.psum(table_grad[:, inner_width:].astype(jnp.bfloat16), "tp").astype(jnp.float32),
    )
    state_low = state_total.reshape(total_rows, 2 * NS).astype(jnp.bfloat16)
    normed_one_grad = normed_one_grad + jnp.einsum(
        "tn,dn->td", state_low, state_full, preferred_element_type=jnp.float32
    )
    state_grad = jnp.einsum("td,tn->dn", normed_one, state_low, preferred_element_type=jnp.float32)
    first_back, first_gain_grad = norm_back(residual, first_inverse, first_gain, normed_one_grad)
    tokens_grad = (middle_grad + first_back).reshape(seq_count, row_count, model_width)
    reduced = (
        lax.psum_scatter(
            jnp.stack([first_gain_grad, second_gain_grad]),
            ("fsdp", "ctx"),
            scatter_dimension=1,
            tiled=True,
        ),
        lax.psum_scatter(query_weight_grad, ("fsdp", "ctx"), scatter_dimension=0, tiled=True),
        lax.psum_scatter(keyvalue_grad, ("fsdp", "ctx"), scatter_dimension=0, tiled=True),
        lax.psum_scatter(output_grad, ("fsdp", "ctx"), scatter_dimension=1, tiled=True),
        lax.psum_scatter(mixer_grad, ("fsdp", "ctx"), scatter_dimension=0, tiled=True),
        lax.psum_scatter(state_grad, ("fsdp", "ctx"), scatter_dimension=0, tiled=True),
        lax.psum_scatter(step_grad, ("fsdp", "ctx"), scatter_dimension=0, tiled=True),
        lax.psum_scatter(mamba_grad, ("fsdp", "ctx"), scatter_dimension=1, tiled=True),
        lax.psum_scatter(gateup_grad, ("fsdp", "ctx"), scatter_dimension=0, tiled=True),
        lax.psum_scatter(down_grad, ("fsdp", "ctx"), scatter_dimension=1, tiled=True),
    )
    vectors = lax.psum(
        (
            table_grad[:, :inner_width],
            conv_state_grad,
            bias_grad,
            decay_log_grad,
            skip_grad,
            gated_gain_grad,
        ),
        ("fsdp", "ctx"),
    )
    (
        gain_total,
        query_total,
        keyvalue_total,
        output_total,
        mixer_total,
        state_weight_total,
        step_total,
        mamba_total,
        gateup_total,
        down_total,
    ) = reduced
    conv_inner_total, conv_state_total, bias_total, decay_total, skip_total, gated_total = vectors
    return (
        out_block,
        tokens_grad,
        gain_total,
        query_total,
        keyvalue_total,
        output_total,
        mixer_total,
        state_weight_total,
        step_total,
        conv_inner_total,
        conv_state_total,
        bias_total,
        decay_total,
        skip_total,
        gated_total,
        mamba_total,
        gateup_total,
        down_total,
    )


def solution(mesh):
    in_specs = (
        P("fsdp", "ctx", None),
        P("fsdp", "ctx", None),
        P(None, ("fsdp", "ctx")),
        P(("fsdp", "ctx"), "tp"),
        P(("fsdp", "ctx"), "tp", None),
        P("tp", ("fsdp", "ctx")),
        P(("fsdp", "ctx"), "tp", None),
        P(("fsdp", "ctx"), None),
        P(("fsdp", "ctx"), "tp"),
        P(None, "tp"),
        P(),
        P("tp"),
        P("tp"),
        P("tp"),
        P("tp"),
        P("tp", ("fsdp", "ctx")),
        P(("fsdp", "ctx"), None, "tp"),
        P("tp", ("fsdp", "ctx")),
    )
    out_specs = (
        P("fsdp", "ctx", "tp"),
        P("fsdp", "ctx", None),
        P(None, ("fsdp", "ctx")),
        P(("fsdp", "ctx"), "tp"),
        P(("fsdp", "ctx"), "tp", None),
        P("tp", ("fsdp", "ctx")),
        P(("fsdp", "ctx"), "tp", None),
        P(("fsdp", "ctx"), None),
        P(("fsdp", "ctx"), "tp"),
        P(None, "tp"),
        P(),
        P("tp"),
        P("tp"),
        P("tp"),
        P("tp"),
        P("tp", ("fsdp", "ctx")),
        P(("fsdp", "ctx"), None, "tp"),
        P("tp", ("fsdp", "ctx")),
    )
    return jax.shard_map(shards, mesh=mesh, in_specs=in_specs, out_specs=out_specs, check_vma=False)
```

profile of v0, /device:TPU:0, one launch (start us, length us, event | category | flops | bytes accessed | tf_op | source)
XLA Modules:
  0.0 2178.8 jit_solution(10043498213875999772)
XLA Ops:
  8.7 42.4 %all-gather.3 = bf16[16,64,2]{1,2,0:T(2,128)(2,1)S(1)} all-gather(bf16[1,64,2]{1,2,0:T(2,128)(2,1)} %bitcast.1009), channel_id=1, replica_groups=mesh['fsdp'=8,'ctx'=2,'tp'=2] {'fsdp','ctx'}, dimensions={0}, use_global_device_ids=true | all-gather | bytes 4352 | tf_op jit(solution)/shard_map/all_gather | solution.py:213
  54.0 38.6 %all_gather.55 = bf16[1024,1,128]{2,0,1:T(8,128)(2,1)S(1)} all-gather(bf16[64,1,128]{2,0,1:T(8,128)(2,1)} %param.34), channel_id=1, replica_groups=mesh['fsdp'=8,'ctx'=2,'tp'=2] {'fsdp','ctx'}, dimensions={0}, use_global_device_ids=true | all-gather | bytes 278528 | tf_op jit(solution)/shard_map/all_gather | solution.py:215
  98.4 41.6 %all_gather.60 = bf16[1024,256]{1,0:T(8,128)(2,1)S(1)} all-gather(bf16[64,256]{1,0:T(8,128)(2,1)S(1)} %copy-done.105), channel_id=1, replica_groups=mesh['fsdp'=8,'ctx'=2,'tp'=2] {'fsdp','ctx'}, dimensions={0}, use_global_device_ids=true | all-gather | bytes 557056 | tf_op jit(solution)/shard_map/all_gather | solution.py:218
  142.5 37.0 %all-gather.4 = bf16[16,64,12]{1,2,0:T(8,128)(2,1)S(1)} all-gather(bf16[1,64,12]{1,2,0:T(8,128)(2,1)S(1)} %bitcast.1006), channel_id=1, replica_groups=mesh['fsdp'=8,'ctx'=2,'tp'=2] {'fsdp','ctx'}, dimensions={0}, use_global_device_ids=true | all-gather | bytes 26112 | tf_op jit(solution)/shard_map/all_gather | solution.py:219
  189.2 39.6 %all_gather.54 = bf16[1024,256]{1,0:T(8,128)(2,1)S(1)} all-gather(bf16[64,256]{1,0:T(8,128)(2,1)S(1)} %copy-done.106), channel_id=1, replica_groups=mesh['fsdp'=8,'ctx'=2,'tp'=2] {'fsdp','ctx'}, dimensions={0}, use_global_device_ids=true | all-gather | bytes 557056 | tf_op jit(solution)/shard_map/all_gather | solution.py:214
  232.4 15.7 while.135
  248.1 42.1 %all_gather.57 = bf16[256,1024]{0,1:T(8,128)(2,1)} all-gather(bf16[256,64]{0,1:T(8,128)(2,1)S(1)} %copy-done.107), channel_id=1, replica_groups=mesh['fsdp'=8,'ctx'=2,'tp'=2] {'fsdp','ctx'}, dimensions={1}, use_global_device_ids=true | all-gather | bytes 557056 | tf_op jit(solution)/shard_map/all_gather | solution.py:216
  353.9 92.4 %while.139 = (s32[]{:T(128)}, f32[2,12,64,128]{3,2,1,0:T(8,128)S(1)}, f32[2,12]{1,0:T(2,128)S(1)}, f32[4,2,128,12,64]{2,4,3,1,0:T(8,128)}, f32[4,2,128,12]{2,0,1...) while((s32[]{:T(128)}, ...), condition=%wide.region_7.8_spmd.clone.clone.clone, body=%wide.region_5.7_spmd.clone.clone.sunk.clone | while | flops 961622080 | bytes 16958932 | solution.py:162
  504.9 22.3 %all-reduce.22.cloned.1.call-done = f32[1024,1024]{1,0:T(8,128)} async-done(((f32[1024,1024]{1,0:T(8,128)}), f32[1024,1024]{1,0:T(8,128)}) %all-reduce.22.cloned.1.call-update) | async-done | bytes 4194320 | tf_op jit(solution)/shard_map/psum | solution.py:384
  532.7 75.4 %all-gather.15.cloned.1.call-done = bf16[1024,2,1024]{2,0,1:T(8,128)(2,1)} async-done(((bf16[64,2,1024]{2,0,1:T(8,128)(2,1)}), bf16[1024,2,1024]{2,0,1:T(8,128)(2,1)}) %all-gather.15.cloned.1.call-update) | async-done | bytes 4194320 | tf_op jit(solution)/shard_map/all_gather | solution.py:221
  619.5 50.8 %all-gather.17.cloned.1.call-done = bf16[1024,1024]{0,1:T(8,128)(2,1)} async-done(((bf16[1024,64]{0,1:T(8,128)(2,1)}), bf16[1024,1024]{0,1:T(8,128)(2,1)}) %all-gather.17.cloned.1.call-update) | async-done | bytes 2097168 | tf_op jit(solution)/shard_map/all_gather | solution.py:222
  781.8 192.9 %while.137 = (s32[]{:T(128)}, f32[2,12,64,128]{3,2,1,0:T(8,128)S(1)}, f32[2,12]{1,0:T(2,128)}, f32[4,2,128,12,64]{2,4,3,1,0:T(8,128)}, f32[4,2,128,128]{3,2,1,0:...) while((s32[]{:T(128)}, ...), condition=%wide.region_37.38_spmd.clone.clone, body=%wide.region_27.37_spmd.clone.sunk.clone | while | flops 1919350784 | bytes 27112624 | solution.py:162
  1025.0 49.6 %while.136 = (s32[]{:T(128)}, f32[2,2048,64]{1,2,0:T(8,128)}, bf16[2,1024,128]{1,2,0:T(8,128)(2,1)}, bf16[2,2048,64]{2,1,0:T(8,128)(2,1)S(1)}, bf16[2,1024,128]{...) while((s32[]{:T(128)}, f32[2,2048,64]{1,2,0:T(8,128)}, ...), condition=%wide.region_19.20_spmd.clone.clone, body=%wide.region_17.19_spmd.clone.sunk.clone | while | flops 1363933184 | bytes 105431744 | solution.py:471
  1120.7 14.3 all-reduce.26.cloned.1.call-done
  1192.2 77.8 %all-reduce.16 = (f32[5,768]{1,0:T(8,128)}, f32[5,256]{1,0:T(8,128)}, f32[12]{0:T(128)}, f32[12]{0:T(128)}, f32[12]{0:T(128)}, /*index=5*/f32[768]{0:T(1024)}) all-reduce(f32[5,768]{1,0:T(8,128)S(1)} %slice.215, bf16[5,256]{1,0:T(8,128)(2,1)S(1)} %psum.98, ...), channel_id=1, replica_groups=mesh['fsdp'=8,'ctx'=2,'tp'=2] {'fsdp','ctx'}, use_global_device_ids=true, to_apply=%region_55.56 | all-reduce | flops 5924 | bytes 44832 | tf_op jit(solution)/shard_map/psum | solution.py:574
  1280.9 22.9 %reduce-scatter.37.cloned.1.call-done = f32[64,2]{1,0:T(8,128)} async-done(((f32[1024,2]{1,0:T(8,128)}), f32[64,2]{1,0:T(8,128)}) %reduce-scatter.37.cloned.1.call-update) | async-done | bytes 528
  1305.2 175.7 %reduce-scatter.33.cloned.1.call-done = f32[64,2,1024]{2,0,1:T(8,128)} async-done(((f32[1024,2,1024]{2,0,1:T(8,128)}), f32[64,2,1024]{2,0,1:T(8,128)}) %reduce-scatter.33.cloned.1.call-update) | async-done | bytes 524304 | tf_op jit(solution)/shard_map/reduce_scatter | solution.py:571
  1483.2 76.3 %reduce-scatter.23.cloned.1.call-done = f32[64,1,128]{2,0,1:T(8,128)} async-done(((f32[1024,1,128]{2,0,1:T(8,128)}), f32[64,1,128]{2,0,1:T(8,128)}) %reduce-scatter.23.cloned.1.call-update) | async-done | bytes 32784 | tf_op jit(solution)/shard_map/reduce_scatter | solution.py:565
  1559.5 76.8 %reduce-scatter.21.cloned.1.call-done = f32[64,256]{1,0:T(8,128)} async-done(((f32[1024,256]{1,0:T(8,128)}), f32[64,256]{1,0:T(8,128)}) %reduce-scatter.21.cloned.1.call-update) | async-done | bytes 65552 | tf_op jit(solution)/shard_map/reduce_scatter | solution.py:564
  1636.3 76.9 %reduce-scatter.25.cloned.1.call-done = f32[256,64]{0,1:T(8,128)} async-done(((f32[256,1024]{0,1:T(8,128)}), f32[256,64]{0,1:T(8,128)}) %reduce-scatter.25.cloned.1.call-update) | async-done | bytes 65552 | tf_op jit(solution)/shard_map/reduce_scatter | solution.py:566
  1713.3 76.9 %reduce-scatter.29.cloned.1.call-done = f32[64,256]{1,0:T(8,128)} async-done(((f32[1024,256]{1,0:T(8,128)}), f32[64,256]{1,0:T(8,128)}) %reduce-scatter.29.cloned.1.call-update) | async-done | bytes 65552 | tf_op jit(solution)/shard_map/reduce_scatter | solution.py:568
  1790.2 94.9 %reduce-scatter.35.cloned.1.call-done = f32[1024,64]{0,1:T(8,128)} async-done(((f32[1024,1024]{0,1:T(8,128)}), f32[1024,64]{0,1:T(8,128)}) %reduce-scatter.35.cloned.1.call-update) | async-done | bytes 262160 | tf_op jit(solution)/shard_map/reduce_scatter | solution.py:572
  1885.0 135.2 %reduce-scatter.31.cloned.1.call-done = f32[768,64]{0,1:T(8,128)} async-done(((f32[768,1024]{0,1:T(8,128)}), f32[768,64]{0,1:T(8,128)}) %reduce-scatter.31.cloned.1.call-update) | async-done | bytes 196624 | tf_op jit(solution)/shard_map/reduce_scatter | solution.py:570
  2020.2 151.9 %reduce-scatter.27.cloned.1.call-done = f32[64,12,128]{2,0,1:T(8,128)} async-done(((f32[1024,12,128]{2,0,1:T(8,128)}), f32[64,12,128]{2,0,1:T(8,128)}) %reduce-scatter.27.cloned.1.call-update) | async-done | bytes 393232 | tf_op jit(solution)/shard_map/reduce_scatter | solution.py:567
  (879 shorter events, 798.1 us)
Async XLA Ops:
  7.2 286.3 %all-gather.11.cloned.1.call-start = ((), (), s32[]{:S(2)}) async-start(), calls=%async_computation.12 | async-start | bytes 3342336 | tf_op jit(solution)/shard_map/all_gather | solution.py:217
  7.9 487.3 %all-gather.13.cloned.1.call-start = ((), (), s32[]{:S(2)}) async-start(), calls=%async_computation.13 | async-start | bytes 1671168 | tf_op jit(solution)/shard_map/all_gather | solution.py:220
  8.7 518.6 %all-reduce.22.cloned.1.call-start = ((), (), s32[]{:S(2)}) async-start(), calls=%async_computation.14 | async-start | bytes 8388608 | tf_op jit(solution)/shard_map/psum | solution.py:384
  93.1 197.8 %copy-start.5 = (bf16[2,512,1024]{2,1,0:T(8,128)(2,1)}, bf16[2,512,1024]{2,1,0:T(8,128)(2,1)S(1)}, u32[]{:S(2)}) copy-start(bf16[2,512,1024]{2,1,0:T(8,128)(2,1)S(1)} %fusion.190) | copy-start | bytes 6291460
  309.2 15.1 collective-permute-start
  489.8 231.9 %copy-start.109 = (f32[1024]{0:T(1024)}, f32[1024]{0:T(1024)S(1)}, u32[]{:S(2)}) copy-start(f32[1024]{0:T(1024)S(1)} %get-tuple-element.2084) | copy-start | bytes 12292
  502.3 105.8 %all-gather.15.cloned.1.call-start = ((), (), s32[]{:S(2)}) async-start(), calls=%async_computation.15 | async-start | bytes 4456448 | tf_op jit(solution)/shard_map/all_gather | solution.py:221
  504.0 166.3 %all-gather.17.cloned.1.call-start = ((), (), s32[]{:S(2)}) async-start(), calls=%async_computation.16 | async-start | bytes 2228224 | tf_op jit(solution)/shard_map/all_gather | solution.py:222
  504.6 202.0 %all-reduce.24.cloned.1.call-start = ((), (), s32[]{:S(2)}) async-start(), calls=%async_computation.18 | async-start | bytes 4194304 | tf_op jit(solution)/shard_map/psum | solution.py:433
  532.7 178.8 %copy-start.57 = (f32[1024]{0:T(1024)}, f32[1024]{0:T(1024)S(1)}, u32[]{:S(2)}) copy-start(f32[1024]{0:T(1024)S(1)} %get-tuple-element.2086) | copy-start | bytes 12292
  686.6 416.7 %reduce-scatter.19.cloned.1.call-start = ((), (), s32[]{:S(2)}) async-start(), calls=%async_computation.19 | async-start | bytes 786432 | tf_op jit(solution)/shard_map/reduce_scatter | solution.py:474
  1022.2 63.5 %collective-permute-start.1 = (bf16[2,3,1024]{2,1,0:T(4,128)(2,1)}, bf16[2,3,1024]{2,1,0:T(4,128)(2,1)}, u32[]{:S(2)}, u32[]{:S(2)}) collective-permute-start(bf16[2,3,1024]{2,1,0:T(4,128)(2,1)} %slice.302), channel_id=1, source_target_pairs={{2,0},{3,1},{6,4},{7,5},{10,8},{11,9},{14,12},{15,13},{18,16},{19,... | collective-permute-start | bytes 36872 | tf_op jit(solution)/shard_map/ppermute | solution.py:21
  1085.7 49.4 %all-reduce.26.cloned.1.call-start = ((), (), s32[]{:S(2)}) async-start(), calls=%async_computation.30 | async-start | bytes 5242880 | tf_op jit(solution)/shard_map/psum | solution.py:546
  1111.1 158.9 %reduce-scatter.39.cloned.1.call-start = ((), (), s32[]{:S(2)}) async-start(), calls=%async_computation.29 | async-start | bytes 557056
  1112.8 158.7 %reduce-scatter.17.cloned.1.call-start = ((), (), s32[]{:S(2)}) async-start(), calls=%async_computation.17 | async-start | bytes 3145728 | tf_op jit(solution)/shard_map/reduce_scatter | solution.py:395
  1120.7 183.1 %reduce-scatter.37.cloned.1.call-start = ((), (), s32[]{:S(2)}) async-start(), calls=%async_computation.28 | async-start | bytes 557056
  1142.1 338.9 %reduce-scatter.33.cloned.1.call-start = ((), (), s32[]{:S(2)}) async-start(), calls=%async_computation.26 | async-start | bytes 8912896 | tf_op jit(solution)/shard_map/reduce_scatter | solution.py:571
  1154.1 405.4 %reduce-scatter.23.cloned.1.call-start = ((), (), s32[]{:S(2)}) async-start(), calls=%async_computation.21 | async-start | bytes 557056 | tf_op jit(solution)/shard_map/reduce_scatter | solution.py:565
  1157.3 479.0 %reduce-scatter.21.cloned.1.call-start = ((), (), s32[]{:S(2)}) async-start(), calls=%async_computation.20 | async-start | bytes 1114112 | tf_op jit(solution)/shard_map/reduce_scatter | solution.py:564
  1159.2 554.1 %reduce-scatter.25.cloned.1.call-start = ((), (), s32[]{:S(2)}) async-start(), calls=%async_computation.22 | async-start | bytes 1114112 | tf_op jit(solution)/shard_map/reduce_scatter | solution.py:566
  1162.8 627.3 %reduce-scatter.29.cloned.1.call-start = ((), (), s32[]{:S(2)}) async-start(), calls=%async_computation.24 | async-start | bytes 1114112 | tf_op jit(solution)/shard_map/reduce_scatter | solution.py:568
  1164.7 720.4 %reduce-scatter.35.cloned.1.call-start = ((), (), s32[]{:S(2)}) async-start(), calls=%async_computation.27 | async-start | bytes 4456448 | tf_op jit(solution)/shard_map/reduce_scatter | solution.py:572
  1173.3 847.0 %reduce-scatter.31.cloned.1.call-start = ((), (), s32[]{:S(2)}) async-start(), calls=%async_computation.25 | async-start | bytes 3342336 | tf_op jit(solution)/shard_map/reduce_scatter | solution.py:570
  1180.4 991.7 %reduce-scatter.27.cloned.1.call-start = ((), (), s32[]{:S(2)}) async-start(), calls=%async_computation.23 | async-start | bytes 6684672 | tf_op jit(solution)/shard_map/reduce_scatter | solution.py:567
  (164 other events, 2379.2 us)
Sparse Core Ops, SparseCore 0:
  10.8 72.5 all-gather.10
  86.2 58.0 all-gather.12
  502.5 24.7 all-reduce.21
  530.8 77.2 all-gather.14
  611.1 59.2 all-gather.16
  686.7 19.8 all-reduce.23
  1085.8 17.4 reduce-scatter.18
  1111.3 23.7 all-reduce.25
  1137.3 77.7 reduce-scatter.38
  1217.3 5.9 reduce-scatter.16
  1226.1 77.6 reduce-scatter.36
  1306.1 174.8 reduce-scatter.32
  1483.8 75.5 reduce-scatter.22
  1562.2 74.1 reduce-scatter.20
  1639.1 74.1 reduce-scatter.24
  1716.0 74.1 reduce-scatter.28
  1793.0 91.9 reduce-scatter.34
  1891.2 128.9 reduce-scatter.30
  2026.9 145.1 reduce-scatter.26
where the time goes:
time: 2190 us; the launch traced here: 2180 us
  waiting for transfers between devices  1060 us (48%)
  blocking collectives  359 us (16%)
  matrix products  306 us (14%)
  local copies, waits for them, and re-layouts  234 us (11%)
  other arithmetic  200 us (9%)
    reduce_scatter x1, waiting for transfers between devices, shards(): lax.psum_scatter(gateup_grad, ('fsdp', 'ctx'), scatter_dimension=0, tiled...  176 us
    reduce_scatter x1, waiting for transfers between devices, shards(): lax.psum_scatter(mixer_grad, ('fsdp', 'ctx'), scatter_dimension=0, tiled=...  152 us
    reduce_scatter x1, waiting for transfers between devices, shards(): lax.psum_scatter(mamba_grad, ('fsdp', 'ctx'), scatter_dimension=1, tiled=...  135 us
    reduce_scatter x1, waiting for transfers between devices, shards(): lax.psum_scatter(down_grad, ('fsdp', 'ctx'), scatter_dimension=1, tiled=T...  94.9 us
    psum x1, blocking collectives, shards(): lax.psum((table_grad[:, :inner_width], conv_state_grad, bias_grad, decay_...  77.8 us
    reduce_scatter x1, waiting for transfers between devices, shards(): lax.psum_scatter(output_grad, ('fsdp', 'ctx'), scatter_dimension=1, tiled...  76.9 us
    reduce_scatter x1, waiting for transfers between devices, shards(): lax.psum_scatter(state_grad, ('fsdp', 'ctx'), scatter_dimension=0, tiled=...  76.9 us
    reduce_scatter x1, waiting for transfers between devices, shards(): lax.psum_scatter(query_weight_grad, ('fsdp', 'ctx'), scatter_dimension=0,...  76.8 us
  transfers between devices with their start and end apart: 21, of which 15 were waited for; matrix products, arithmetic and copies ran while one was open for 18% of the time, Pallas kernels for 0%

commit v1 on v0

v1 whole, which is shorter than its diff:
```python
import jax
import jax.numpy as jnp
from jax import lax
from jax.sharding import PartitionSpec as P

HEAD_DIMENSION = 64
MP = 64
NS = 128
SPAN = 128


EPSILON = 1e-05
HIGHEST = lax.Precision.HIGHEST
MASKED = -1e30
ROPE_BASE = 10000.0
WEIGHT_AXES = ("fsdp", "ctx")


def shift_along(block, axis, distance):
    devices = range(lax.axis_size(axis))
    route = [(i - distance, i) for i in devices if i - distance in devices]
    return lax.ppermute(block, axis, route)


def sum_over(value, axis):
    count = lax.axis_size(axis)
    if count & (count - 1):
        return lax.psum(value, axis)
    stride = 1
    while stride < count:
        other = lax.ppermute(value, axis, [(i, i ^ stride) for i in range(count)])
        value = value + other
        stride *= 2
    return value


def gather_ctx(block, dim):
    count = lax.axis_size("ctx")
    if count == 1:
        return block
    if count > 2:
        return lax.all_gather(block, "ctx", axis=dim, tiled=True)
    other = lax.ppermute(block, "ctx", [(0, 1), (1, 0)])
    first = lax.axis_index("ctx") == 0
    return jnp.concatenate(
        [jnp.where(first, block, other), jnp.where(first, other, block)], axis=dim
    )


def scatter_sum_ctx(whole, dim):
    count = lax.axis_size("ctx")
    if count == 1:
        return whole
    if count > 2:
        return lax.psum_scatter(whole, "ctx", scatter_dimension=dim, tiled=True)
    half = whole.shape[dim] // 2
    low = lax.slice_in_dim(whole, 0, half, axis=dim)
    high = lax.slice_in_dim(whole, half, 2 * half, axis=dim)
    first = lax.axis_index("ctx") == 0
    kept = jnp.where(first, low, high)
    sent = jnp.where(first, high, low)
    return kept + lax.ppermute(sent, "ctx", [(0, 1), (1, 0)])


def carry_over(decay, state, forward):
    count = lax.axis_size("ctx")
    if count <= 2:
        moved = shift_along(state.astype(jnp.bfloat16), "ctx", 1 if forward else -1)
        return moved.astype(jnp.float32)
    place = lax.axis_index("ctx")
    decays = lax.all_gather(decay.astype(jnp.bfloat16), "ctx").astype(jnp.float32)
    states = lax.all_gather(state.astype(jnp.bfloat16), "ctx").astype(jnp.float32)
    total = jnp.zeros_like(state)
    order = range(count) if forward else range(count - 1, -1, -1)
    for k in order:
        reached = k < place if forward else k > place
        new = decays[k][:, :, None, None] * total + states[k]
        total = jnp.where(reached, new, total)
    return total


def rms_inverse(values):
    return lax.rsqrt(jnp.mean(values * values, axis=-1, keepdims=True) + EPSILON)


def norm_back(values, inverse, gain_values, gradient):
    weighted = gradient * gain_values
    inner_sum = jnp.sum(weighted * values, axis=-1, keepdims=True) / values.shape[-1]
    return (
        inverse * weighted - values * inverse**3 * inner_sum,
        jnp.sum(gradient * values * inverse, axis=0),
    )


def rope_tables(first_place, place_count, head_width):
    position = (first_place + jnp.arange(place_count)).astype(jnp.float32)
    frequency = ROPE_BASE ** (-(jnp.arange(head_width // 2).astype(jnp.float32) * 2.0 / head_width))
    angles = position[:, None] * frequency[None, :]
    return (jnp.cos(angles), jnp.sin(angles))


def rotate(values, cosines, sines):
    half_width = values.shape[-1] // 2
    front = values[..., :half_width]
    behind = values[..., half_width:]
    return jnp.concatenate(
        [front * cosines - behind * sines, behind * cosines + front * sines], axis=-1
    )


def conv_silu(padded, conv_table):
    tap_count = conv_table.shape[0] - 1
    length_out = padded.shape[1] - tap_count + 1
    summed = conv_table[tap_count]
    for tap_index in range(tap_count):
        summed = summed + conv_table[tap_index] * padded[:, tap_index : tap_index + length_out]
    return jax.nn.silu(summed)


def running_sum(values):
    length = values.shape[1]
    ones = (jnp.arange(length)[:, None] >= jnp.arange(length)[None, :]).astype(jnp.float32)
    return jnp.einsum("ts,gsh->gth", ones, values, precision=HIGHEST)


def block_step(carry_state, pieces):
    block_x, block_write, block_read, block_size, block_rate = pieces
    block_len = block_x.shape[1]
    cumulative = running_sum(block_rate)
    lower_mask = jnp.arange(block_len)[:, None] >= jnp.arange(block_len)[None, :]
    log_decay = jnp.where(
        lower_mask[None, :, :, None], cumulative[:, :, None, :] - cumulative[:, None, :, :], MASKED
    )
    intersection = jnp.einsum("gtn,gsn->gts", block_read, block_write, precision=HIGHEST)
    mixing = intersection[..., None] * jnp.exp(log_decay) * block_size[:, None, :, :]
    inside = jnp.einsum("gtsh,gshp->gthp", mixing, block_x, precision=HIGHEST)
    carried = (
        jnp.einsum("gtn,ghpn->gthp", block_read, carry_state, precision=HIGHEST)
        * jnp.exp(cumulative)[..., None]
    )
    tail_decay = jnp.exp(cumulative[:, -1:, :] - cumulative) * block_size
    fresh_state = jnp.einsum(
        "gsh,gshp,gsn->ghpn", tail_decay, block_x, block_write, precision=HIGHEST
    )
    updated = carry_state * jnp.exp(cumulative[:, -1])[:, :, None, None] + fresh_state
    return (updated, inside + carried, cumulative)


def mamba_local(padded, conv_table, step_raw, bias_values, decay_values):
    conv_output = conv_silu(padded, conv_table)
    seq_count, row_count, channels = conv_output.shape
    head_count = step_raw.shape[-1]
    inner_width = channels - 2 * NS
    head_inputs = conv_output[..., :inner_width].reshape(
        seq_count, row_count, head_count, inner_width // head_count
    )
    write_vectors = conv_output[..., inner_width : inner_width + NS]
    read_vectors = conv_output[..., inner_width + NS :]
    step_size = jax.nn.softplus(step_raw + bias_values)
    decay_rate = step_size * -jnp.exp(decay_values)
    block_count = row_count // SPAN

    def to_blocks(values):
        return jnp.moveaxis(values.reshape((seq_count, block_count, SPAN) + values.shape[2:]), 1, 0)

    def from_blocks(values):
        return jnp.moveaxis(values, 0, 1).reshape((seq_count, row_count) + values.shape[3:])

    def advance(carry, pieces):
        carry_state, offset = carry
        updated, output, cumulative = block_step(carry_state, pieces)
        return ((updated, offset + cumulative[:, -1]), (output, cumulative + offset[:, None, :]))

    initial = (
        jnp.zeros((seq_count, head_count, inner_width // head_count, NS), jnp.float32),
        jnp.zeros((seq_count, head_count), jnp.float32),
    )
    (final_state, total_rate), (outputs, cumulatives) = lax.scan(
        advance,
        initial,
        (
            to_blocks(head_inputs),
            to_blocks(write_vectors),
            to_blocks(read_vectors),
            to_blocks(step_size),
            to_blocks(decay_rate),
        ),
    )
    return (
        from_blocks(outputs),
        head_inputs,
        read_vectors,
        from_blocks(cumulatives),
        final_state,
        jnp.exp(total_rate),
    )


def mamba_finish(local_out, head_inputs, read_vectors, cumulative, incoming, skip_values, gate_z):
    carried = (
        jnp.einsum("gtn,ghpn->gthp", read_vectors, incoming, precision=HIGHEST)
        * jnp.exp(cumulative)[..., None]
    )
    values = local_out + carried + skip_values[:, None] * head_inputs
    return values.reshape(gate_z.shape) * jax.nn.silu(gate_z)


def dot(a, b):
    return jnp.dot(a, b, preferred_element_type=jnp.float32)


def dot_t(a, b):
    return lax.dot_general(a, b, (((1,), (1,)), ((), ())), preferred_element_type=jnp.float32)


def t_dot(a, b):
    return lax.dot_general(a, b, (((0,), (0,)), ((), ())), preferred_element_type=jnp.float32)


def shards(
    tokens,
    out_grad,
    norm_gains,
    query_weight,
    key_value_matrix,
    output_weight,
    mixer_weight,
    state_weight,
    step_weight,
    conv_inner,
    conv_state,
    step_bias,
    decay_log,
    skip_scale,
    gated_gain,
    mamba_weight,
    gateup_weight,
    down_weight,
):
    seq_count, row_count, model_width = tokens.shape
    total_rows = seq_count * row_count
    context_index = lax.axis_index("ctx")
    tensor_index = lax.axis_index("tp")
    tensor_count = lax.axis_size("tp")
    key_length = row_count * lax.axis_size("ctx")
    query_width = query_weight.shape[1]
    query_heads = query_width // HEAD_DIMENSION
    state_heads = step_bias.shape[0]
    inner_width = state_heads * MP
    hidden = down_weight.shape[0]
    own_rows = query_weight.shape[0]
    score_scale = HEAD_DIMENSION ** (-0.5)

    c_state = inner_width
    c_gate = c_state + 2 * NS
    c_query = c_gate + inner_width
    c_pair = c_query + query_width
    c_step = c_pair + 2 * HEAD_DIMENSION
    c_gain = c_step + state_heads
    pad = -(c_gain + 2) % 128
    mixer_parts = jnp.swapaxes(mixer_weight.reshape(own_rows, state_heads, 2, MP), 1, 2).reshape(
        own_rows, 2, inner_width
    )
    first_pack = jnp.concatenate(
        [
            mixer_parts[:, 1],
            state_weight,
            mixer_parts[:, 0],
            query_weight,
            key_value_matrix.reshape(own_rows, -1),
            step_weight,
            norm_gains.T,
            jnp.zeros((own_rows, pad), jnp.bfloat16),
        ],
        axis=1,
    )
    second_pack = jnp.concatenate(
        [gateup_weight.reshape(own_rows, 2 * hidden), down_weight.T, mamba_weight.T, output_weight.T],
        axis=1,
    )
    first_all = lax.all_gather(first_pack, WEIGHT_AXES, axis=0, tiled=True)
    second_all = lax.all_gather(second_pack, WEIGHT_AXES, axis=0, tiled=True)
    gateup_all = second_all[:, : 2 * hidden]
    down_all = second_all[:, 2 * hidden : 3 * hidden]
    mix_all = second_all[:, 3 * hidden :]

    residual = tokens.astype(jnp.float32).reshape(total_rows, model_width)
    first_inverse = rms_inverse(residual)
    first_gain = first_all[:, c_gain].astype(jnp.float32)
    second_gain = first_all[:, c_gain + 1].astype(jnp.float32)
    normed_one = (residual * first_inverse * first_gain).astype(jnp.bfloat16)
    cosines, sines = rope_tables(context_index * row_count, row_count, HEAD_DIMENSION)
    cos_grid = cosines[None, :, None, :]
    sin_grid = sines[None, :, None, :]
    conv_in = dot(normed_one, first_all[:, :c_gate]).astype(jnp.bfloat16).reshape(
        seq_count, row_count, c_gate
    )
    gate_z = dot(normed_one, first_all[:, c_gate:c_query]).reshape(
        seq_count, row_count, inner_width
    )
    small_lin = dot(normed_one, first_all[:, c_query:])
    query_lin = small_lin[:, :query_width].reshape(
        seq_count, row_count, query_heads, HEAD_DIMENSION
    )
    rotated_query = rotate(query_lin, cos_grid, sin_grid).astype(jnp.bfloat16)
    pair_lin = small_lin[:, query_width : query_width + 2 * HEAD_DIMENSION].reshape(
        seq_count, row_count, 2 * HEAD_DIMENSION
    )
    step_raw = small_lin[:, c_step - c_query : c_gain - c_query].reshape(
        seq_count, row_count, state_heads
    )
    key_rot = rotate(pair_lin[:, :, None, :HEAD_DIMENSION], cos_grid, sin_grid)[:, :, 0, :].astype(
        jnp.bfloat16
    )
    local_pairs = jnp.concatenate(
        [key_rot, pair_lin[..., HEAD_DIMENSION:].astype(jnp.bfloat16)], axis=-1
    )
    all_pairs = gather_ctx(local_pairs, 1)
    rim_width = conv_inner.shape[0] - 2
    rim_rows = shift_along(conv_in[:, row_count - rim_width :], "ctx", 1)

    query_rows = jnp.transpose(rotated_query, (0, 2, 1, 3)).reshape(
        seq_count, query_heads * row_count, HEAD_DIMENSION
    )
    query_place = context_index * row_count + jnp.tile(jnp.arange(row_count), query_heads)
    visible = jnp.arange(key_length)[None, :] <= query_place[:, None]

    def attend(pieces):
        query_one, pair_one = pieces
        logits = dot_t(query_one, pair_one[:, :HEAD_DIMENSION]) * score_scale
        logits = jnp.where(visible, logits, MASKED)
        largest = jnp.max(logits, axis=-1, keepdims=True)
        log_total = largest + jnp.log(jnp.sum(jnp.exp(logits - largest), axis=-1, keepdims=True))
        prob_low = jnp.exp(logits - log_total).astype(jnp.bfloat16)
        return (dot(prob_low, pair_one[:, HEAD_DIMENSION:]), log_total[:, 0])

    attended_rows, log_totals = lax.map(attend, (query_rows, all_pairs))
    attended = (
        jnp.transpose(
            attended_rows.reshape(seq_count, query_heads, row_count, HEAD_DIMENSION), (0, 2, 1, 3)
        )
        .reshape(total_rows, query_width)
        .astype(jnp.bfloat16)
    )
    padded = jnp.concatenate([rim_rows, conv_in], axis=1).astype(jnp.float32)
    conv_table = jnp.concatenate([conv_inner, conv_state], axis=1).astype(jnp.float32)
    local_values, local_back = jax.vjp(
        mamba_local,
        padded,
        conv_table,
        step_raw,
        step_bias.astype(jnp.float32),
        decay_log.astype(jnp.float32),
    )
    local_out, head_inputs, read_vectors, cumulative, final_state, block_decay = local_values
    incoming = carry_over(block_decay, final_state, True)
    gated_values, finish_back = jax.vjp(
        mamba_finish,
        local_out,
        head_inputs,
        read_vectors,
        cumulative,
        incoming,
        skip_scale.astype(jnp.float32),
        gate_z,
    )
    gated = gated_values.reshape(total_rows, inner_width)
    gate_gain = gated_gain.astype(jnp.float32)
    square_sum = sum_over(jnp.sum(gated * gated, axis=-1), "tp")
    gate_inverse = lax.rsqrt(square_sum / (inner_width * tensor_count) + EPSILON)[:, None]
    gated_low = (gated * gate_inverse * gate_gain).astype(jnp.bfloat16)
    mixed = jnp.concatenate([gated_low, attended], axis=1)
    branch = sum_over(dot_t(mixed, mix_all), "tp")
    middle = residual + branch
    second_inverse = rms_inverse(middle)
    normed_two = (middle * second_inverse * second_gain).astype(jnp.bfloat16)
    gate_val = dot(normed_two, gateup_all[:, :hidden])
    up_val = dot(normed_two, gateup_all[:, hidden:])
    sigmoid_gate = jax.nn.sigmoid(gate_val)
    silu_gate = gate_val * sigmoid_gate
    act_low = (silu_gate * up_val).astype(jnp.bfloat16)
    share_width = model_width // tensor_count
    feed_part = dot_t(act_low, down_all).astype(jnp.bfloat16)
    if tensor_count == 2:
        start_own = tensor_index * share_width
        own_part = lax.dynamic_slice_in_dim(feed_part, start_own, share_width, 1)
        other_part = lax.dynamic_slice_in_dim(feed_part, share_width - start_own, share_width, 1)
        feed_share = own_part.astype(jnp.float32) + lax.ppermute(
            other_part, "tp", [(0, 1), (1, 0)]
        ).astype(jnp.float32)
    else:
        feed_share = lax.psum_scatter(feed_part, "tp", scatter_dimension=1, tiled=True).astype(
            jnp.float32
        )
    middle_share = lax.dynamic_slice_in_dim(middle, tensor_index * share_width, share_width, 1)
    out_block = (
        (middle_share + feed_share).astype(jnp.bfloat16).reshape(seq_count, row_count, share_width)
    )
    cotangent = out_grad.reshape(total_rows, model_width)
    act_grad = dot(cotangent, down_all)
    gate_grad = (act_grad * up_val * sigmoid_gate * (1.0 + gate_val * (1.0 - sigmoid_gate))).astype(
        jnp.bfloat16
    )
    up_grad = (act_grad * silu_gate).astype(jnp.bfloat16)
    both_grads = jnp.concatenate([gate_grad, up_grad], axis=1)
    normed_two_grad = sum_over(dot_t(both_grads, gateup_all), "tp")
    second_back, second_gain_grad = norm_back(middle, second_inverse, second_gain, normed_two_grad)
    middle_grad = cotangent.astype(jnp.float32) + second_back
    branch_grad = middle_grad.astype(jnp.bfloat16)
    second_grads = jnp.concatenate(
        [
            t_dot(normed_two, both_grads).astype(jnp.bfloat16),
            t_dot(cotangent, act_low).astype(jnp.bfloat16),
            t_dot(branch_grad, mixed).astype(jnp.bfloat16),
        ],
        axis=1,
    )
    second_total = lax.psum_scatter(second_grads, WEIGHT_AXES, scatter_dimension=0, tiled=True)

    mixed_grad = dot(branch_grad, mix_all)
    attended_grad = mixed_grad[:, inner_width:].astype(jnp.bfloat16)
    gated_low_grad = mixed_grad[:, :inner_width]
    attended_grad_rows = jnp.transpose(
        attended_grad.reshape(seq_count, row_count, query_heads, HEAD_DIMENSION), (0, 2, 1, 3)
    ).reshape(seq_count, query_heads * row_count, HEAD_DIMENSION)

    def attend_back(pieces):
        query_one, pair_one, total_one, grad_one = pieces
        key_one = pair_one[:, :HEAD_DIMENSION]
        value_one = pair_one[:, HEAD_DIMENSION:]
        logits = dot_t(query_one, key_one) * score_scale
        logits = jnp.where(visible, logits, MASKED)
        prob_full = jnp.exp(logits - total_one[:, None])
        prob_grad = dot_t(grad_one, value_one)
        row_inner = jnp.sum(prob_full * prob_grad, axis=-1, keepdims=True)
        logit_grad = (prob_full * (prob_grad - row_inner)).astype(jnp.bfloat16)
        query_part = dot(logit_grad, key_one) * score_scale
        key_part = t_dot(logit_grad, query_one) * score_scale
        value_part = t_dot(prob_full.astype(jnp.bfloat16), grad_one)
        return (query_part, jnp.concatenate([key_part, value_part], axis=-1))

    coupling = sum_over(jnp.sum(gated_low_grad * gate_gain * gated, axis=-1), "tp")[:, None]
    query_grad_rows, pair_grad_all = lax.map(
        attend_back, (query_rows, all_pairs, log_totals, attended_grad_rows)
    )
    pair_grad = scatter_sum_ctx(pair_grad_all.astype(jnp.bfloat16), 1).astype(jnp.float32)
    query_grad = jnp.transpose(
        query_grad_rows.reshape(seq_count, query_heads, row_count, HEAD_DIMENSION), (0, 2, 1, 3)
    )
    query_lin_grad = (
        rotate(query_grad, cos_grid, -sin_grid)
        .reshape(total_rows, query_width)
        .astype(jnp.bfloat16)
    )
    key_lin_grad = rotate(pair_grad[:, :, None, :HEAD_DIMENSION], cos_grid, -sin_grid)[:, :, 0, :]
    pair_lin_grad = (
        jnp.concatenate([key_lin_grad, pair_grad[..., HEAD_DIMENSION:]], axis=-1)
        .reshape(total_rows, 2 * HEAD_DIMENSION)
        .astype(jnp.bfloat16)
    )
    gated_gain_grad = jnp.sum(gated_low_grad * gated * gate_inverse, axis=0)
    gated_grad = gate_inverse * gate_gain * gated_low_grad - gated * gate_inverse**3 * coupling / (
        inner_width * tensor_count
    )
    local_grad, inputs_grad, read_grad, cumulative_grad, incoming_grad, skip_grad, gate_z_grad = (
        finish_back(gated_grad.reshape(seq_count, row_count, inner_width))
    )
    later_grad = carry_over(block_decay, incoming_grad, False)
    decay_grad = jnp.sum(later_grad * incoming, axis=(2, 3))
    padded_grad, table_grad, step_raw_grad, bias_grad, decay_log_grad = local_back(
        (local_grad, inputs_grad, read_grad, cumulative_grad, later_grad, decay_grad)
    )
    rim_grad = shift_along(padded_grad[:, :rim_width].astype(jnp.bfloat16), "ctx", -1).astype(
        jnp.float32
    )
    conv_grad = padded_grad[:, rim_width:] + jnp.pad(
        rim_grad, ((0, 0), (row_count - rim_width, 0), (0, 0))
    )
    first_grads = jnp.concatenate(
        [
            conv_grad.reshape(total_rows, c_gate).astype(jnp.bfloat16),
            gate_z_grad.reshape(total_rows, inner_width).astype(jnp.bfloat16),
            query_lin_grad,
            pair_lin_grad,
            step_raw_grad.reshape(total_rows, state_heads).astype(jnp.bfloat16),
            jnp.zeros((total_rows, 2 + pad), jnp.bfloat16),
        ],
        axis=1,
    )
    first_total = lax.psum_scatter(
        t_dot(normed_one, first_grads).astype(jnp.bfloat16),
        WEIGHT_AXES,
        scatter_dimension=0,
        tiled=True,
    )
    normed_one_grad = sum_over(dot_t(first_grads, first_all), "tp")
    first_back, first_gain_grad = norm_back(residual, first_inverse, first_gain, normed_one_grad)
    tokens_grad = (middle_grad + first_back).reshape(seq_count, row_count, model_width)

    state_table = sum_over(table_grad[:, inner_width:], "tp")
    flat = jnp.concatenate(
        [
            table_grad[:, :inner_width].reshape(-1),
            state_table.reshape(-1),
            gated_gain_grad,
            bias_grad,
            decay_log_grad,
            skip_grad,
            first_gain_grad,
            second_gain_grad,
        ]
    )
    flat_size = flat.shape[0]
    flat = jnp.pad(flat, (0, -flat_size % 1024)).reshape(-1, 128)
    for axis in WEIGHT_AXES:
        flat = sum_over(flat, axis)
    flat = flat.reshape(-1)
    tap_rows = conv_inner.shape[0]
    sizes = (
        tap_rows * inner_width,
        tap_rows * 2 * NS,
        inner_width,
        state_heads,
        state_heads,
        state_heads,
        model_width,
        model_width,
    )
    pieces, start = [], 0
    for size in sizes:
        pieces.append(flat[start : start + size])
        start += size
    conv_inner_total = pieces[0].reshape(tap_rows, inner_width)
    conv_state_total = pieces[1].reshape(tap_rows, 2 * NS)
    gated_total, bias_total, decay_total, skip_total = pieces[2:6]
    gain_start = (lax.axis_index("fsdp") * lax.axis_size("ctx") + context_index) * own_rows
    gain_total = lax.dynamic_slice_in_dim(jnp.stack(pieces[6:8]), gain_start, own_rows, 1)

    wide_one = first_total.astype(jnp.float32)
    wide_two = second_total.astype(jnp.float32)
    mixer_total = jnp.stack(
        [
            wide_one[:, c_gate:c_query].reshape(own_rows, state_heads, MP),
            wide_one[:, :inner_width].reshape(own_rows, state_heads, MP),
        ],
        axis=2,
    ).reshape(own_rows, state_heads, 2 * MP)
    state_weight_total = sum_over(wide_one[:, c_state:c_gate], "tp")
    return (
        out_block,
        tokens_grad,
        gain_total,
        wide_one[:, c_query:c_pair],
        wide_one[:, c_pair:c_step].reshape(own_rows, 1, 2 * HEAD_DIMENSION),
        wide_two[:, 3 * hidden + inner_width :].T,
        mixer_total,
        state_weight_total,
        wide_one[:, c_step:c_gain],
        conv_inner_total,
        conv_state_total,
        bias_total,
        decay_total,
        skip_total,
        gated_total,
        wide_two[:, 3 * hidden : 3 * hidden + inner_width].T,
        wide_two[:, : 2 * hidden].reshape(own_rows, 2, hidden),
        wide_two[:, 2 * hidden : 3 * hidden].T,
    )


def solution(mesh):
    in_specs = (
        P("fsdp", "ctx", None),
        P("fsdp", "ctx", None),
        P(None, ("fsdp", "ctx")),
        P(("fsdp", "ctx"), "tp"),
        P(("fsdp", "ctx"), "tp", None),
        P("tp", ("fsdp", "ctx")),
        P(("fsdp", "ctx"), "tp", None),
        P(("fsdp", "ctx"), None),
        P(("fsdp", "ctx"), "tp"),
        P(None, "tp"),
        P(),
        P("tp"),
        P("tp"),
        P("tp"),
        P("tp"),
        P("tp", ("fsdp", "ctx")),
        P(("fsdp", "ctx"), None, "tp"),
        P("tp", ("fsdp", "ctx")),
    )
    out_specs = (
        P("fsdp", "ctx", "tp"),
        P("fsdp", "ctx", None),
        P(None, ("fsdp", "ctx")),
        P(("fsdp", "ctx"), "tp"),
        P(("fsdp", "ctx"), "tp", None),
        P("tp", ("fsdp", "ctx")),
        P(("fsdp", "ctx"), "tp", None),
        P(("fsdp", "ctx"), None),
        P(("fsdp", "ctx"), "tp"),
        P(None, "tp"),
        P(),
        P("tp"),
        P("tp"),
        P("tp"),
        P("tp"),
        P("tp", ("fsdp", "ctx")),
        P(("fsdp", "ctx"), None, "tp"),
        P("tp", ("fsdp", "ctx")),
    )
    return jax.shard_map(shards, mesh=mesh, in_specs=in_specs, out_specs=out_specs, check_vma=False)
```

time: 2190 us -> 1070 us (0.49)
  waiting for transfers between devices: 1060 us -> 348 us
  blocking collectives: 359 us -> 0 us
  matrix products: 306 us -> 266 us
    reduce_scatter x10 -> x2, waiting for transfers between devices: 866 us -> 244 us  [the longest x1 173 us: shards(): lax.psum_scatter(second_grads, WEIGHT_AXES, scatter_dimension=0, tiled=True)]
    all_gather x10 -> x0, blocking collectives: 274 us -> none  [the longest x1 42.4 us: fetch_weights(): lax.all_gather(norm_gains, ('fsdp', 'ctx'), axis=1, tiled=True)]
    psum x4 -> x0, blocking collectives: 85.6 us -> none  [the longest x1 77.8 us: shards(): lax.psum((table_grad[:, :inner_width], conv_state_grad, bias_grad, decay_...]
    all_gather x4 -> x2, waiting for transfers between devices: 126 us -> 73.5 us  [the longest x1 73.5 us: shards(): first_all = lax.all_gather(first_pack, WEIGHT_AXES, axis=0, tiled=True)]
    psum x3 -> x0, waiting for transfers between devices: 38.4 us -> none  [the longest x1 22.3 us: shards(): branch = lax.psum(branch_part, 'tp')]
    dot_general x41 -> x37, matrix products: 161 us -> 126 us  [the longest x10 45.9 us: dot_t(): lax.dot_general(a, b, (((1,), (1,)), ((), ())), preferred_element_type=jn...]
    ppermute x2 -> x18, waiting for transfers between devices: 0.01 us -> 30.2 us  [the longest x11 16.5 us: sum_over(): other = lax.ppermute(value, axis, [(i, i ^ stride) for i in range(count)])]
    unnamed x21 -> x4, waiting for transfers between devices: 25.1 us -> 0.07 us
  transfers between devices with their start and end apart: 21 -> 22, of which waited for: 15 -> 11; matrix products, arithmetic and copies ran while one was open for 18% -> 35% of each run, Pallas kernels for 0% -> 0%
where the time goes in v1:
time: 1070 us; the launch traced here: 1060 us
  waiting for transfers between devices  348 us (33%)
  matrix products  266 us (25%)
  local copies, waits for them, and re-layouts  216 us (20%)
  other arithmetic  192 us (18%)
  starting transfers between devices  19.8 us (2%)
  between operations  15.9 us (1%)
    reduce_scatter x1, waiting for transfers between devices, shards(): lax.psum_scatter(second_grads, WEIGHT_AXES, scatter_dimension=0, tiled=True)  173 us
    all_gather x1, waiting for transfers between devices, shards(): first_all = lax.all_gather(first_pack, WEIGHT_AXES, axis=0, tiled=True)  73.5 us
    reduce_scatter x1, waiting for transfers between devices, shards(): lax.psum_scatter(t_dot(normed_one, first_grads).astype(jnp.bfloat16), WEI...  70.6 us
    dot_general x12, matrix products, block_step(): inside = jnp.einsum('gtsh,gshp->gthp', mixing, block_x, precision=HIGHEST)  60 us
    dot_general x10, matrix products, dot_t(): lax.dot_general(a, b, (((1,), (1,)), ((), ())), preferred_element_type=jn...  45.9 us
    dot_general x11, matrix products, dot(): return jnp.dot(a, b, preferred_element_type=jnp.float32)  35.2 us
    dot_general x8, matrix products, t_dot(): lax.dot_general(a, b, (((0,), (0,)), ((), ())), preferred_element_type=jn...  34.4 us
    dynamic_update_slice x20, other arithmetic, mamba_local(): lax.scan(advance, initial, (to_blocks(head_inputs), to_blocks(write_vecto...  31 us
  transfers between devices with their start and end apart: 22, of which 11 were waited for; matrix products, arithmetic and copies ran while one was open for 35% of the time, Pallas kernels for 0%

profile of v1, /device:TPU:0, one launch (start us, length us, event | category | flops | bytes accessed | tf_op | source)
XLA Modules:
  0.0 1057.6 jit_solution(17266928560989186213)
XLA Ops:
  22.2 73.5 %all-gather.3.cloned.1.call-done = bf16[1024,2304]{1,0:T(8,128)(2,1)} async-done(((bf16[64,2304]{1,0:T(8,128)(2,1)}), bf16[1024,2304]{1,0:T(8,128)(2,1)}) %all-gather.3.cloned.1.call-update) | async-done | bytes 4718608 | tf_op jit(solution)/shard_map/all_gather | solution.py:281
  158.2 104.8 %while.107 = (s32[]{:T(128)}, f32[2,12,64,128]{3,2,1,0:T(8,128)S(1)}, f32[2,12]{1,0:T(2,128)}, f32[4,2,128,12,64]{2,4,3,1,0:T(8,128)}, f32[4,2,128,12]{2,0,1,3:T...) while((s32[]{:T(128)}, ...), condition=%wide.region_2.3_spmd.clone.clone.clone, body=%wide.region_1.2_spmd.clone.clone.sunk.clone | while | flops 965977152 | bytes 29535440 | solution.py:178
  275.1 7.6 fusion.196
  282.8 16.0 %copy.312 = f32[2,512,768]{2,1,0:T(8,128)} copy(f32[2,512,768]{1,2,0:T(8,128)} %bitcast.820) | data formatting | bytes 6291456 | tf_op jit(solution)/shard_map/jvp()/reshape | solution.py:205
  298.8 6.2 multiply_reduce_fusion.10
  305.2 16.2 %while.104 = (s32[]{:T(128)}, bf16[2,2048,64]{1,2,0:T(8,128)(2,1)S(1)}, f32[2,2048]{1,0:T(2,128)S(1)}, bf16[2,2048,64]{2,1,0:T(8,128)(2,1)}, bf16[2,1024,128]{2,1,0:T(8,128)(2,1)}, /*index=5*/s32[2048]{0:T(1024)S(1)}) while((s32[]{:T(128)}, bf16[2,2048,64]{1,2,0:T(8,128)(2,1)S(1)}, f32[2,2048]{1,0:T(2,128)S(1)}, ...), condition=%wide.region_7.8_spmd.clone.clone, body=%wide.region_4.7_spmd.clone.sunk.clone | while | flops 566228992 | bytes 27361872 | solution.py:337
  349.9 6.5 fusion.174
  357.5 6.4 collective-permute-done.6
  363.9 6.6 multiply_reduce_fusion.1
  384.7 50.2 %while.106 = (s32[]{:T(128)}, f32[2,2048,64]{1,2,0:T(8,128)}, bf16[2,1024,128]{1,2,0:T(8,128)(2,1)S(1)}, bf16[2,2048,64]{2,1,0:T(8,128)(2,1)S(1)}, bf16[2,1024,1...) while((s32[]{:T(128)}, f32[2,2048,64]{1,2,0:T(8,128)}, ...), condition=%wide.region_25.26_spmd.clone.clone, body=%wide.region_23.25_spmd.clone.sunk.clone | while | flops 1363933184 | bytes 103335064 | solution.py:443
  394.0 8.0 multiply_convert_fusion.5
  419.0 8.0 multiply_convert_fusion.5
  442.6 8.9 multiply_reduce_fusion.8
  471.9 9.0 collective-permute-done.8
  487.2 178.2 %while.105 = (s32[]{:T(128)}, f32[2,12,64,128]{3,2,1,0:T(8,128)S(1)}, f32[2,12]{1,0:T(2,128)}, f32[4,2,128,12,64]{2,4,3,1,0:T(8,128)}, f32[4,2,128,128]{3,2,1,0:...) while((s32[]{:T(128)}, ...), condition=%wide.region_22.23_spmd.clone.clone, body=%wide.region_13.22_spmd.clone.sunk.clone | while | flops 1923718144 | bytes 24831064 | solution.py:178
  491.6 5.9 fusion.433
  536.1 5.9 fusion.433
  668.7 6.1 copy.333
  711.6 7.4 concatenate.74
  719.0 9.4 convolution_convert_fusion
  734.2 6.2 convolution_convert_fusion.1
  746.7 10.3 fusion.285
  794.7 70.6 %reduce-scatter.3.cloned.1.call-done = bf16[64,2304]{1,0:T(8,128)(2,1)} async-done(((bf16[1024,2304]{1,0:T(8,128)(2,1)}), bf16[64,2304]{1,0:T(8,128)(2,1)}) %reduce-scatter.3.cloned.1.call-update) | async-done | bytes 294928 | tf_op jit(solution)/shard_map/reduce_scatter | solution.py:490
  871.9 173.3 %reduce-scatter.5.cloned.1.call-done = bf16[64,4096]{1,0:T(8,128)(2,1)} async-done(((bf16[1024,4096]{1,0:T(8,128)(2,1)}), bf16[64,4096]{1,0:T(8,128)(2,1)}) %reduce-scatter.5.cloned.1.call-update) | async-done | bytes 524304 | tf_op jit(solution)/shard_map/reduce_scatter | solution.py:418
  (798 shorter events, 588.9 us)
Async XLA Ops:
  7.3 88.4 %all-gather.3.cloned.1.call-start = ((), (), s32[]{:S(2)}) async-start(), calls=%async_computation.2 | async-start | bytes 5013504 | tf_op jit(solution)/shard_map/all_gather | solution.py:281
  12.4 314.4 %all-gather.5.cloned.1.call-start = ((), (), s32[]{:S(2)}) async-start(), calls=%async_computation.3 | async-start | bytes 8912896 | tf_op jit(solution)/shard_map/all_gather | solution.py:282
  15.1 850.2 %reduce-scatter.3.cloned.1.call-start = ((), (), s32[]{:S(2)}) async-start(), calls=%async_computation.4 | async-start | bytes 5013504 | tf_op jit(solution)/shard_map/reduce_scatter | solution.py:490
  21.2 108.0 %copy-start.83 = (f32[1,1024]{1,0:T(1,128)}, f32[1,1024]{1,0:T(1,128)S(1)}, u32[]{:S(2)}) copy-start(f32[1,1024]{1,0:T(1,128)S(1)} %get-tuple-element.1899) | copy-start | bytes 12292
  21.2 108.0 %copy-start.85 = (f32[1,1024]{1,0:T(1,128)}, f32[1,1024]{1,0:T(1,128)S(1)}, u32[]{:S(2)}) copy-start(f32[1,1024]{1,0:T(1,128)S(1)} %get-tuple-element.1900) | copy-start | bytes 12292
  106.5 20.4 %collective-permute-start = (bf16[2,3,1024]{2,1,0:T(4,128)(2,1)}, bf16[2,3,1024]{2,1,0:T(4,128)(2,1)}, u32[]{:S(2)}, u32[]{:S(2)}) collective-permute-start(bf16[2,3,1024]{2,1,0:T(4,128)(2,1)} %slice.313), channel_id=1, source_target_pairs={{0,2},{1,3},{4,6},{5,7},{8,10},{9,11},{12,14},{13,15},{16,18},{17,... | collective-permute-start | bytes 36872 | tf_op jit(solution)/shard_map/ppermute | solution.py:22
  116.4 152.4 %collective-permute-start.3 = (bf16[2,512,128]{1,2,0:T(8,128)(2,1)}, bf16[2,512,128]{1,2,0:T(8,128)(2,1)}, u32[]{:S(2)}, u32[]{:S(2)}) collective-permute-start(bf16[2,512,128]{1,2,0:T(8,128)(2,1)} %pad_maximum_fusion.11), channel_id=1, source_target_pairs={{0,2},{2,0},{1,3},{3,1},{4,6},{6,4},{5,7},{7,5},{8,10},{10,8},{9,1... | collective-permute-start | bytes 786440 | tf_op jit(solution)/shard_map/ppermute | solution.py:43
  264.0 11.1 %collective-permute-start.1 = (bf16[2,12,64,128]{3,2,1,0:T(8,128)(2,1)}, bf16[2,12,64,128]{3,2,1,0:T(8,128)(2,1)S(1)}, u32[]{:S(2)}, u32[]{:S(2)}) collective-permute-start(bf16[2,12,64,128]{3,2,1,0:T(8,128)(2,1)} %convert_element_type.203), channel_id=1, source_target_pairs={{0,2},{1,3},{4,6},{5,7},{8,10},{9,11},{12,14},{13,15},{16,18},{17,... | collective-permute-start | bytes 1179656 | tf_op jit(solution)/shard_map/ppermute | solution.py:22
  305.1 17.6 %collective-permute-start.2 = (f32[1024]{0:T(1024)S(1)}, f32[1024]{0:T(1024)S(1)}, u32[]{:S(2)}, u32[]{:S(2)}) collective-permute-start(f32[1024]{0:T(1024)S(1)} %bitcast.892), channel_id=1, source_target_pairs={{0,1},{1,0},{2,3},{3,2},{4,5},{5,4},{6,7},{7,6},{8,9},{9,8},{10,11... | collective-permute-start | bytes 12296 | tf_op jit(solution)/shard_map/ppermute | solution.py:31
  331.3 7.3 collective-permute-start.4
  356.4 7.5 collective-permute-start.6
  382.3 60.2 %collective-permute-start.7 = (f32[1024]{0:T(1024)S(1)}, f32[1024]{0:T(1024)S(1)}, u32[]{:S(2)}, u32[]{:S(2)}) collective-permute-start(f32[1024]{0:T(1024)S(1)} %get-tuple-element.1679), channel_id=1, source_target_pairs={{0,1},{1,0},{2,3},{3,2},{4,5},{5,4},{6,7},{7,6},{8,9},{9,8},{10,11... | collective-permute-start | bytes 12296 | tf_op jit(solution)/shard_map/ppermute | solution.py:31
  435.0 35.1 %collective-permute-start.10 = (bf16[2,512,128]{1,2,0:T(8,128)(2,1)S(1)}, bf16[2,512,128]{1,2,0:T(8,128)(2,1)S(1)}, u32[]{:S(2)}, u32[]{:S(2)}) collective-permute-start(bf16[2,512,128]{1,2,0:T(8,128)(2,1)S(1)} %broadcast_select_fusion.1), channel_id=1, source_target_pairs={{0,2},{2,0},{1,3},{3,1},{4,6},{6,4},{5,7},{7,5},{8,10},{10,8},{9,1... | collective-permute-start | bytes 786440 | tf_op jit(solution)/shard_map/ppermute | solution.py:62
  468.1 12.8 %collective-permute-start.8 = (bf16[2,12,64,128]{3,2,1,0:T(8,128)(2,1)S(1)}, bf16[2,12,64,128]{3,2,1,0:T(8,128)(2,1)S(1)}, u32[]{:S(2)}, u32[]{:S(2)}) collective-permute-start(bf16[2,12,64,128]{3,2,1,0:T(8,128)(2,1)S(1)} %fusion.232), channel_id=1, source_target_pairs={{2,0},{3,1},{6,4},{7,5},{10,8},{11,9},{14,12},{15,13},{18,16},{19,... | collective-permute-start | bytes 1179656 | tf_op jit(solution)/shard_map/ppermute | solution.py:22
  705.1 5.8 collective-permute-start.9
  728.5 316.8 %reduce-scatter.5.cloned.1.call-start = ((), (), s32[]{:S(2)}) async-start(), calls=%async_computation.5 | async-start | bytes 8912896 | tf_op jit(solution)/shard_map/reduce_scatter | solution.py:418
  757.0 9.5 collective-permute-start.11
  763.6 13.4 %collective-permute-start.5 = (bf16[1024,512]{1,0:T(8,128)(2,1)}, bf16[1024,512]{1,0:T(8,128)(2,1)}, u32[]{:S(2)}, u32[]{:S(2)}) collective-permute-start(bf16[1024,512]{1,0:T(8,128)(2,1)} %constant_dynamic-slice_fusion.8), channel_id=1, source_target_pairs={{0,1},{1,0},{2,3},{3,2},{4,5},{5,4},{6,7},{7,6},{8,9},{9,8},{10,11... | collective-permute-start | bytes 3145736 | tf_op jit(solution)/shard_map/ppermute | solution.py:388
  764.6 1.9 collective-permute-start.12
  771.7 4.1 collective-permute-start.13
  775.8 4.9 collective-permute-start.14
  780.6 5.2 collective-permute-start.15
  785.9 5.7 collective-permute-start.16
  866.8 4.5 collective-permute-start.17
  (153 other events, 1442.2 us)
Sparse Core Ops, SparseCore 0:
  12.5 83.1 all-gather.2
  98.9 111.5 all-gather.4
  728.6 136.6 reduce-scatter.2
  867.6 177.6 reduce-scatter.4

commit v2 on v1

--- a/solution.py
+++ b/solution.py
@@ -1,6 +1,10 @@
+import functools
+
 import jax
 import jax.numpy as jnp
 from jax import lax
+from jax.experimental import pallas as pl
+from jax.experimental.pallas import tpu as pltpu
 from jax.sharding import PartitionSpec as P
 
 HEAD_DIMENSION = 64
@@ -14,6 +18,9 @@
 MASKED = -1e30
 ROPE_BASE = 10000.0
 WEIGHT_AXES = ("fsdp", "ctx")
+VMEM_LIMIT = 48 * 1024 * 1024
+TAPS = 4
+EDGE = 16
 
 
 def shift_along(block, axis, distance):
@@ -62,21 +69,138 @@
     return kept + lax.ppermute(sent, "ctx", [(0, 1), (1, 0)])
 
 
-def carry_over(decay, state, forward):
+def carry_over(total_rate, state, forward):
     count = lax.axis_size("ctx")
     if count <= 2:
-        moved = shift_along(state.astype(jnp.bfloat16), "ctx", 1 if forward else -1)
-        return moved.astype(jnp.float32)
+        return shift_along(state, "ctx", 1 if forward else -1)
     place = lax.axis_index("ctx")
-    decays = lax.all_gather(decay.astype(jnp.bfloat16), "ctx").astype(jnp.float32)
-    states = lax.all_gather(state.astype(jnp.bfloat16), "ctx").astype(jnp.float32)
-    total = jnp.zeros_like(state)
+    heads = state.shape[2] // MP
+    decay = jnp.exp(total_rate[:, :, :heads]).astype(jnp.bfloat16)
+    decays = jnp.repeat(lax.all_gather(decay, "ctx").astype(jnp.float32), MP, axis=3)
+    states = lax.all_gather(state, "ctx").astype(jnp.float32)
+    total = jnp.zeros(state.shape, jnp.float32)
     order = range(count) if forward else range(count - 1, -1, -1)
     for k in order:
         reached = k < place if forward else k > place
-        new = decays[k][:, :, None, None] * total + states[k]
-        total = jnp.where(reached, new, total)
-    return total
+        total = jnp.where(reached, decays[k] * total + states[k], total)
+    return total.astype(jnp.bfloat16)
+
+
+def torus_route(step):
+    def index(z, x, y):
+        return (z * 2 + x) * 2 + y
+
+    return [
+        (index(z, x, y), index(*step(z, x, y)))
+        for z in range(4)
+        for x in range(2)
+        for y in range(2)
+    ]
+
+
+def across(value, name, hop=1):
+    step = {
+        "x": lambda z, x, y: (z, 1 - x, y),
+        "y": lambda z, x, y: (z, x, 1 - y),
+        "z": lambda z, x, y: ((z + hop) % 4, x, y),
+    }[name]
+    return lax.ppermute(value, WEIGHT_AXES, torus_route(step))
+
+
+def is_torus():
+    return lax.axis_size("fsdp") == 8 and lax.axis_size("ctx") == 2
+
+
+def torus_place():
+    fsdp = lax.axis_index("fsdp")
+    return {"z": fsdp // 2, "x": fsdp % 2, "y": lax.axis_index("ctx")}
+
+
+def gather_weights(shard, order):
+    if not is_torus():
+        return lax.all_gather(shard, WEIGHT_AXES, axis=0, tiled=True)
+    place = torus_place()
+    done = ""
+    value = shard
+    for name in order:
+        spot = sum(1 for other in "zxy" if other in done and "zxy".index(other) < "zxy".index(name))
+        if name == "z":
+            parts = [value] + [across(value, "z", hop) for hop in (1, 2, 3)]
+            gathered = jnp.zeros((4, *value.shape), value.dtype)
+            for hop, part in enumerate(parts):
+                gathered = lax.dynamic_update_index_in_dim(
+                    gathered, part, (place["z"] - hop) % 4, 0
+                )
+            value = gathered
+        else:
+            other = across(value, name)
+            low = place[name] == 0
+            value = jnp.stack(
+                [jnp.where(low, value, other), jnp.where(low, other, value)], axis=spot
+            )
+        done += name
+    return value.reshape(-1, shard.shape[1])
+
+
+def scatter_begin(whole):
+    if not is_torus():
+        return lax.psum_scatter(whole, WEIGHT_AXES, scatter_dimension=0, tiled=True), ""
+    return whole.reshape(4, 2, 2, -1, whole.shape[1]), "zxy"
+
+
+def scatter_stage(state, name):
+    value, left = state
+    if not left:
+        return state
+    place = torus_place()[name]
+    dim = left.index(name)
+
+    def part(at):
+        return lax.dynamic_index_in_dim(value, at, dim, keepdims=False)
+
+    total = part(place).astype(jnp.float32)
+    if name == "z":
+        for hop in (1, 2, 3):
+            total = total + across(part((place + hop) % 4), "z", hop).astype(jnp.float32)
+    else:
+        total = total + across(part(1 - place), name).astype(jnp.float32)
+    left = left.replace(name, "")
+    return (total.astype(jnp.bfloat16) if left else total), left
+
+
+def scatter_end(state):
+    return state[0].astype(jnp.float32)
+
+
+def scatter_weights(whole, order):
+    state = scatter_begin(whole)
+    for name in order:
+        state = scatter_stage(state, name)
+    return scatter_end(state)
+
+
+def scatter_gain(values):
+    if not is_torus():
+        return lax.psum_scatter(values, WEIGHT_AXES, scatter_dimension=0, tiled=True)
+    place = torus_place()
+    value = values.reshape(4, 4, -1)
+
+    def part(array, at):
+        return lax.dynamic_index_in_dim(array, at, 0, keepdims=False)
+
+    total = part(value, place["z"])
+    for hop in (1, 2, 3):
+        total = total + across(part(value, (place["z"] + hop) % 4), "z", hop)
+    result = part(total, 2 * place["x"] + place["y"])
+    for dx, dy in ((0, 1), (1, 0), (1, 1)):
+        sent = part(total, 2 * (place["x"] ^ dx) + (place["y"] ^ dy))
+        route = torus_route(lambda z, x, y: (z, x ^ dx, y ^ dy))
+        result = result + lax.ppermute(sent, WEIGHT_AXES, route)
+    return result
+
+
+def tie(*values):
+    return lax.optimization_barrier(values)
 
 
 def rms_inverse(values):
@@ -108,103 +232,6 @@
     )
 
 
-def conv_silu(padded, conv_table):
-    tap_count = conv_table.shape[0] - 1
-    length_out = padded.shape[1] - tap_count + 1
-    summed = conv_table[tap_count]
-    for tap_index in range(tap_count):
-        summed = summed + conv_table[tap_index] * padded[:, tap_index : tap_index + length_out]
-    return jax.nn.silu(summed)
-
-
-def running_sum(values):
-    length = values.shape[1]
-    ones = (jnp.arange(length)[:, None] >= jnp.arange(length)[None, :]).astype(jnp.float32)
-    return jnp.einsum("ts,gsh->gth", ones, values, precision=HIGHEST)
-
-
-def block_step(carry_state, pieces):
-    block_x, block_write, block_read, block_size, block_rate = pieces
-    block_len = block_x.shape[1]
-    cumulative = running_sum(block_rate)
-    lower_mask = jnp.arange(block_len)[:, None] >= jnp.arange(block_len)[None, :]
-    log_decay = jnp.where(
-        lower_mask[None, :, :, None], cumulative[:, :, None, :] - cumulative[:, None, :, :], MASKED
-    )
-    intersection = jnp.einsum("gtn,gsn->gts", block_read, block_write, precision=HIGHEST)
-    mixing = intersection[..., None] * jnp.exp(log_decay) * block_size[:, None, :, :]
-    inside = jnp.einsum("gtsh,gshp->gthp", mixing, block_x, precision=HIGHEST)
-    carried = (
-        jnp.einsum("gtn,ghpn->gthp", block_read, carry_state, precision=HIGHEST)
-        * jnp.exp(cumulative)[..., None]
-    )
-    tail_decay = jnp.exp(cumulative[:, -1:, :] - cumulative) * block_size
-    fresh_state = jnp.einsum(
-        "gsh,gshp,gsn->ghpn", tail_decay, block_x, block_write, precision=HIGHEST
-    )
-    updated = carry_state * jnp.exp(cumulative[:, -1])[:, :, None, None] + fresh_state
-    return (updated, inside + carried, cumulative)
-
-
-def mamba_local(padded, conv_table, step_raw, bias_values, decay_values):
-    conv_output = conv_silu(padded, conv_table)
-    seq_count, row_count, channels = conv_output.shape
-    head_count = step_raw.shape[-1]
-    inner_width = channels - 2 * NS
-    head_inputs = conv_output[..., :inner_width].reshape(
-        seq_count, row_count, head_count, inner_width // head_count
-    )
-    write_vectors = conv_output[..., inner_width : inner_width + NS]
-    read_vectors = conv_output[..., inner_width + NS :]
-    step_size = jax.nn.softplus(step_raw + bias_values)
-    decay_rate = step_size * -jnp.exp(decay_values)
-    block_count = row_count // SPAN
-
-    def to_blocks(values):
-        return jnp.moveaxis(values.reshape((seq_count, block_count, SPAN) + values.shape[2:]), 1, 0)
-
-    def from_blocks(values):
-        return jnp.moveaxis(values, 0, 1).reshape((seq_count, row_count) + values.shape[3:])
-
-    def advance(carry, pieces):
-        carry_state, offset = carry
-        updated, output, cumulative = block_step(carry_state, pieces)
-        return ((updated, offset + cumulative[:, -1]), (output, cumulative + offset[:, None, :]))
-
-    initial = (
-        jnp.zeros((seq_count, head_count, inner_width // head_count, NS), jnp.float32),
-        jnp.zeros((seq_count, head_count), jnp.float32),
-    )
-    (final_state, total_rate), (outputs, cumulatives) = lax.scan(
-        advance,
-        initial,
-        (
-            to_blocks(head_inputs),
-            to_blocks(write_vectors),
-            to_blocks(read_vectors),
-            to_blocks(step_size),
-            to_blocks(decay_rate),
-        ),
-    )
-    return (
-        from_blocks(outputs),
-        head_inputs,
-        read_vectors,
-        from_blocks(cumulatives),
-        final_state,
-        jnp.exp(total_rate),
-    )
-
-
-def mamba_finish(local_out, head_inputs, read_vectors, cumulative, incoming, skip_values, gate_z):
-    carried = (
-        jnp.einsum("gtn,ghpn->gthp", read_vectors, incoming, precision=HIGHEST)
-        * jnp.exp(cumulative)[..., None]
-    )
-    values = local_out + carried + skip_values[:, None] * head_inputs
-    return values.reshape(gate_z.shape) * jax.nn.silu(gate_z)
-
-
 def dot(a, b):
     return jnp.dot(a, b, preferred_element_type=jnp.float32)
 
@@ -215,6 +242,460 @@
 
 def t_dot(a, b):
     return lax.dot_general(a, b, (((0,), (0,)), ((), ())), preferred_element_type=jnp.float32)
+
+
+def tall(kernel, grid, in_specs, out_specs, out_shape, scratch, flops, moved, exps):
+    return pl.pallas_call(
+        kernel,
+        grid=grid,
+        in_specs=in_specs,
+        out_specs=out_specs,
+        out_shape=out_shape,
+        scratch_shapes=scratch,
+        compiler_params=pltpu.CompilerParams(
+            dimension_semantics=("arbitrary",) * len(grid), vmem_limit_bytes=VMEM_LIMIT
+        ),
+        cost_estimate=pl.CostEstimate(flops=flops, bytes_accessed=moved, transcendentals=exps),
+    )
+
+
+def lower_ones(transposed=False):
+    rows = lax.broadcasted_iota(jnp.int32, (SPAN, SPAN), 0)
+    columns = lax.broadcasted_iota(jnp.int32, (SPAN, SPAN), 1)
+    return rows <= columns if transposed else rows >= columns
+
+
+def exact_dot(a, b):
+    return jnp.dot(a, b, preferred_element_type=jnp.float32, precision=HIGHEST)
+
+
+def split_dot(a, b):
+    high = a.astype(jnp.bfloat16)
+    rest = (a - high.astype(jnp.float32)).astype(jnp.bfloat16)
+    return dot(high, b) + dot(rest, b)
+
+
+def pair_lanes(columns, pair):
+    rows = columns.shape[0]
+    lane = lax.broadcasted_iota(jnp.int32, (rows, 2 * MP), 1)
+    left = jnp.broadcast_to(columns[:, 2 * pair : 2 * pair + 1], (rows, 2 * MP))
+    right = jnp.broadcast_to(columns[:, 2 * pair + 1 : 2 * pair + 2], (rows, 2 * MP))
+    return jnp.where(lane < MP, left, right)
+
+
+def head_lanes(columns, pairs):
+    return jnp.concatenate([pair_lanes(columns, j) for j in range(pairs)], axis=1)
+
+
+def stacked_pair(values):
+    lane = lax.broadcasted_iota(jnp.int32, values.shape, 1)
+    zero = jnp.zeros_like(values)
+    return jnp.concatenate(
+        [jnp.where(lane < MP, values, zero), jnp.where(lane < MP, zero, values)], axis=0
+    )
+
+
+def load_window(window, edge_ref, before_ref, block_ref, first):
+    edge = jnp.where(first, edge_ref[0].astype(jnp.float32), before_ref[...].astype(jnp.float32))
+    window[0:EDGE, :] = edge
+    window[EDGE:, :] = block_ref[...].astype(jnp.float32)
+
+
+def window_conv(window, taps, lanes):
+    total = taps[TAPS : TAPS + 1, lanes]
+    for k in range(TAPS):
+        start = EDGE - TAPS + 1 + k
+        total = total + taps[k : k + 1, lanes] * window[start : start + SPAN, lanes]
+    return total
+
+
+def step_values(raw, heads):
+    argument = raw + heads[0:1, :]
+    size = jnp.maximum(argument, 0.0) + jnp.log1p(jnp.exp(-jnp.abs(argument)))
+    rate = size * heads[1:2, :]
+    return size, exact_dot(lower_ones().astype(jnp.float32), rate), rate, argument
+
+
+def state_kernel(pairs, last, edge_ref, before_ref, block_ref, raw_ref, taps, heads, state_out, total_out, window, state, total):
+    block = pl.program_id(1)
+    inner = pairs * 2 * MP
+
+    @pl.when(block == 0)
+    def _():
+        state[...] = jnp.zeros_like(state)
+        total[...] = jnp.zeros_like(total)
+
+    load_window(window, edge_ref, before_ref, block_ref, block == 0)
+    conv = window_conv(window, taps, slice(0, inner + NS))
+    conv = conv * jax.nn.sigmoid(conv)
+    size, running, _, _ = step_values(raw_ref[...], heads[...])
+    final = running[SPAN - 1 : SPAN, :]
+    weight = jnp.exp(final - running) * size
+    weighted = (conv[:, :inner] * head_lanes(weight, pairs)).astype(jnp.bfloat16)
+    write_t = conv[:, inner:].T.astype(jnp.bfloat16)
+    state[...] = state[...] * head_lanes(jnp.exp(final), pairs) + dot(write_t, weighted)
+    total[...] = total[...] + final
+
+    @pl.when(block == last)
+    def _():
+        state_out[0] = state[...].astype(jnp.bfloat16)
+        total_out[0] = total[...]
+
+
+def forward_kernel(pairs, edge_ref, before_ref, block_ref, raw_ref, taps, heads, gate_ref, skip_ref, incoming_ref, y_out, gated_out, square_out, entering_out, leaving_out, window, state):
+    block = pl.program_id(1)
+    inner = pairs * 2 * MP
+
+    @pl.when(block == 0)
+    def _():
+        state[...] = incoming_ref[0].astype(jnp.float32)
+
+    load_window(window, edge_ref, before_ref, block_ref, block == 0)
+    conv = window_conv(window, taps, slice(0, inner + 2 * NS))
+    conv = conv * jax.nn.sigmoid(conv)
+    head_x = conv[:, :inner]
+    write = conv[:, inner : inner + NS]
+    read_low = conv[:, inner + NS :].astype(jnp.bfloat16)
+    write_low = write.astype(jnp.bfloat16)
+    size, running, _, _ = step_values(raw_ref[...], heads[...])
+    running_t = running.T
+    final = running[SPAN - 1 : SPAN, :]
+    mask = lower_ones()
+    product = dot_t(read_low, write_low)
+    entering = state[...].astype(jnp.bfloat16)
+    entering_out[0, 0] = entering
+    carried = dot(read_low, entering) * head_lanes(jnp.exp(running), pairs)
+    stepped = head_x * head_lanes(size, pairs)
+    stepped_low = stepped.astype(jnp.bfloat16)
+    inside = []
+    for pair in range(pairs):
+        mixing = []
+        for head in (2 * pair, 2 * pair + 1):
+            gap = running[:, head : head + 1] - running_t[head : head + 1, :]
+            mixing.append((product * jnp.exp(jnp.where(mask, gap, MASKED))).astype(jnp.bfloat16))
+        lanes = slice(pair * 2 * MP, (pair + 1) * 2 * MP)
+        inside.append(dot(jnp.concatenate(mixing, axis=1), stacked_pair(stepped_low[:, lanes])))
+    y = jnp.concatenate(inside, axis=1) + carried + skip_ref[0:1, :] * head_x
+    gate = gate_ref[...]
+    gated = y * (gate * jax.nn.sigmoid(gate))
+    y_out[...] = y
+    gated_out[...] = gated
+    square_out[...] = jnp.sum(gated * gated, axis=1, keepdims=True)
+    weighted = (stepped * head_lanes(jnp.exp(final - running), pairs)).astype(jnp.bfloat16)
+    state[...] = state[...] * head_lanes(jnp.exp(final), pairs) + dot(
+        write.T.astype(jnp.bfloat16), weighted
+    )
+    leaving_out[0, 0] = state[...].astype(jnp.bfloat16)
+
+
+def gate_back_kernel(pairs, channels, last, edge_ref, before_ref, block_ref, raw_ref, taps, heads, gate_ref, y_ref, low_grad_ref, inverse_ref, coupling_ref, gain_ref, gate_grad_out, y_grad_out, gain_out, state_grad_out, window, state_grad, total):
+    block = pl.program_id(1)
+    first_of_all = (block == 0) & (pl.program_id(0) == 0)
+    inner = pairs * 2 * MP
+
+    @pl.when(block == 0)
+    def _():
+        state_grad[...] = jnp.zeros_like(state_grad)
+        total[...] = jnp.zeros_like(total)
+
+    @pl.when(first_of_all)
+    def _():
+        gain_out[...] = jnp.zeros_like(gain_out)
+
+    gate = gate_ref[...]
+    y = y_ref[...]
+    low_grad = low_grad_ref[...]
+    inverse = inverse_ref[...]
+    sigmoid = jax.nn.sigmoid(gate)
+    silu = gate * sigmoid
+    gated = y * silu
+    normed = gated * inverse
+    gain_out[0:1, :] += jnp.sum(low_grad * normed, axis=0, keepdims=True)
+    gated_grad = inverse * (
+        gain_ref[0:1, :] * low_grad - normed * (inverse * coupling_ref[...] / channels)
+    )
+    y_grad = (gated_grad * silu).astype(jnp.bfloat16)
+    y_grad_out[...] = y_grad
+    gate_grad_out[...] = (gated_grad * y * (sigmoid * (1.0 + gate * (1.0 - sigmoid)))).astype(
+        jnp.bfloat16
+    )
+    lanes = slice(inner + NS, inner + 2 * NS)
+    load_window(window, edge_ref, before_ref, block_ref, block == 0)
+    read = window_conv(window, taps, lanes)
+    read = read * jax.nn.sigmoid(read)
+    _, running, _, _ = step_values(raw_ref[...], heads[...])
+    scaled = (
+        y_grad.astype(jnp.float32) * head_lanes(jnp.exp(total[...] + running), pairs)
+    ).astype(jnp.bfloat16)
+    state_grad[...] += dot(read.T.astype(jnp.bfloat16), scaled)
+    total[...] = total[...] + running[SPAN - 1 : SPAN, :]
+
+    @pl.when(block == last)
+    def _():
+        state_grad_out[0] = state_grad[...].astype(jnp.bfloat16)
+
+
+def backward_kernel(pairs, last, edge_ref, before_ref, block_ref, raw_ref, taps, heads, skip_ref, later_ref, entering_ref, leaving_ref, y_ref, y_grad_ref, conv_grad_out, step_grad_out, front_out, taps_out, heads_out, skip_out, window, state_grad, slopes):
+    block = last - pl.program_id(1)
+    first_step = pl.program_id(1) == 0
+    inner = pairs * 2 * MP
+
+    @pl.when(first_step)
+    def _():
+        state_grad[...] = later_ref[0].astype(jnp.float32)
+        slopes[SPAN:, :] = jnp.zeros((8, slopes.shape[1]), jnp.float32)
+
+    @pl.when(first_step & (pl.program_id(0) == 0))
+    def _():
+        taps_out[...] = jnp.zeros_like(taps_out)
+        heads_out[...] = jnp.zeros_like(heads_out)
+        skip_out[...] = jnp.zeros_like(skip_out)
+
+    load_window(window, edge_ref, before_ref, block_ref, block == 0)
+    before_silu = window_conv(window, taps, slice(0, inner + 2 * NS))
+    sigmoid = jax.nn.sigmoid(before_silu)
+    conv = before_silu * sigmoid
+    head_x = conv[:, :inner]
+    write = conv[:, inner : inner + NS]
+    read = conv[:, inner + NS :]
+    write_low = write.astype(jnp.bfloat16)
+    read_low = read.astype(jnp.bfloat16)
+    size, running, rate, argument = step_values(raw_ref[...], heads[...])
+    running_t = running.T
+    final = running[SPAN - 1 : SPAN, :]
+    mask = lower_ones()
+    mask_t = lower_ones(True)
+    product = dot_t(read_low, write_low)
+    product_t = dot_t(write_low, read_low)
+    grad_low = y_grad_ref[...]
+    grad = grad_low.astype(jnp.float32)
+    entering = entering_ref[0, 0]
+    state_low = state_grad[...].astype(jnp.bfloat16)
+    grown = head_lanes(jnp.exp(running), pairs)
+    tail = head_lanes(jnp.exp(final - running), pairs)
+    size_lanes = head_lanes(size, pairs)
+    stepped = head_x * size_lanes
+    stepped_low = stepped.astype(jnp.bfloat16)
+    from_state = dot(write_low, state_low) * tail
+    product_grad = jnp.zeros((SPAN, SPAN), jnp.float32)
+    slope_parts = []
+    lane = lax.broadcasted_iota(jnp.int32, (SPAN, 2 * MP), 1)
+    for pair in range(pairs):
+        lanes = slice(pair * 2 * MP, (pair + 1) * 2 * MP)
+        pair_grad = grad_low[:, lanes]
+        mixing_t = []
+        for side in (0, 1):
+            head = 2 * pair + side
+            column = running[:, head : head + 1]
+            row = running_t[head : head + 1, :]
+            decay = jnp.exp(jnp.where(mask, column - row, MASKED))
+            decay_t = jnp.exp(jnp.where(mask_t, row - column, MASKED))
+            mixing_t.append((product_t * decay_t).astype(jnp.bfloat16))
+            own = (lane < MP) if side == 0 else (lane >= MP)
+            one_head = jnp.where(own, pair_grad, jnp.zeros_like(pair_grad))
+            product_grad = product_grad + dot_t(one_head, stepped_low[:, lanes]) * decay
+        slope_parts.append(dot(jnp.concatenate(mixing_t, axis=1), stacked_pair(pair_grad)))
+    slope = jnp.concatenate(slope_parts, axis=1) + from_state
+    skip = skip_ref[0:1, :]
+    x_grad = size_lanes * slope + skip * grad
+    skip_out[0:1, :] += jnp.sum(grad * head_x, axis=0, keepdims=True)
+    owner = lax.broadcasted_iota(jnp.int32, (inner, SPAN), 0) // MP
+    ones = (owner == lax.broadcasted_iota(jnp.int32, (inner, SPAN), 1)).astype(jnp.bfloat16)
+    y_scan = y_ref[...] - skip * head_x
+    running_grad = split_dot(grad * y_scan - stepped * slope, ones)
+    size_direct = split_dot(head_x * slope, ones)
+    at_end = jnp.sum(
+        state_grad[...] * leaving_ref[0, 0].astype(jnp.float32), axis=0, keepdims=True
+    )
+    at_end = split_dot(jnp.broadcast_to(at_end, (8, inner)), ones)[0:1, :]
+    rate_grad = exact_dot(mask_t.astype(jnp.float32), running_grad) + at_end
+    size_grad = size_direct + rate_grad * heads[1:2, :]
+    valid = lax.broadcasted_iota(jnp.int32, (SPAN, SPAN), 1) < 2 * pairs
+    raw_grad = jnp.where(valid, size_grad * jax.nn.sigmoid(argument), 0.0)
+    step_grad_out[...] = raw_grad.astype(jnp.bfloat16)
+    heads_out[0:1, :] += jnp.sum(raw_grad, axis=0, keepdims=True)
+    heads_out[1:2, :] += jnp.sum(rate_grad * rate, axis=0, keepdims=True)
+    grown_grad = (grad * grown).astype(jnp.bfloat16)
+    product_grad_low = product_grad.astype(jnp.bfloat16)
+    read_grad = dot(product_grad_low, write_low) + dot_t(grown_grad, entering)
+    write_grad = dot(product_grad.T.astype(jnp.bfloat16), read_low) + dot_t(
+        (stepped * tail).astype(jnp.bfloat16), state_low
+    )
+    state_grad[...] = state_grad[...] * head_lanes(jnp.exp(final), pairs) + dot(
+        read.T.astype(jnp.bfloat16), grown_grad
+    )
+    conv_slope = jnp.concatenate([x_grad, write_grad, read_grad], axis=1) * (
+        sigmoid * (1.0 + before_silu * (1.0 - sigmoid))
+    )
+    slopes[0:SPAN, :] = conv_slope
+    taps_out[TAPS : TAPS + 1, :] += jnp.sum(conv_slope, axis=0, keepdims=True)
+    total = jnp.zeros_like(conv_slope)
+    for k in range(TAPS):
+        start = EDGE - TAPS + 1 + k
+        taps_out[k : k + 1, :] += jnp.sum(
+            conv_slope * window[start : start + SPAN, :], axis=0, keepdims=True
+        )
+        ahead = TAPS - 1 - k
+        total = total + taps[k : k + 1, :] * slopes[ahead : ahead + SPAN, :]
+    conv_grad_out[...] = total.astype(jnp.bfloat16)
+    slopes[SPAN:, :] = conv_slope[0:8, :]
+
+    @pl.when(block == 0)
+    def _():
+        front_out[0] = conv_slope[0:EDGE, :].astype(jnp.bfloat16)
+
+
+class Mixer:
+    def __init__(self, conv_in, edge, step_lin, taps, heads, skip, gate_z, seq_count, step_block):
+        self.seqs = seq_count
+        self.rows = conv_in.shape[0] // seq_count
+        self.blocks = self.rows // SPAN
+        self.inner = gate_z.shape[1]
+        self.pairs = self.inner // (2 * MP)
+        self.width = conv_in.shape[1]
+        self.base = (edge, conv_in, conv_in, step_lin, taps, heads)
+        self.step_block = step_block
+        self.skip, self.gate_z = skip, gate_z
+        self.grid = (seq_count, self.blocks)
+
+    def where(self, reverse):
+        blocks = self.blocks
+        return (lambda g, b: blocks - 1 - b) if reverse else (lambda g, b: b)
+
+    def base_specs(self, reverse=False):
+        at, blocks, per = self.where(reverse), self.blocks, SPAN // EDGE
+        width, column = self.width, self.step_block
+        return [
+            pl.BlockSpec((1, EDGE, width), lambda g, b: (g, 0, 0)),
+            pl.BlockSpec(
+                (EDGE, width), lambda g, b: (g * blocks * per + jnp.maximum(at(g, b) * per - 1, 0), 0)
+            ),
+            pl.BlockSpec((SPAN, width), lambda g, b: (g * blocks + at(g, b), 0)),
+            pl.BlockSpec((SPAN, SPAN), lambda g, b: (g * blocks + at(g, b), column)),
+            pl.BlockSpec((8, width), lambda g, b: (0, 0)),
+            pl.BlockSpec((8, SPAN), lambda g, b: (0, 0)),
+        ]
+
+    def rows_spec(self, width, reverse=False, dtype=None):
+        at, blocks = self.where(reverse), self.blocks
+        return pl.BlockSpec((SPAN, width), lambda g, b: (g * blocks + at(g, b), 0))
+
+    def const_spec(self, width, rows=8):
+        return pl.BlockSpec((rows, width), lambda g, b: (0, 0))
+
+    def seq_spec(self, rows, width):
+        return pl.BlockSpec((1, rows, width), lambda g, b: (g, 0, 0))
+
+    def cost(self, products, arrays):
+        count = self.seqs * self.blocks
+        return (
+            2 * count * products * SPAN * SPAN * self.inner,
+            arrays * self.seqs * self.rows * self.inner,
+            count * 2 * self.pairs * SPAN * SPAN,
+        )
+
+    def shape(self, width, dtype):
+        return jax.ShapeDtypeStruct((self.seqs * self.rows, width), dtype)
+
+    def window(self):
+        return pltpu.VMEM((SPAN + EDGE, self.width), jnp.float32)
+
+    def states(self):
+        inner, last = self.inner, self.blocks - 1
+        return tall(
+            functools.partial(state_kernel, self.pairs, last),
+            self.grid,
+            self.base_specs(),
+            [self.seq_spec(NS, inner), self.seq_spec(1, SPAN)],
+            [
+                jax.ShapeDtypeStruct((self.seqs, NS, inner), jnp.bfloat16),
+                jax.ShapeDtypeStruct((self.seqs, 1, SPAN), jnp.float32),
+            ],
+            [self.window(), pltpu.VMEM((NS, inner), jnp.float32), pltpu.VMEM((1, SPAN), jnp.float32)],
+            *self.cost(1, 3),
+        )(*self.base)
+
+    def forward(self, incoming):
+        inner, blocks = self.inner, self.blocks
+        rows = self.rows_spec
+        saved = pl.BlockSpec((1, 1, NS, inner), lambda g, b: (g, b, 0, 0))
+        return tall(
+            functools.partial(forward_kernel, self.pairs),
+            self.grid,
+            [*self.base_specs(), rows(inner), self.const_spec(inner), self.seq_spec(NS, inner)],
+            [rows(inner), rows(inner), rows(1), saved, saved],
+            [
+                self.shape(inner, jnp.float32),
+                self.shape(inner, jnp.float32),
+                self.shape(1, jnp.float32),
+                jax.ShapeDtypeStruct((self.seqs, blocks, NS, inner), jnp.bfloat16),
+                jax.ShapeDtypeStruct((self.seqs, blocks, NS, inner), jnp.bfloat16),
+            ],
+            [self.window(), pltpu.VMEM((NS, inner), jnp.float32)],
+            *self.cost(4, 18),
+        )(*self.base, self.gate_z, self.skip, incoming)
+
+    def gate_back(self, y, low_grad, inverse, coupling, gain, channels):
+        inner, last = self.inner, self.blocks - 1
+        rows = self.rows_spec
+        return tall(
+            functools.partial(gate_back_kernel, self.pairs, channels, last),
+            self.grid,
+            [
+                *self.base_specs(),
+                *(rows(width) for width in (inner, inner, inner, 1, 1)),
+                self.const_spec(inner),
+            ],
+            [rows(inner), rows(inner), self.const_spec(inner), self.seq_spec(NS, inner)],
+            [
+                self.shape(inner, jnp.bfloat16),
+                self.shape(inner, jnp.bfloat16),
+                jax.ShapeDtypeStruct((8, inner), jnp.float32),
+                jax.ShapeDtypeStruct((self.seqs, NS, inner), jnp.bfloat16),
+            ],
+            [self.window(), pltpu.VMEM((NS, inner), jnp.float32), pltpu.VMEM((1, SPAN), jnp.float32)],
+            *self.cost(1, 20),
+        )(*self.base, self.gate_z, y, low_grad, inverse, coupling, gain)
+
+    def backward(self, later, entering, leaving, y, y_grad):
+        inner, width, last = self.inner, self.width, self.blocks - 1
+        saved = pl.BlockSpec((1, 1, NS, inner), lambda g, b: (g, last - b, 0, 0))
+        back = functools.partial(self.rows_spec, reverse=True)
+        return tall(
+            functools.partial(backward_kernel, self.pairs, last),
+            self.grid,
+            [
+                *self.base_specs(True),
+                self.const_spec(inner),
+                self.seq_spec(NS, inner),
+                saved,
+                saved,
+                back(inner),
+                back(inner),
+            ],
+            [
+                back(width),
+                back(SPAN),
+                self.seq_spec(EDGE, width),
+                self.const_spec(width),
+                self.const_spec(SPAN),
+                self.const_spec(inner),
+            ],
+            [
+                self.shape(width, jnp.bfloat16),
+                self.shape(SPAN, jnp.bfloat16),
+                jax.ShapeDtypeStruct((self.seqs, EDGE, width), jnp.bfloat16),
+                jax.ShapeDtypeStruct((8, width), jnp.float32),
+                jax.ShapeDtypeStruct((8, SPAN), jnp.float32),
+                jax.ShapeDtypeStruct((8, inner), jnp.float32),
+            ],
+            [
+                self.window(),
+                pltpu.VMEM((NS, inner), jnp.float32),
+                pltpu.VMEM((SPAN + 8, width), jnp.float32),
+            ],
+            *self.cost(9, 16),
+        )(*self.base, self.skip, later, entering, leaving, y, y_grad)
 
 
 def shards(
@@ -261,11 +742,9 @@
     mixer_parts = jnp.swapaxes(mixer_weight.reshape(own_rows, state_heads, 2, MP), 1, 2).reshape(
         own_rows, 2, inner_width
     )
-    first_pack = jnp.concatenate(
+    pack_conv = jnp.concatenate([mixer_parts[:, 1], state_weight], axis=1)
+    pack_small = jnp.concatenate(
         [
-            mixer_parts[:, 1],
-            state_weight,
-            mixer_parts[:, 0],
             query_weight,
             key_value_matrix.reshape(own_rows, -1),
             step_weight,
@@ -278,7 +757,10 @@
         [gateup_weight.reshape(own_rows, 2 * hidden), down_weight.T, mamba_weight.T, output_weight.T],
         axis=1,
     )
-    first_all = lax.all_gather(first_pack, WEIGHT_AXES, axis=0, tiled=True)
+    small_all = gather_weights(pack_small, "xyz")
+    conv_all = gather_weights(pack_conv, "zxy")
+    gate_all = gather_weights(mixer_parts[:, 0], "yzx")
+    second_pack, small_all, conv_all, gate_all = tie(second_pack, small_all, conv_all, gate_all)
     second_all = lax.all_gather(second_pack, WEIGHT_AXES, axis=0, tiled=True)
     gateup_all = second_all[:, : 2 * hidden]
     down_all = second_all[:, 2 * hidden : 3 * hidden]
@@ -286,19 +768,15 @@
 
     residual = tokens.astype(jnp.float32).reshape(total_rows, model_width)
     first_inverse = rms_inverse(residual)
-    first_gain = first_all[:, c_gain].astype(jnp.float32)
-    second_gain = first_all[:, c_gain + 1].astype(jnp.float32)
+    first_gain = small_all[:, c_gain - c_query].astype(jnp.float32)
+    second_gain = small_all[:, c_gain + 1 - c_query].astype(jnp.float32)
     normed_one = (residual * first_inverse * first_gain).astype(jnp.bfloat16)
     cosines, sines = rope_tables(context_index * row_count, row_count, HEAD_DIMENSION)
     cos_grid = cosines[None, :, None, :]
     sin_grid = sines[None, :, None, :]
-    conv_in = dot(normed_one, first_all[:, :c_gate]).astype(jnp.bfloat16).reshape(
-        seq_count, row_count, c_gate
-    )
-    gate_z = dot(normed_one, first_all[:, c_gate:c_query]).reshape(
-        seq_count, row_count, inner_width
-    )
-    small_lin = dot(normed_one, first_all[:, c_query:])
+    conv_in = dot(normed_one, conv_all).astype(jnp.bfloat16)
+    gate_z = dot(normed_one, gate_all)
+    small_lin = dot(normed_one, small_all)
     query_lin = small_lin[:, :query_width].reshape(
         seq_count, row_count, query_heads, HEAD_DIMENSION
     )
@@ -306,9 +784,6 @@
     pair_lin = small_lin[:, query_width : query_width + 2 * HEAD_DIMENSION].reshape(
         seq_count, row_count, 2 * HEAD_DIMENSION
     )
-    step_raw = small_lin[:, c_step - c_query : c_gain - c_query].reshape(
-        seq_count, row_count, state_heads
-    )
     key_rot = rotate(pair_lin[:, :, None, :HEAD_DIMENSION], cos_grid, sin_grid)[:, :, 0, :].astype(
         jnp.bfloat16
     )
@@ -316,8 +791,28 @@
         [key_rot, pair_lin[..., HEAD_DIMENSION:].astype(jnp.bfloat16)], axis=-1
     )
     all_pairs = gather_ctx(local_pairs, 1)
-    rim_width = conv_inner.shape[0] - 2
-    rim_rows = shift_along(conv_in[:, row_count - rim_width :], "ctx", 1)
+    conv_rows = conv_in.reshape(seq_count, row_count, c_gate)
+    edge = shift_along(conv_rows[:, row_count - EDGE :], "ctx", 1)
+    taps = jnp.pad(
+        jnp.concatenate([conv_inner, conv_state], axis=1).astype(jnp.float32),
+        ((0, 8 - conv_inner.shape[0]), (0, 0)),
+    )
+    head_rows = jnp.stack([step_bias.astype(jnp.float32), -jnp.exp(decay_log.astype(jnp.float32))])
+    head_rows = jnp.pad(head_rows, ((0, 6), (0, SPAN - state_heads)))
+    skip_rows = jnp.pad(jnp.repeat(skip_scale.astype(jnp.float32), MP)[None], ((0, 7), (0, 0)))
+    mixer = Mixer(
+        conv_in,
+        edge,
+        small_lin,
+        taps,
+        head_rows,
+        skip_rows,
+        gate_z,
+        seq_count,
+        (c_step - c_query) // SPAN,
+    )
+    final_state, total_rate = mixer.states()
+    incoming = carry_over(total_rate, final_state, True)
 
     query_rows = jnp.transpose(rotated_query, (0, 2, 1, 3)).reshape(
         seq_count, query_heads * row_count, HEAD_DIMENSION
@@ -342,32 +837,10 @@
         .reshape(total_rows, query_width)
         .astype(jnp.bfloat16)
     )
-    padded = jnp.concatenate([rim_rows, conv_in], axis=1).astype(jnp.float32)
-    conv_table = jnp.concatenate([conv_inner, conv_state], axis=1).astype(jnp.float32)
-    local_values, local_back = jax.vjp(
-        mamba_local,
-        padded,
-        conv_table,
-        step_raw,
-        step_bias.astype(jnp.float32),
-        decay_log.astype(jnp.float32),
-    )
-    local_out, head_inputs, read_vectors, cumulative, final_state, block_decay = local_values
-    incoming = carry_over(block_decay, final_state, True)
-    gated_values, finish_back = jax.vjp(
-        mamba_finish,
-        local_out,
-        head_inputs,
-        read_vectors,
-        cumulative,
-        incoming,
-        skip_scale.astype(jnp.float32),
-        gate_z,
-    )
-    gated = gated_values.reshape(total_rows, inner_width)
+    y_scan, gated, squares, entering, leaving = mixer.forward(incoming)
     gate_gain = gated_gain.astype(jnp.float32)
-    square_sum = sum_over(jnp.sum(gated * gated, axis=-1), "tp")
-    gate_inverse = lax.rsqrt(square_sum / (inner_width * tensor_count) + EPSILON)[:, None]
+    square_sum = sum_over(squares, "tp")
+    gate_inverse = lax.rsqrt(square_sum / (inner_width * tensor_count) + EPSILON)
     gated_low = (gated * gate_inverse * gate_gain).astype(jnp.bfloat16)
     mixed = jnp.concatenate([gated_low, attended], axis=1)
     branch = sum_over(dot_t(mixed, mix_all), "tp")
@@ -415,11 +888,11 @@
         ],
         axis=1,
     )
+    branch_grad, second_grads = lax.optimization_barrier((branch_grad, second_grads))
     second_total = lax.psum_scatter(second_grads, WEIGHT_AXES, scatter_dimension=0, tiled=True)
 
-    mixed_grad = dot(branch_grad, mix_all)
-    attended_grad = mixed_grad[:, inner_width:].astype(jnp.bfloat16)
-    gated_low_grad = mixed_grad[:, :inner_width]
+    attended_grad = dot(branch_grad, mix_all[:, inner_width:]).astype(jnp.bfloat16)
+    gated_low_grad = dot(branch_grad, mix_all[:, :inner_width])
     attended_grad_rows = jnp.transpose(
         attended_grad.reshape(seq_count, row_count, query_heads, HEAD_DIMENSION), (0, 2, 1, 3)
     ).reshape(seq_count, query_heads * row_count, HEAD_DIMENSION)
@@ -439,7 +912,15 @@
         value_part = t_dot(prob_full.astype(jnp.bfloat16), grad_one)
         return (query_part, jnp.concatenate([key_part, value_part], axis=-1))
 
-    coupling = sum_over(jnp.sum(gated_low_grad * gate_gain * gated, axis=-1), "tp")[:, None]
+    coupling = sum_over(
+        jnp.sum(gated_low_grad * gate_gain * gated, axis=-1, keepdims=True), "tp"
+    )
+    gain_rows = jnp.pad(gate_gain[None], ((0, 7), (0, 0)))
+    gate_z_grad, y_grad, gain_sums, incoming_grad = mixer.gate_back(
+        y_scan, gated_low_grad, gate_inverse, coupling, gain_rows, inner_width * tensor_count
+    )
+    gated_gain_grad = gain_sums[0]
+    later_grad = carry_over(total_rate, incoming_grad, False)
     query_grad_rows, pair_grad_all = lax.map(
         attend_back, (query_rows, all_pairs, log_totals, attended_grad_rows)
     )
@@ -458,42 +939,48 @@
         .reshape(total_rows, 2 * HEAD_DIMENSION)
         .astype(jnp.bfloat16)
     )
-    gated_gain_grad = jnp.sum(gated_low_grad * gated * gate_inverse, axis=0)
-    gated_grad = gate_inverse * gate_gain * gated_low_grad - gated * gate_inverse**3 * coupling / (
-        inner_width * tensor_count
-    )
-    local_grad, inputs_grad, read_grad, cumulative_grad, incoming_grad, skip_grad, gate_z_grad = (
-        finish_back(gated_grad.reshape(seq_count, row_count, inner_width))
-    )
-    later_grad = carry_over(block_decay, incoming_grad, False)
-    decay_grad = jnp.sum(later_grad * incoming, axis=(2, 3))
-    padded_grad, table_grad, step_raw_grad, bias_grad, decay_log_grad = local_back(
-        (local_grad, inputs_grad, read_grad, cumulative_grad, later_grad, decay_grad)
-    )
-    rim_grad = shift_along(padded_grad[:, :rim_width].astype(jnp.bfloat16), "ctx", -1).astype(
-        jnp.float32
-    )
-    conv_grad = padded_grad[:, rim_width:] + jnp.pad(
-        rim_grad, ((0, 0), (row_count - rim_width, 0), (0, 0))
-    )
-    first_grads = jnp.concatenate(
-        [
-            conv_grad.reshape(total_rows, c_gate).astype(jnp.bfloat16),
-            gate_z_grad.reshape(total_rows, inner_width).astype(jnp.bfloat16),
-            query_lin_grad,
-            pair_lin_grad,
-            step_raw_grad.reshape(total_rows, state_heads).astype(jnp.bfloat16),
-            jnp.zeros((total_rows, 2 + pad), jnp.bfloat16),
-        ],
-        axis=1,
-    )
-    first_total = lax.psum_scatter(
-        t_dot(normed_one, first_grads).astype(jnp.bfloat16),
-        WEIGHT_AXES,
-        scatter_dimension=0,
-        tiled=True,
-    )
-    normed_one_grad = sum_over(dot_t(first_grads, first_all), "tp")
+    early_grads = jnp.concatenate([gate_z_grad, query_lin_grad, pair_lin_grad], axis=1)
+    early = t_dot(normed_one, early_grads).astype(jnp.bfloat16)
+    early, y_grad = tie(early, y_grad)
+    early = scatter_stage(scatter_begin(early), "y")
+    conv_grad, step_grad, front_slopes, tap_sums, head_sums, skip_sums = mixer.backward(
+        later_grad, entering, leaving, y_scan, y_grad
+    )
+    early_value, conv_grad = tie(early[0], conv_grad)
+    early = scatter_stage((early_value, early[1]), "x")
+    table_grad = tap_sums[: conv_inner.shape[0]]
+    bias_grad = head_sums[0, :state_heads]
+    decay_log_grad = head_sums[1, :state_heads]
+    skip_grad = jnp.sum(skip_sums[0].reshape(state_heads, MP), axis=1)
+    rim = TAPS - 1
+    ahead = shift_along(front_slopes[:, :8], "ctx", -1).astype(jnp.float32)
+    rim_grad = jnp.stack(
+        [sum(taps[k] * ahead[:, i - k] for k in range(i + 1)) for i in range(rim)], axis=1
+    )
+    conv_grad = conv_grad.reshape(seq_count, row_count, c_gate)
+    ending = conv_grad[:, row_count - rim :].astype(jnp.float32) + rim_grad
+    conv_grad = lax.dynamic_update_slice_in_dim(
+        conv_grad, ending.astype(jnp.bfloat16), row_count - rim, 1
+    ).reshape(total_rows, c_gate)
+    late_grads = jnp.concatenate([conv_grad, step_grad], axis=1)
+    late = t_dot(normed_one, late_grads).astype(jnp.bfloat16)
+    late_width = late.shape[1] // 2 // SPAN * SPAN
+    late_one, late_two, late_grads = tie(late[:, :late_width], late[:, late_width:], late_grads)
+    late_one = scatter_stage(scatter_begin(late_one), "y")
+    late_two = scatter_stage(scatter_begin(late_two), "x")
+    small_grads = jnp.concatenate([query_lin_grad, pair_lin_grad, step_grad], axis=1)
+    normed_one_part = (
+        dot_t(conv_grad, conv_all) + dot_t(gate_z_grad, gate_all) + dot_t(small_grads, small_all)
+    )
+    late_value, early_value, normed_one_part = tie(late_one[0], early[0], normed_one_part)
+    late_one = scatter_stage((late_value, late_one[1]), "x")
+    late_two = scatter_stage(late_two, "y")
+    early = scatter_stage((early_value, early[1]), "z")
+    normed_one_grad = sum_over(normed_one_part, "tp")
+    late_total = jnp.concatenate(
+        [scatter_end(scatter_stage(late_one, "z")), scatter_end(scatter_stage(late_two, "z"))], axis=1
+    )
+    early_total = scatter_end(early)
     first_back, first_gain_grad = norm_back(residual, first_inverse, first_gain, normed_one_grad)
     tokens_grad = (middle_grad + first_back).reshape(seq_count, row_count, model_width)
 
@@ -506,8 +993,6 @@
             bias_grad,
             decay_log_grad,
             skip_grad,
-            first_gain_grad,
-            second_gain_grad,
         ]
     )
     flat_size = flat.shape[0]
@@ -523,8 +1008,6 @@
         state_heads,
         state_heads,
         state_heads,
-        model_width,
-        model_width,
     )
     pieces, start = [], 0
     for size in sizes:
@@ -533,29 +1016,27 @@
     conv_inner_total = pieces[0].reshape(tap_rows, inner_width)
     conv_state_total = pieces[1].reshape(tap_rows, 2 * NS)
     gated_total, bias_total, decay_total, skip_total = pieces[2:6]
-    gain_start = (lax.axis_index("fsdp") * lax.axis_size("ctx") + context_index) * own_rows
-    gain_total = lax.dynamic_slice_in_dim(jnp.stack(pieces[6:8]), gain_start, own_rows, 1)
-
-    wide_one = first_total.astype(jnp.float32)
+    gain_total = jnp.stack([scatter_gain(first_gain_grad), scatter_gain(second_gain_grad)])
+
     wide_two = second_total.astype(jnp.float32)
     mixer_total = jnp.stack(
         [
-            wide_one[:, c_gate:c_query].reshape(own_rows, state_heads, MP),
-            wide_one[:, :inner_width].reshape(own_rows, state_heads, MP),
+            early_total[:, :inner_width].reshape(own_rows, state_heads, MP),
+            late_total[:, :inner_width].reshape(own_rows, state_heads, MP),
         ],
         axis=2,
     ).reshape(own_rows, state_heads, 2 * MP)
-    state_weight_total = sum_over(wide_one[:, c_state:c_gate], "tp")
+    state_weight_total = sum_over(late_total[:, c_state:c_gate], "tp")
     return (
         out_block,
         tokens_grad,
         gain_total,
-        wide_one[:, c_query:c_pair],
-        wide_one[:, c_pair:c_step].reshape(own_rows, 1, 2 * HEAD_DIMENSION),
+        early_total[:, inner_width : inner_width + query_width],
+        early_total[:, inner_width + query_width :].reshape(own_rows, 1, 2 * HEAD_DIMENSION),
         wide_two[:, 3 * hidden + inner_width :].T,
         mixer_total,
         state_weight_total,
-        wide_one[:, c_step:c_gain],
+        late_total[:, c_gate : c_gate + state_heads],
         conv_inner_total,
         conv_state_total,
         bias_total,

time: 1070 us -> 616 us (0.58)
  waiting for transfers between devices: 348 us -> 161 us
  matrix products: 266 us -> 119 us
  local copies, waits for them, and re-layouts: 216 us -> 74.8 us
  other arithmetic: 192 us -> 91.4 us
  Pallas kernels: 0 us -> 66.5 us
  starting transfers between devices: 19.8 us -> 76.8 us
    reduce_scatter x1, waiting for transfers between devices: 173 us -> 0.01 us  [shards(): lax.psum_scatter(second_grads, WEIGHT_AXES, scatter_dimension=0, tiled=True)]
    dot_general x59 -> x0, matrix products: 150 us -> none  [the longest x12 60 us: block_step(): inside = jnp.einsum('gtsh,gshp->gthp', mixing, block_x, precision=HIGHEST)]
    all_gather x1 -> x0, waiting for transfers between devices: 73.5 us -> none  [shards(): first_all = lax.all_gather(first_pack, WEIGHT_AXES, axis=0, tiled=True)]
    reduce_scatter x1 -> x0, waiting for transfers between devices: 70.6 us -> none  [shards(): lax.psum_scatter(t_dot(normed_one, first_grads).astype(jnp.bfloat16), WEI...]
    pallas_call x0 -> x4, Pallas kernels: none -> 66.5 us  [the longest x1 31 us: backward(): tall(functools.partial(backward_kernel, self.pairs, last), self.grid, [*s...]
    ppermute x0 -> x42, waiting for transfers between devices: none -> 63.3 us  [the longest x36 60.6 us: across(): return lax.ppermute(value, WEIGHT_AXES, torus_route(step))]
    ppermute x0 -> x42, starting transfers between devices: none -> 61.6 us  [the longest x36 54.5 us: across(): return lax.ppermute(value, WEIGHT_AXES, torus_route(step))]
    ppermute x4, waiting for transfers between devices: 13.7 us -> 53.1 us  [shift_along(): return lax.ppermute(block, axis, route)]
  transfers between devices with their start and end apart: 22 -> 62, of which waited for: 11 -> 28; matrix products, arithmetic and copies ran while one was open for 35% -> 34% of each run, Pallas kernels for 0% -> 11%
where the time goes in v2:
time: 616 us; the launch traced here: 606 us
  waiting for transfers between devices  161 us (26%)
  matrix products  119 us (19%)
  other arithmetic  91.4 us (15%)
  starting transfers between devices  76.8 us (12%)
  local copies, waits for them, and re-layouts  74.8 us (12%)
  Pallas kernels  66.5 us (11%)
  between operations  16.2 us (3%)
    ppermute x36, waiting for transfers between devices, across(): return lax.ppermute(value, WEIGHT_AXES, torus_route(step))  60.6 us
    ppermute x36, starting transfers between devices, across(): return lax.ppermute(value, WEIGHT_AXES, torus_route(step))  54.5 us
    ppermute x4, waiting for transfers between devices, shift_along(): return lax.ppermute(block, axis, route)  53.1 us
    dot_general x12, matrix products, dot_t(): lax.dot_general(a, b, (((1,), (1,)), ((), ())), preferred_element_type=jn...  45.9 us
    dot_general x9, matrix products, t_dot(): lax.dot_general(a, b, (((0,), (0,)), ((), ())), preferred_element_type=jn...  38.3 us
    dot_general x12, matrix products, dot(): return jnp.dot(a, b, preferred_element_type=jnp.float32)  35.2 us
    all_gather x1, waiting for transfers between devices, shards(): second_all = lax.all_gather(second_pack, WEIGHT_AXES, axis=0, tiled=True)  33.3 us
    pallas_call x1, Pallas kernels, backward(): tall(functools.partial(backward_kernel, self.pairs, last), self.grid, [*s...  31 us
  transfers between devices with their start and end apart: 62, of which 28 were waited for; matrix products, arithmetic and copies ran while one was open for 34% of the time, Pallas kernels for 11%

profile of v2, /device:TPU:0, one launch (start us, length us, event | category | flops | bytes accessed | tf_op | source)
XLA Modules:
  0.0 606.5 jit_solution(1025178272738628879)
XLA Ops:
  39.0 10.5 %collective-permute-start.2 = (bf16[2,2,64,512]{3,2,1,0:T(8,128)(2,1)S(1)}, bf16[2,2,64,512]{3,2,1,0:T(8,128)(2,1)S(1)}, u32[]{:S(2)}, u32[]{:S(2)}) collective-permute-start(bf16[2,2,64,512]{3,2,1,0:T(8,128)(2,1)S(1)} %pad_maximum_fusion.15), channel_id=1, source_target_pairs={{0,8},{2,10},{4,12},{6,14},{8,16},{10,18},{12,20},{14,22},{16,24},... | collective-permute-start | bytes 786440 | tf_op jit(solution)/shard_map/ppermute | solution.py:107
  69.6 5.9 collective-permute-done.9
  99.5 7.7 %shard_map.313 = (bf16[2,128,768]{2,1,0:T(8,128)(2,1)S(1)}, f32[2,1,128]{2,1,0:T(1,128)}) custom-call(bf16[2,16,1024]{2,1,0:T(8,128)(2,1)S(1)} %collective-permute-done.15.edge_ref, bf16[1024,1024]{1,0:T(8,128)(2,1)S(1)} %convolution_convert_fusion.5.before_ref.block_ref, bf16[1024,1024]{1,0:T(8,128)(2,1)S(1)} %convolution_convert_fusion.5.before_ref.block_ref, ...), custom_call_target="tpu_custom_call" | custom-call | flops 201326592 | bytes 2359296 | tf_op jit(solution)/shard_map/pallas_call | solution.py:605
  112.8 9.5 %collective-permute-done.16.incoming_ref = bf16[2,128,768]{2,1,0:T(8,128)(2,1)S(1)} collective-permute-done((bf16[2,128,768]{2,1,0:T(8,128)(2,1)S(1)}, bf16[2,128,768]{2,1,0:T(8,128)(2,1)S(1)}, u32[]{:S(2)}, u32[]{:S(2)}) %collective-permute-start.16) | collective-permute-done | bytes 393248 | tf_op jit(solution)/shard_map/ppermute | solution.py:29
  122.3 17.2 %shard_map.314 = (f32[1024,768]{1,0:T(8,128)}, f32[1024,768]{1,0:T(8,128)}, f32[1024,1]{1,0:T(8,128)S(1)}, bf16[2,4,128,768]{3,2,1,0:T(8,128)(2,1)S(1)}, bf16[2,4,128,768]{3,2,1,0:T(8,128)(2,1)S(1)}) custom-call(bf16[2,16,1024]{2,1,0:T(8,128)(2,1)S(1)} %collective-permute-done.15.edge_ref, bf16[1024,1024]{1,0:T(8,128)(2,1)} %copy-done, ...), custom_call_target="tpu_custom_call" | custom-call | flops 805306368 | bytes 14155776 | tf_op jit(solution)/shard_map/pallas_call | solution.py:622
  141.9 14.3 %while.28 = (s32[]{:T(128)}, bf16[2,2048,64]{1,2,0:T(8,128)(2,1)S(1)}, f32[2,2048]{1,0:T(2,128)S(1)}, bf16[2,2048,64]{2,1,0:T(8,128)(2,1)S(1)}, bf16[2,1024,128]{2,1,0:T(8,128)(2,1)}, /*index=5*/s32[2048]{0:T(1024)S(1)}) while((s32[]{:T(128)}, bf16[2,2048,64]{1,2,0:T(8,128)(2,1)S(1)}, f32[2,2048]{1,0:T(2,128)S(1)}, ...), condition=%wide.region_4.5_spmd.clone.clone, body=%wide.region_1.4_spmd.clone.sunk.clone | while | flops 566228992 | bytes 27361372 | solution.py:832
  162.8 33.3 %all-gather.2.cloned.1.call-done = bf16[1024,4096]{1,0:T(8,128)(2,1)} async-done(((bf16[64,4096]{1,0:T(8,128)(2,1)}), bf16[1024,4096]{1,0:T(8,128)(2,1)}) %all-gather.2.cloned.1.call-update) | async-done | bytes 8388624 | tf_op jit(solution)/shard_map/all_gather | solution.py:764
  220.8 8.5 %fusion.37 = f32[1024,1024]{1,0:T(8,128)} fusion(bf16[1024,4096]{1,0:T(8,128)(2,1)S(1)} %copy-done.75, bf16[1024,1024]{0,1:T(8,128)(2,1)} %get-tuple-element.367, bf16[1024,1024]{0,1:T(8,128)(2,1)S(1)} %get-tuple-element.366), kind=kOutput, calls=%fused_computation.51 | convolution fusion | flops 4303355904 | bytes 12582912 | tf_op jit(solution)/shard_map/dot_general | solution.py:240
  240.7 7.7 %convolution_convert_fusion.2 = bf16[1024,2048]{1,0:T(8,128)(2,1)} fusion(bf16[1024,1024]{1,0:T(8,128)(2,1)S(1)} %copy-done.40, bf16[1024,1024]{0,1:T(8,128)(2,1)S(1)} %copy-done.81, bf16[1024,1024]{0,1:T(8,128)(2,1)S(1)} %copy-done.80), kind=kOutput, calls=%fused_computation.86 | convolution fusion | flops 4305453056 | bytes 10485760 | tf_op jit(solution)/shard_map/dot_general | solution.py:244
  251.5 6.0 multiply_reduce_fusion.1
  257.6 8.0 %fusion.126 = (bf16[1024,1024]{1,0:T(8,128)(2,1)S(1)}, f32[1024,1024]{1,0:T(8,128)}) fusion(f32[1024]{0:T(1024)S(1)} %broadcast_multiply_fusion.2, f32[1024,1024]{1,0:T(8,128)} %get-tuple-element.359, f32[1024]{0:T(1024)S(1)} %get-tuple-element.423, f32[1024]{0:T(1024)S(1)} %get-tuple-element.326, f32[1024,1024]{1,0:T(8,128)} %fusion.37, ...), kind=kLoop, calls=%fused_computation.307 | loop fusion | flops 9437184 | bytes 20987904 | tf_op jit(solution)/shard_map/convert_element_type | solution.py:882
  281.9 57.7 %while.29 = (s32[]{:T(128)}, f32[2,2048,64]{1,2,0:T(8,128)}, bf16[2,1024,128]{1,2,0:T(8,128)(2,1)}, bf16[2,2048,64]{2,1,0:T(8,128)(2,1)S(1)}, bf16[2,1024,128]{2...) while((s32[]{:T(128)}, f32[2,2048,64]{1,2,0:T(8,128)}, ...), condition=%wide.region_10.11_spmd.clone.clone, body=%wide.region_8.10_spmd.clone.sunk.clone | while | flops 1363933184 | bytes 113819904 | solution.py:924
  293.4 8.1 %multiply_convert_fusion.6 = bf16[2048,1024]{0,1:T(8,128)(2,1)S(1)} fusion(f32[2048,1024]{0,1:T(8,128)} %get-tuple-element.556, f32[2048,1024]{0,1:T(8,128)} %copy-done.19, f32[2048]{0:T(1024)S(1)} %get-tuple-element.557), kind=kLoop, calls=%fused_computation.21.clone.1.clone | loop fusion | flops 6291456 | bytes 20979712 | tf_op jit(solution)/shard_map/while/body/eval_jaxpr/convert_element_type | solution.py:909
  322.2 8.1 %multiply_convert_fusion.6 = bf16[2048,1024]{0,1:T(8,128)(2,1)S(1)} fusion(f32[2048,1024]{0,1:T(8,128)} %get-tuple-element.556, f32[2048,1024]{0,1:T(8,128)} %copy-done.19, f32[2048]{0:T(1024)S(1)} %get-tuple-element.557), kind=kLoop, calls=%fused_computation.21.clone.1.clone | loop fusion | flops 6291456 | bytes 20979712 | tf_op jit(solution)/shard_map/while/body/eval_jaxpr/convert_element_type | solution.py:909
  339.7 6.5 %multiply_reduce_fusion.4 = (f32[1024]{0:T(1024)S(1)}, f32[1024,768]{1,0:T(8,128)}) fusion(f32[1024,768]{1,0:T(8,128)} %get-tuple-element.129, f32[768]{0:T(1024)S(1)} %copy-done.64, bf16[1024,1024]{1,0:T(8,128)(2,1)} %copy-done.35, bf16[1024,4096]{1,0:T(8,128)(2,1)} %all-gather.2.cloned.1.call-done), kind=kOutput, calls=%fused_computation.87 | convolution fusion | flops 1612971008 | bytes 9968640 | tf_op jit(solution)/shard_map/dot_general | solution.py:236
  354.6 10.6 %shard_map.315 = (bf16[1024,768]{1,0:T(8,128)(2,1)S(1)}, bf16[1024,768]{1,0:T(8,128)(2,1)S(1)}, f32[8,768]{1,0:T(8,128)S(1)}, bf16[2,128,768]{2,1,0:T(8,128)(2,1)}) custom-call(bf16[2,16,1024]{2,1,0:T(8,128)(2,1)S(1)} %collective-permute-done.15.edge_ref, bf16[1024,1024]{1,0:T(8,128)(2,1)} %copy-done, bf16[1024,1024]{1,0:T(8,128)(2,1)} %copy-done, ...), custom_call_target="tpu_custom_call" | custom-call | flops 201326592 | bytes 15728640 | tf_op jit(solution)/shard_map/pallas_call | solution.py:641
  376.1 6.7 %convolution_convert_fusion.1 = bf16[1024,1152]{1,0:T(8,128)(2,1)} fusion(bf16[1024,1024]{1,0:T(8,128)(2,1)} %copy-done.37, bf16[1024,1152]{1,0:T(8,128)(2,1)} %concatenate.85), kind=kOutput, calls=%fused_computation.85 | convolution fusion | flops 2417098752 | bytes 6815744 | tf_op jit(solution)/shard_map/dot_general | solution.py:244
  390.3 7.1 %collective-permute-done.25.later_ref = bf16[2,128,768]{2,1,0:T(8,128)(2,1)} collective-permute-done((bf16[2,128,768]{2,1,0:T(8,128)(2,1)}, bf16[2,128,768]{2,1,0:T(8,128)(2,1)}, u32[]{:S(2)}, u32[]{:S(2)}) %collective-permute-start.25) | collective-permute-done | bytes 393248 | tf_op jit(solution)/shard_map/ppermute | solution.py:29
  397.4 31.0 %shard_map.316 = (bf16[1024,1024]{1,0:T(8,128)(2,1)}, bf16[1024,128]{1,0:T(8,128)(2,1)S(1)}, bf16[2,16,1024]{2,1,0:T(8,128)(2,1)S(1)}, f32[8,1024]{1,0:T(8,128)}...) custom-call(bf16[2,16,1024]{2,1,0:T(8,128)(2,1)S(1)} %copy-done.10, bf16[1024,1024]{1,0:T(8,128)(2,1)} %copy-done, ...), custom_call_target="tpu_custom_call" | custom-call | flops 1811939328 | bytes 12582912 | tf_op jit(solution)/shard_map/pallas_call | solution.py:664
  439.3 36.4 %collective-permute-done.26 = bf16[2,8,1024]{2,1,0:T(8,128)(2,1)S(1)} collective-permute-done((bf16[2,8,1024]{2,1,0:T(8,128)(2,1)S(1)}, bf16[2,8,1024]{2,1,0:T(8,128)(2,1)S(1)}, u32[]{:S(2)}, u32[]{:S(2)}) %collective-permute-start.26) | collective-permute-done | bytes 32800 | tf_op jit(solution)/shard_map/ppermute | solution.py:29
  494.9 7.5 %collective-permute-done.27 = bf16[4,2,64,512]{3,2,1,0:T(8,128)(2,1)S(1)} collective-permute-done((bf16[4,2,64,512]{3,2,1,0:T(8,128)(2,1)S(1)}, bf16[4,2,64,512]{3,2,1,0:T(8,128)(2,1)S(1)}, u32[]{:S(2)}, u32[]{:S(2)}) %collective-permute-start.27) | collective-permute-done | bytes 524320 | tf_op jit(solution)/shard_map/ppermute | solution.py:107
  525.9 7.8 %collective-permute-done.49 = bf16[4,2,64,640]{3,2,1,0:T(8,128)(2,1)S(1)} collective-permute-done((bf16[4,2,64,640]{3,2,1,0:T(8,128)(2,1)}, bf16[4,2,64,640]{3,2,1,0:T(8,128)(2,1)S(1)}, u32[]{:S(2)}, u32[]{:S(2)}) %collective-permute-start.49) | collective-permute-done | bytes 655392 | tf_op jit(solution)/shard_map/ppermute | solution.py:107
  537.0 7.7 %collective-permute-done.43 = bf16[64,1152]{1,0:T(8,128)(2,1)S(1)} collective-permute-done((bf16[64,1152]{1,0:T(8,128)(2,1)S(1)}, bf16[64,1152]{1,0:T(8,128)(2,1)S(1)}, u32[]{:S(2)}, u32[]{:S(2)}) %collective-permute-start.43) | collective-permute-done | bytes 147488 | tf_op jit(solution)/shard_map/ppermute | solution.py:107
  586.5 6.9 %fusion.48 = f32[1024,1024]{1,0:T(8,128)} fusion(f32[1024,1024]{1,0:T(8,128)} %get-tuple-element.357, bf16[2,512,1024]{2,1,0:T(8,128)(2,1)S(1)} %copy-done.22, f32[1024]{0:T(1024)S(1)} %broadcast_multiply_fusion.1, f32[1024]{0:T(1024)S(1)} %copy-done.68, f32[1024]{0:T(1024)S(1)} %copy-done.61, f32[1024]{0:T(1024)S(1)} %bitcast.479, ...), kind=kLoop, calls=%fused_computation.71 | loop fusion | flops 8388608 | bytes 18890752 | tf_op jit(solution)/shard_map/add | solution.py:985
  (531 shorter events, 331.0 us)
Async XLA Ops:
  7.2 188.9 %all-gather.2.cloned.1.call-start = ((), (), s32[]{:S(2)}) async-start(), calls=%async_computation.1 | async-start | bytes 8912896 | tf_op jit(solution)/shard_map/all_gather | solution.py:764
  9.7 17.8 %collective-permute-start.6 = (bf16[64,1024]{1,0:T(8,128)(2,1)S(1)}, bf16[64,1024]{1,0:T(8,128)(2,1)S(1)}, u32[]{:S(2)}, u32[]{:S(2)}) collective-permute-start(bf16[64,1024]{1,0:T(8,128)(2,1)S(1)} %pad_maximum_fusion.20), channel_id=1, source_target_pairs={{0,16},{2,18},{4,20},{6,22},{8,24},{10,26},{12,28},{14,30},{16,0},... | collective-permute-start | bytes 393224 | tf_op jit(solution)/shard_map/ppermute | solution.py:107
  26.8 24.9 %collective-permute-start.12 = (bf16[2,64,768]{2,1,0:T(8,128)(2,1)S(1)}, bf16[2,64,768]{2,1,0:T(8,128)(2,1)S(1)}, u32[]{:S(2)}, u32[]{:S(2)}) collective-permute-start(bf16[2,64,768]{2,1,0:T(8,128)(2,1)S(1)} %pad_maximum_fusion.18), channel_id=1, source_target_pairs={{0,16},{2,18},{4,20},{6,22},{8,24},{10,26},{12,28},{14,30},{16,0},... | collective-permute-start | bytes 589832 | tf_op jit(solution)/shard_map/ppermute | solution.py:107
  27.6 24.1 %collective-permute-start.13 = (bf16[2,64,768]{2,1,0:T(8,128)(2,1)S(1)}, bf16[2,64,768]{2,1,0:T(8,128)(2,1)S(1)}, u32[]{:S(2)}, u32[]{:S(2)}) collective-permute-start(bf16[2,64,768]{2,1,0:T(8,128)(2,1)S(1)} %pad_maximum_fusion.18), channel_id=1, source_target_pairs={{0,24},{2,26},{4,28},{6,30},{8,0},{10,2},{12,4},{14,6},{16,8},{18,... | collective-permute-start | bytes 589832 | tf_op jit(solution)/shard_map/ppermute | solution.py:107
  30.9 20.9 %collective-permute-start.8 = (bf16[4,64,1024]{2,1,0:T(8,128)(2,1)S(1)}, bf16[4,64,1024]{2,1,0:T(8,128)(2,1)S(1)}, u32[]{:S(2)}, u32[]{:S(2)}) collective-permute-start(bf16[4,64,1024]{2,1,0:T(8,128)(2,1)S(1)} %bitcast_dynamic-update-slice_fusion.8), channel_id=1, source_target_pairs={{0,4},{2,6},{4,0},{6,2},{8,12},{10,14},{12,8},{14,10},{16,20},{18,... | collective-permute-start | bytes 1572872 | tf_op jit(solution)/shard_map/ppermute | solution.py:107
  31.9 29.6 %collective-permute-start.3 = (bf16[2,2,64,512]{3,2,1,0:T(8,128)(2,1)S(1)}, bf16[2,2,64,512]{3,2,1,0:T(8,128)(2,1)S(1)}, u32[]{:S(2)}, u32[]{:S(2)}) collective-permute-start(bf16[2,2,64,512]{3,2,1,0:T(8,128)(2,1)S(1)} %pad_maximum_fusion.15), channel_id=1, source_target_pairs={{0,16},{2,18},{4,20},{6,22},{8,24},{10,26},{12,28},{14,30},{16,0},... | collective-permute-start | bytes 786440 | tf_op jit(solution)/shard_map/ppermute | solution.py:107
  39.0 17.2 %collective-permute-start.2 = (bf16[2,2,64,512]{3,2,1,0:T(8,128)(2,1)S(1)}, bf16[2,2,64,512]{3,2,1,0:T(8,128)(2,1)S(1)}, u32[]{:S(2)}, u32[]{:S(2)}) collective-permute-start(bf16[2,2,64,512]{3,2,1,0:T(8,128)(2,1)S(1)} %pad_maximum_fusion.15), channel_id=1, source_target_pairs={{0,8},{2,10},{4,12},{6,14},{8,16},{10,18},{12,20},{14,22},{16,24},... | collective-permute-start | bytes 786440 | tf_op jit(solution)/shard_map/ppermute | solution.py:107
  51.7 16.4 %collective-permute-start.14 = (bf16[4,2,64,768]{3,2,1,0:T(8,128)(2,1)S(1)}, bf16[4,2,64,768]{3,2,1,0:T(8,128)(2,1)S(1)}, u32[]{:S(2)}, u32[]{:S(2)}) collective-permute-start(bf16[4,2,64,768]{3,2,1,0:T(8,128)(2,1)S(1)} %bitcast_dynamic-update-slice_fusion.4), channel_id=1, source_target_pairs={{0,4},{2,6},{4,0},{6,2},{8,12},{10,14},{12,8},{14,10},{16,20},{18,... | collective-permute-start | bytes 2359304 | tf_op jit(solution)/shard_map/ppermute | solution.py:107
  52.0 23.5 %collective-permute-start.9 = (bf16[4,2,64,1024]{3,2,1,0:T(8,128)(2,1)S(1)}, bf16[4,2,64,1024]{3,2,1,0:T(8,128)(2,1)S(1)}, u32[]{:S(2)}, u32[]{:S(2)}) collective-permute-start(bf16[4,2,64,1024]{3,2,1,0:T(8,128)(2,1)S(1)} %pad_maximum_fusion.10), channel_id=1, source_target_pairs={{0,2},{2,0},{4,6},{6,4},{8,10},{10,8},{12,14},{14,12},{16,18},{18,... | collective-permute-start | bytes 3145736 | tf_op jit(solution)/shard_map/ppermute | solution.py:107
  77.3 516.7 %reduce-scatter.2.cloned.1.call-start = ((), (), s32[]{:S(2)}) async-start(), calls=%async_computation.2 | async-start | bytes 8912896 | tf_op jit(solution)/shard_map/reduce_scatter | solution.py:892
  85.1 25.5 %collective-permute-start.18 = (bf16[2,512,128]{1,2,0:T(8,128)(2,1)}, bf16[2,512,128]{1,2,0:T(8,128)(2,1)}, u32[]{:S(2)}, u32[]{:S(2)}) collective-permute-start(bf16[2,512,128]{1,2,0:T(8,128)(2,1)} %pad_maximum_fusion.16), channel_id=1, source_target_pairs={{0,2},{2,0},{1,3},{3,1},{4,6},{6,4},{5,7},{7,5},{8,10},{10,8},{9,1... | collective-permute-start | bytes 786440 | tf_op jit(solution)/shard_map/ppermute | solution.py:50
  141.9 17.4 %collective-permute-start.17 = (f32[1024,1]{1,0:T(8,128)S(1)}, f32[1024,1]{1,0:T(8,128)}, u32[]{:S(2)}, u32[]{:S(2)}) collective-permute-start(f32[1024,1]{1,0:T(8,128)S(1)} %get-tuple-element.130), channel_id=1, source_target_pairs={{0,1},{1,0},{2,3},{3,2},{4,5},{5,4},{6,7},{7,6},{8,9},{9,8},{10,11... | collective-permute-start | bytes 12296 | tf_op jit(solution)/shard_map/ppermute | solution.py:38
  229.3 22.2 %collective-permute-start.21 = (f32[1024,1024]{1,0:T(8,128)}, f32[1024,1024]{1,0:T(8,128)}, u32[]{:S(2)}, u32[]{:S(2)}) collective-permute-start(f32[1024,1024]{1,0:T(8,128)} %fusion.37), channel_id=1, source_target_pairs={{0,1},{1,0},{2,3},{3,2},{4,5},{5,4},{6,7},{7,6},{8,9},{9,8},{10,11... | collective-permute-start | bytes 12582920 | tf_op jit(solution)/shard_map/ppermute | solution.py:38
  276.6 227.4 %collective-permute-start.36 = (f32[4,64]{1,0:T(4,128)}, f32[4,64]{1,0:T(4,128)}, u32[]{:S(2)}, u32[]{:S(2)}) collective-permute-start(f32[4,64]{1,0:T(4,128)} %get-tuple-element.418), channel_id=1, source_target_pairs={{0,8},{2,10},{4,12},{6,14},{8,16},{10,18},{12,20},{14,22},{16,24},... | collective-permute-start | bytes 3080 | tf_op jit(solution)/shard_map/ppermute | solution.py:107
  276.9 227.1 %collective-permute-start.38 = (f32[4,64]{1,0:T(4,128)}, f32[4,64]{1,0:T(4,128)}, u32[]{:S(2)}, u32[]{:S(2)}) collective-permute-start(f32[4,64]{1,0:T(4,128)} %get-tuple-element.419), channel_id=1, source_target_pairs={{0,24},{2,26},{4,28},{6,30},{8,0},{10,2},{12,4},{14,6},{16,8},{18,... | collective-permute-start | bytes 3080 | tf_op jit(solution)/shard_map/ppermute | solution.py:107
  280.4 223.6 %collective-permute-start.37 = (f32[4,64]{1,0:T(4,128)}, f32[4,64]{1,0:T(4,128)}, u32[]{:S(2)}, u32[]{:S(2)}) collective-permute-start(f32[4,64]{1,0:T(4,128)} %get-tuple-element.420), channel_id=1, source_target_pairs={{0,16},{2,18},{4,20},{6,22},{8,24},{10,26},{12,28},{14,30},{16,0},... | collective-permute-start | bytes 3080 | tf_op jit(solution)/shard_map/ppermute | solution.py:107
  349.9 21.1 %collective-permute-start.23 = (bf16[2,512,128]{1,2,0:T(8,128)(2,1)}, bf16[2,512,128]{1,2,0:T(8,128)(2,1)}, u32[]{:S(2)}, u32[]{:S(2)}) collective-permute-start(bf16[2,512,128]{1,2,0:T(8,128)(2,1)} %broadcast_select_fusion), channel_id=1, source_target_pairs={{0,2},{2,0},{1,3},{3,1},{4,6},{6,4},{5,7},{7,5},{8,10},{10,8},{9,1... | collective-permute-start | bytes 786440 | tf_op jit(solution)/shard_map/ppermute | solution.py:69
  366.3 31.0 %collective-permute-start.25 = (bf16[2,128,768]{2,1,0:T(8,128)(2,1)}, bf16[2,128,768]{2,1,0:T(8,128)(2,1)}, u32[]{:S(2)}, u32[]{:S(2)}) collective-permute-start(bf16[2,128,768]{2,1,0:T(8,128)(2,1)} %get-tuple-element.141), channel_id=1, source_target_pairs={{2,0},{3,1},{6,4},{7,5},{10,8},{11,9},{14,12},{15,13},{18,16},{19,... | collective-permute-start | bytes 1179656 | tf_op jit(solution)/shard_map/ppermute | solution.py:29
  389.5 86.3 %collective-permute-start.24 = (bf16[4,2,64,1152]{3,2,0,1:T(8,128)(2,1)}, bf16[4,2,64,1152]{3,2,0,1:T(8,128)(2,1)}, u32[]{:S(2)}, u32[]{:S(2)}) collective-permute-start(bf16[4,2,64,1152]{3,2,0,1:T(8,128)(2,1)} %bitcast.389), channel_id=1, source_target_pairs={{0,2},{2,0},{4,6},{6,4},{8,10},{10,8},{12,14},{14,12},{16,18},{18,... | collective-permute-start | bytes 3538952 | tf_op jit(solution)/shard_map/ppermute | solution.py:107
  437.3 38.3 %collective-permute-start.26 = (bf16[2,8,1024]{2,1,0:T(8,128)(2,1)S(1)}, bf16[2,8,1024]{2,1,0:T(8,128)(2,1)S(1)}, u32[]{:S(2)}, u32[]{:S(2)}) collective-permute-start(bf16[2,8,1024]{2,1,0:T(8,128)(2,1)S(1)} %slice.253), channel_id=1, source_target_pairs={{2,0},{3,1},{6,4},{7,5},{10,8},{11,9},{14,12},{15,13},{18,16},{19,... | collective-permute-start | bytes 98312 | tf_op jit(solution)/shard_map/ppermute | solution.py:29
  487.3 16.4 %collective-permute-start.28 = (bf16[4,64,1152]{2,1,0:T(8,128)(2,1)S(1)}, bf16[4,64,1152]{2,1,0:T(8,128)(2,1)S(1)}, u32[]{:S(2)}, u32[]{:S(2)}) collective-permute-start(bf16[4,64,1152]{2,1,0:T(8,128)(2,1)S(1)} %dynamic-slice_bitcast_fusion.3), channel_id=1, source_target_pairs={{0,4},{2,6},{4,0},{6,2},{8,12},{10,14},{12,8},{14,10},{16,20},{18,... | collective-permute-start | bytes 1769480 | tf_op jit(solution)/shard_map/ppermute | solution.py:107
  503.9 65.7 %collective-permute-start.29 = (f32[1024,1024]{1,0:T(8,128)}, f32[1024,1024]{1,0:T(8,128)}, u32[]{:S(2)}, u32[]{:S(2)}) collective-permute-start(f32[1024,1024]{1,0:T(8,128)} %add_add_fusion), channel_id=1, source_target_pairs={{0,1},{1,0},{2,3},{3,2},{4,5},{5,4},{6,7},{7,6},{8,9},{9,8},{10,11... | collective-permute-start | bytes 12582920 | tf_op jit(solution)/shard_map/ppermute | solution.py:38
  516.9 16.8 %collective-permute-start.49 = (bf16[4,2,64,640]{3,2,1,0:T(8,128)(2,1)}, bf16[4,2,64,640]{3,2,1,0:T(8,128)(2,1)S(1)}, u32[]{:S(2)}, u32[]{:S(2)}) collective-permute-start(bf16[4,2,64,640]{3,2,1,0:T(8,128)(2,1)} %dynamic-slice_bitcast_fusion.2), channel_id=1, source_target_pairs={{0,4},{2,6},{4,0},{6,2},{8,12},{10,14},{12,8},{14,10},{16,20},{18,... | collective-permute-start | bytes 1966088 | tf_op jit(solution)/shard_map/ppermute | solution.py:107
  521.5 25.5 %collective-permute-start.45 = (bf16[4,64,512]{2,1,0:T(8,128)(2,1)}, bf16[4,64,512]{2,1,0:T(8,128)(2,1)}, u32[]{:S(2)}, u32[]{:S(2)}) collective-permute-start(bf16[4,64,512]{2,1,0:T(8,128)(2,1)} %dynamic-slice_bitcast_fusion.6), channel_id=1, source_target_pairs={{0,4},{2,6},{4,0},{6,2},{8,12},{10,14},{12,8},{14,10},{16,20},{18,... | collective-permute-start | bytes 786440 | tf_op jit(solution)/shard_map/ppermute | solution.py:107
  (125 other events, 2131.4 us)
Sparse Core Ops, SparseCore 0:
  77.4 118.6 all-gather.1
  276.1 216.2 reduce-scatter.1

commit v3 on v2

--- a/solution.py
+++ b/solution.py
@@ -118,10 +118,11 @@
 
 def gather_weights(shard, order):
     if not is_torus():
-        return lax.all_gather(shard, WEIGHT_AXES, axis=0, tiled=True)
+        return lax.all_gather(shard, WEIGHT_AXES, axis=0, tiled=True), shard
     place = torus_place()
     done = ""
     value = shard
+    early = None
     for name in order:
         spot = sum(1 for other in "zxy" if other in done and "zxy".index(other) < "zxy".index(name))
         if name == "z":
@@ -139,7 +140,8 @@
                 [jnp.where(low, value, other), jnp.where(low, other, value)], axis=spot
             )
         done += name
-    return value.reshape(-1, shard.shape[1])
+        early = value if early is None else early
+    return value.reshape(-1, shard.shape[1]), early
 
 
 def scatter_begin(whole):
@@ -221,15 +223,6 @@
     frequency = ROPE_BASE ** (-(jnp.arange(head_width // 2).astype(jnp.float32) * 2.0 / head_width))
     angles = position[:, None] * frequency[None, :]
     return (jnp.cos(angles), jnp.sin(angles))
-
-
-def rotate(values, cosines, sines):
-    half_width = values.shape[-1] // 2
-    front = values[..., :half_width]
-    behind = values[..., half_width:]
-    return jnp.concatenate(
-        [front * cosines - behind * sines, behind * cosines + front * sines], axis=-1
-    )
 
 
 def dot(a, b):
@@ -257,6 +250,200 @@
         ),
         cost_estimate=pl.CostEstimate(flops=flops, bytes_accessed=moved, transcendentals=exps),
     )
+
+
+def turn(values, cosines, sines):
+    rows, width = values.shape
+    half = HEAD_DIMENSION // 2
+    lane = lax.broadcasted_iota(jnp.int32, (rows, width), 1)
+    swapped = jnp.where(
+        lane % HEAD_DIMENSION < half, pltpu.roll(values, width - half, 1), pltpu.roll(values, half, 1)
+    )
+    times = width // cosines.shape[1]
+    if times > 1:
+        cosines = jnp.concatenate([cosines] * times, axis=1)
+        sines = jnp.concatenate([sines] * times, axis=1)
+    return values * cosines + swapped * sines
+
+
+def turn_kernel(query_width, lin_ref, tables, query_out, pair_out):
+    lin = lin_ref[...]
+    query_out[...] = turn(lin[:, :query_width], tables[0], tables[1]).astype(jnp.bfloat16)
+    pair_out[...] = turn(lin[:, query_width:], tables[2], tables[3]).astype(jnp.bfloat16)
+
+
+def turn_back_kernel(grad_ref, tables, grad_out):
+    grad = grad_ref[...].astype(jnp.float32)
+    grad_out[...] = turn(grad, tables[2], -tables[3]).astype(jnp.bfloat16)
+
+
+def one_head(tile_ref, head, to_left):
+    start = head // 2 * 2 * HEAD_DIMENSION
+    tile = tile_ref[:, start : start + 2 * HEAD_DIMENSION]
+    is_left = head % 2 == 0
+    if is_left != to_left:
+        tile = pltpu.roll(tile.astype(jnp.float32), HEAD_DIMENSION, 1).astype(jnp.bfloat16)
+    lane = lax.broadcasted_iota(jnp.int32, tile.shape, 1)
+    kept = lane < HEAD_DIMENSION if to_left else lane >= HEAD_DIMENSION
+    return jnp.where(kept, tile, jnp.zeros_like(tile))
+
+
+def logits_t(pair, query, start, scale):
+    logits = dot_t(pair, query) * scale
+    key = lax.broadcasted_iota(jnp.int32, logits.shape, 0)
+    place = lax.broadcasted_iota(jnp.int32, logits.shape, 1) + start
+    return jnp.where(key <= place, logits, MASKED)
+
+
+def join_heads(parts_t, on_left):
+    tiles = []
+    for left, right in zip(parts_t[::2], parts_t[1::2]):
+        half = HEAD_DIMENSION
+        pick = (lambda v: v[:half]) if on_left else (lambda v: v[half:])
+        tiles.append(jnp.concatenate([pick(left), pick(right)], axis=0).T)
+    return jnp.concatenate(tiles, axis=1)
+
+
+def attend_kernel(heads, scale, start_ref, query_ref, pair_ref, out_ref, total_ref, pair_t):
+    @pl.when(pl.program_id(1) == 0)
+    def _():
+        pair_t[...] = pair_ref[0].astype(jnp.float32).T.astype(jnp.bfloat16)
+
+    pair = pair_ref[0]
+    rows = query_ref.shape[0]
+    start = start_ref[0] + pl.program_id(1) * rows
+    outs = []
+    for head in range(heads):
+        logits = logits_t(pair, one_head(query_ref, head, True), start, scale)
+        largest = jnp.max(logits, axis=0, keepdims=True)
+        weights = jnp.exp(logits - largest)
+        total = jnp.sum(weights, axis=0, keepdims=True)
+        total_ref[0, head : head + 1, :] = largest + jnp.log(total)
+        probs = (weights * (1.0 / total)).astype(jnp.bfloat16)
+        outs.append(dot(pair_t[...], probs))
+    out_ref[...] = join_heads(outs, False).astype(jnp.bfloat16)
+
+
+def attend_back_kernel(heads, scale, last, start_ref, query_ref, pair_ref, total_ref, grad_ref, tables, query_out, pair_out, pair_t, pair_sum):
+    @pl.when(pl.program_id(1) == 0)
+    def _():
+        pair_t[...] = pair_ref[0].astype(jnp.float32).T.astype(jnp.bfloat16)
+        pair_sum[...] = jnp.zeros_like(pair_sum)
+
+    pair = pair_ref[0]
+    rows = query_ref.shape[0]
+    start = start_ref[0] + pl.program_id(1) * rows
+    outs = []
+    for head in range(heads):
+        query = one_head(query_ref, head, True)
+        grad = one_head(grad_ref, head, False)
+        probs = jnp.exp(
+            logits_t(pair, query, start, scale) - total_ref[0, head : head + 1, :]
+        )
+        prob_grad = dot_t(pair, grad)
+        inner_sum = jnp.sum(probs * prob_grad, axis=0, keepdims=True)
+        logit_grad = (probs * (prob_grad - inner_sum)).astype(jnp.bfloat16)
+        outs.append(dot(pair_t[...], logit_grad))
+        pair_sum[...] += dot(logit_grad, query) * scale + dot(probs.astype(jnp.bfloat16), grad)
+    query_grad = join_heads(outs, True) * scale
+    query_out[...] = turn(query_grad, tables[0], -tables[1]).astype(jnp.bfloat16)
+
+    @pl.when(pl.program_id(1) == last)
+    def _():
+        pair_out[0] = pair_sum[...].astype(jnp.bfloat16)
+
+
+class Attention:
+    def __init__(self, tables, start, seq_count, rows, keys, heads):
+        self.tables, self.start = tables, start
+        self.seqs, self.rows, self.keys, self.heads = seq_count, rows, keys, heads
+        self.width = heads * HEAD_DIMENSION
+        self.tile = min(256, rows)
+        self.tiles = rows // self.tile
+        self.scale = HEAD_DIMENSION ** (-0.5)
+
+    def specs(self):
+        tile, tiles, pair_width = self.tile, self.tiles, 2 * HEAD_DIMENSION
+        return {
+            "start": pl.BlockSpec(memory_space=pltpu.SMEM),
+            "query": pl.BlockSpec((tile, self.width), lambda g, b: (g * tiles + b, 0)),
+            "local": pl.BlockSpec((tile, pair_width), lambda g, b: (g * tiles + b, 0)),
+            "lin": pl.BlockSpec((tile, self.width + pair_width), lambda g, b: (g * tiles + b, 0)),
+            "pair": pl.BlockSpec((1, self.keys, pair_width), lambda g, b: (g, 0, 0)),
+            "total": pl.BlockSpec((1, 8, tile), lambda g, b: (g, 0, b)),
+            "tables": pl.BlockSpec((4, tile, 2 * HEAD_DIMENSION), lambda g, b: (0, b, 0)),
+        }
+
+    def call(self, kernel, ins, outs, shapes, scratch, products, operands):
+        specs = self.specs()
+        size = self.seqs * self.rows * self.keys * self.heads
+        return tall(
+            kernel,
+            (self.seqs, self.tiles),
+            [specs[name] for name in ins],
+            [specs[name] for name in outs],
+            shapes,
+            scratch,
+            2 * products * size * 2 * HEAD_DIMENSION,
+            self.seqs * (self.rows + self.keys) * 1024,
+            size if products else 0,
+        )(*operands)
+
+    def pair_shape(self):
+        return jax.ShapeDtypeStruct((self.seqs * self.rows, 2 * HEAD_DIMENSION), jnp.bfloat16)
+
+    def query_shape(self):
+        return jax.ShapeDtypeStruct((self.seqs * self.rows, self.width), jnp.bfloat16)
+
+    def prepare(self, lin):
+        return self.call(
+            functools.partial(turn_kernel, self.width),
+            ("lin", "tables"),
+            ("query", "local"),
+            [self.query_shape(), self.pair_shape()],
+            [],
+            0,
+            (lin, self.tables),
+        )
+
+    def forward(self, query, pairs):
+        return self.call(
+            functools.partial(attend_kernel, self.heads, self.scale),
+            ("start", "query", "pair"),
+            ("query", "total"),
+            [self.query_shape(), jax.ShapeDtypeStruct((self.seqs, 8, self.rows), jnp.float32)],
+            [pltpu.VMEM((2 * HEAD_DIMENSION, self.keys), jnp.bfloat16)],
+            2,
+            (self.start, query, pairs),
+        )
+
+    def backward(self, query, pairs, totals, grad):
+        return self.call(
+            functools.partial(attend_back_kernel, self.heads, self.scale, self.tiles - 1),
+            ("start", "query", "pair", "total", "query", "tables"),
+            ("query", "pair"),
+            [
+                self.query_shape(),
+                jax.ShapeDtypeStruct((self.seqs, self.keys, 2 * HEAD_DIMENSION), jnp.bfloat16),
+            ],
+            [
+                pltpu.VMEM((2 * HEAD_DIMENSION, self.keys), jnp.bfloat16),
+                pltpu.VMEM((self.keys, 2 * HEAD_DIMENSION), jnp.float32),
+            ],
+            5,
+            (self.start, query, pairs, totals, grad, self.tables),
+        )
+
+    def pair_back(self, grad):
+        return self.call(
+            turn_back_kernel,
+            ("local", "tables"),
+            ("local",),
+            [self.pair_shape()],
+            [],
+            0,
+            (grad, self.tables),
+        )[0]
 
 
 def lower_ones(transposed=False):
@@ -730,7 +917,6 @@
     inner_width = state_heads * MP
     hidden = down_weight.shape[0]
     own_rows = query_weight.shape[0]
-    score_scale = HEAD_DIMENSION ** (-0.5)
 
     c_state = inner_width
     c_gate = c_state + 2 * NS
@@ -757,10 +943,10 @@
         [gateup_weight.reshape(own_rows, 2 * hidden), down_weight.T, mamba_weight.T, output_weight.T],
         axis=1,
     )
-    small_all = gather_weights(pack_small, "xyz")
-    conv_all = gather_weights(pack_conv, "zxy")
-    gate_all = gather_weights(mixer_parts[:, 0], "yzx")
-    second_pack, small_all, conv_all, gate_all = tie(second_pack, small_all, conv_all, gate_all)
+    small_all, _ = gather_weights(pack_small, "xyz")
+    conv_all, under_way = gather_weights(pack_conv, "zxy")
+    gate_all, _ = gather_weights(mixer_parts[:, 0], "yzx")
+    second_pack, _ = tie(second_pack, under_way)
     second_all = lax.all_gather(second_pack, WEIGHT_AXES, axis=0, tiled=True)
     gateup_all = second_all[:, : 2 * hidden]
     down_all = second_all[:, 2 * hidden : 3 * hidden]
@@ -772,25 +958,29 @@
     second_gain = small_all[:, c_gain + 1 - c_query].astype(jnp.float32)
     normed_one = (residual * first_inverse * first_gain).astype(jnp.bfloat16)
     cosines, sines = rope_tables(context_index * row_count, row_count, HEAD_DIMENSION)
-    cos_grid = cosines[None, :, None, :]
-    sin_grid = sines[None, :, None, :]
+    whole_cos = jnp.concatenate([cosines, cosines], axis=1)
+    whole_sin = jnp.concatenate([-sines, sines], axis=1)
+    tables = jnp.stack(
+        [
+            jnp.concatenate([whole_cos, whole_cos], axis=1),
+            jnp.concatenate([whole_sin, whole_sin], axis=1),
+            jnp.concatenate([whole_cos, jnp.ones_like(whole_cos)], axis=1),
+            jnp.concatenate([whole_sin, jnp.zeros_like(whole_sin)], axis=1),
+        ]
+    )
+    attention = Attention(
+        tables,
+        (context_index * row_count).astype(jnp.int32)[None],
+        seq_count,
+        row_count,
+        key_length,
+        query_heads,
+    )
     conv_in = dot(normed_one, conv_all).astype(jnp.bfloat16)
     gate_z = dot(normed_one, gate_all)
     small_lin = dot(normed_one, small_all)
-    query_lin = small_lin[:, :query_width].reshape(
-        seq_count, row_count, query_heads, HEAD_DIMENSION
-    )
-    rotated_query = rotate(query_lin, cos_grid, sin_grid).astype(jnp.bfloat16)
-    pair_lin = small_lin[:, query_width : query_width + 2 * HEAD_DIMENSION].reshape(
-        seq_count, row_count, 2 * HEAD_DIMENSION
-    )
-    key_rot = rotate(pair_lin[:, :, None, :HEAD_DIMENSION], cos_grid, sin_grid)[:, :, 0, :].astype(
-        jnp.bfloat16
-    )
-    local_pairs = jnp.concatenate(
-        [key_rot, pair_lin[..., HEAD_DIMENSION:].astype(jnp.bfloat16)], axis=-1
-    )
-    all_pairs = gather_ctx(local_pairs, 1)
+    rotated_query, local_pairs = attention.prepare(small_lin)
+    all_pairs = gather_ctx(local_pairs.reshape(seq_count, row_count, -1), 1)
     conv_rows = conv_in.reshape(seq_count, row_count, c_gate)
     edge = shift_along(conv_rows[:, row_count - EDGE :], "ctx", 1)
     taps = jnp.pad(
@@ -814,29 +1004,7 @@
     final_state, total_rate = mixer.states()
     incoming = carry_over(total_rate, final_state, True)
 
-    query_rows = jnp.transpose(rotated_query, (0, 2, 1, 3)).reshape(
-        seq_count, query_heads * row_count, HEAD_DIMENSION
-    )
-    query_place = context_index * row_count + jnp.tile(jnp.arange(row_count), query_heads)
-    visible = jnp.arange(key_length)[None, :] <= query_place[:, None]
-
-    def attend(pieces):
-        query_one, pair_one = pieces
-        logits = dot_t(query_one, pair_one[:, :HEAD_DIMENSION]) * score_scale
-        logits = jnp.where(visible, logits, MASKED)
-        largest = jnp.max(logits, axis=-1, keepdims=True)
-        log_total = largest + jnp.log(jnp.sum(jnp.exp(logits - largest), axis=-1, keepdims=True))
-        prob_low = jnp.exp(logits - log_total).astype(jnp.bfloat16)
-        return (dot(prob_low, pair_one[:, HEAD_DIMENSION:]), log_total[:, 0])
-
-    attended_rows, log_totals = lax.map(attend, (query_rows, all_pairs))
-    attended = (
-        jnp.transpose(
-            attended_rows.reshape(seq_count, query_heads, row_count, HEAD_DIMENSION), (0, 2, 1, 3)
-        )
-        .reshape(total_rows, query_width)
-        .astype(jnp.bfloat16)
-    )
+    attended, log_totals = attention.forward(rotated_query, all_pairs)
     y_scan, gated, squares, entering, leaving = mixer.forward(incoming)
     gate_gain = gated_gain.astype(jnp.float32)
     square_sum = sum_over(squares, "tp")
@@ -876,42 +1044,25 @@
     )
     up_grad = (act_grad * silu_gate).astype(jnp.bfloat16)
     both_grads = jnp.concatenate([gate_grad, up_grad], axis=1)
+    feed_grads = jnp.concatenate(
+        [
+            t_dot(normed_two, both_grads).astype(jnp.bfloat16),
+            t_dot(cotangent, act_low).astype(jnp.bfloat16),
+        ],
+        axis=1,
+    )
+    feed_grads, both_grads = tie(feed_grads, both_grads)
+    feed_total = lax.psum_scatter(feed_grads, WEIGHT_AXES, scatter_dimension=0, tiled=True)
     normed_two_grad = sum_over(dot_t(both_grads, gateup_all), "tp")
     second_back, second_gain_grad = norm_back(middle, second_inverse, second_gain, normed_two_grad)
     middle_grad = cotangent.astype(jnp.float32) + second_back
     branch_grad = middle_grad.astype(jnp.bfloat16)
-    second_grads = jnp.concatenate(
-        [
-            t_dot(normed_two, both_grads).astype(jnp.bfloat16),
-            t_dot(cotangent, act_low).astype(jnp.bfloat16),
-            t_dot(branch_grad, mixed).astype(jnp.bfloat16),
-        ],
-        axis=1,
-    )
-    branch_grad, second_grads = lax.optimization_barrier((branch_grad, second_grads))
-    second_total = lax.psum_scatter(second_grads, WEIGHT_AXES, scatter_dimension=0, tiled=True)
+    mixed_grads = t_dot(branch_grad, mixed).astype(jnp.bfloat16)
+    branch_grad, mixed_grads = tie(branch_grad, mixed_grads)
+    mix_sum = scatter_stage(scatter_begin(mixed_grads), "x")
 
     attended_grad = dot(branch_grad, mix_all[:, inner_width:]).astype(jnp.bfloat16)
     gated_low_grad = dot(branch_grad, mix_all[:, :inner_width])
-    attended_grad_rows = jnp.transpose(
-        attended_grad.reshape(seq_count, row_count, query_heads, HEAD_DIMENSION), (0, 2, 1, 3)
-    ).reshape(seq_count, query_heads * row_count, HEAD_DIMENSION)
-
-    def attend_back(pieces):
-        query_one, pair_one, total_one, grad_one = pieces
-        key_one = pair_one[:, :HEAD_DIMENSION]
-        value_one = pair_one[:, HEAD_DIMENSION:]
-        logits = dot_t(query_one, key_one) * score_scale
-        logits = jnp.where(visible, logits, MASKED)
-        prob_full = jnp.exp(logits - total_one[:, None])
-        prob_grad = dot_t(grad_one, value_one)
-        row_inner = jnp.sum(prob_full * prob_grad, axis=-1, keepdims=True)
-        logit_grad = (prob_full * (prob_grad - row_inner)).astype(jnp.bfloat16)
-        query_part = dot(logit_grad, key_one) * score_scale
-        key_part = t_dot(logit_grad, query_one) * score_scale
-        value_part = t_dot(prob_full.astype(jnp.bfloat16), grad_one)
-        return (query_part, jnp.concatenate([key_part, value_part], axis=-1))
-
     coupling = sum_over(
         jnp.sum(gated_low_grad * gate_gain * gated, axis=-1, keepdims=True), "tp"
     )
@@ -921,32 +1072,26 @@
     )
     gated_gain_grad = gain_sums[0]
     later_grad = carry_over(total_rate, incoming_grad, False)
-    query_grad_rows, pair_grad_all = lax.map(
-        attend_back, (query_rows, all_pairs, log_totals, attended_grad_rows)
-    )
-    pair_grad = scatter_sum_ctx(pair_grad_all.astype(jnp.bfloat16), 1).astype(jnp.float32)
-    query_grad = jnp.transpose(
-        query_grad_rows.reshape(seq_count, query_heads, row_count, HEAD_DIMENSION), (0, 2, 1, 3)
-    )
-    query_lin_grad = (
-        rotate(query_grad, cos_grid, -sin_grid)
-        .reshape(total_rows, query_width)
-        .astype(jnp.bfloat16)
-    )
-    key_lin_grad = rotate(pair_grad[:, :, None, :HEAD_DIMENSION], cos_grid, -sin_grid)[:, :, 0, :]
-    pair_lin_grad = (
-        jnp.concatenate([key_lin_grad, pair_grad[..., HEAD_DIMENSION:]], axis=-1)
-        .reshape(total_rows, 2 * HEAD_DIMENSION)
-        .astype(jnp.bfloat16)
-    )
+    query_lin_grad, pair_grad_all = attention.backward(
+        rotated_query, all_pairs, log_totals, attended_grad
+    )
+    mix_value, pair_grad_all = tie(mix_sum[0], pair_grad_all)
+    mix_sum = scatter_stage((mix_value, mix_sum[1]), "y")
+    pair_grad = scatter_sum_ctx(pair_grad_all, 1)
+    pair_lin_grad = attention.pair_back(pair_grad.reshape(total_rows, -1))
     early_grads = jnp.concatenate([gate_z_grad, query_lin_grad, pair_lin_grad], axis=1)
     early = t_dot(normed_one, early_grads).astype(jnp.bfloat16)
-    early, y_grad = tie(early, y_grad)
+    small_all_early = small_all[:, : c_step - c_query]
+    early_part = dot_t(gate_z_grad, gate_all) + dot_t(
+        jnp.concatenate([query_lin_grad, pair_lin_grad], axis=1), small_all_early
+    )
+    mix_value, early, early_part, y_grad = tie(mix_sum[0], early, early_part, y_grad)
+    mix_sum = scatter_stage((mix_value, mix_sum[1]), "z")
     early = scatter_stage(scatter_begin(early), "y")
     conv_grad, step_grad, front_slopes, tap_sums, head_sums, skip_sums = mixer.backward(
         later_grad, entering, leaving, y_scan, y_grad
     )
-    early_value, conv_grad = tie(early[0], conv_grad)
+    early_value, mix_total, conv_grad = tie(early[0], scatter_end(mix_sum), conv_grad)
     early = scatter_stage((early_value, early[1]), "x")
     table_grad = tap_sums[: conv_inner.shape[0]]
     bias_grad = head_sums[0, :state_heads]
@@ -968,9 +1113,8 @@
     late_one, late_two, late_grads = tie(late[:, :late_width], late[:, late_width:], late_grads)
     late_one = scatter_stage(scatter_begin(late_one), "y")
     late_two = scatter_stage(scatter_begin(late_two), "x")
-    small_grads = jnp.concatenate([query_lin_grad, pair_lin_grad, step_grad], axis=1)
     normed_one_part = (
-        dot_t(conv_grad, conv_all) + dot_t(gate_z_grad, gate_all) + dot_t(small_grads, small_all)
+        early_part + dot_t(conv_grad, conv_all) + dot_t(step_grad, small_all[:, c_step - c_query :])
     )
     late_value, early_value, normed_one_part = tie(late_one[0], early[0], normed_one_part)
     late_one = scatter_stage((late_value, late_one[1]), "x")
@@ -1018,7 +1162,7 @@
     gated_total, bias_total, decay_total, skip_total = pieces[2:6]
     gain_total = jnp.stack([scatter_gain(first_gain_grad), scatter_gain(second_gain_grad)])
 
-    wide_two = second_total.astype(jnp.float32)
+    wide_two = feed_total.astype(jnp.float32)
     mixer_total = jnp.stack(
         [
             early_total[:, :inner_width].reshape(own_rows, state_heads, MP),
@@ -1033,7 +1177,7 @@
         gain_total,
         early_total[:, inner_width : inner_width + query_width],
         early_total[:, inner_width + query_width :].reshape(own_rows, 1, 2 * HEAD_DIMENSION),
-        wide_two[:, 3 * hidden + inner_width :].T,
+        mix_total[:, inner_width:].T,
         mixer_total,
         state_weight_total,
         late_total[:, c_gate : c_gate + state_heads],
@@ -1043,7 +1187,7 @@
         decay_total,
         skip_total,
         gated_total,
-        wide_two[:, 3 * hidden : 3 * hidden + inner_width].T,
+        mix_total[:, :inner_width].T,
         wide_two[:, : 2 * hidden].reshape(own_rows, 2, hidden),
         wide_two[:, 2 * hidden : 3 * hidden].T,
     )

time: 616 us -> 563 us (0.914)
  local copies, waits for them, and re-layouts: 74.8 us -> 32 us
  starting transfers between devices: 76.8 us -> 118 us
  Pallas kernels: 66.5 us -> 100 us
  other arithmetic: 91.4 us -> 59.7 us
  matrix products: 119 us -> 90.7 us
  waiting for transfers between devices: 161 us -> 136 us
    pallas_call x0 -> x4, Pallas kernels: none -> 35 us  [call(): tall(kernel, (self.seqs, self.tiles), [specs[name] for name in ins], [spe...]
    ppermute x4, waiting for transfers between devices: 53.1 us -> 19.5 us  [shift_along(): return lax.ppermute(block, axis, route)]
    all_gather x1, waiting for transfers between devices: 33.3 us -> 0.01 us  [shards(): second_all = lax.all_gather(second_pack, WEIGHT_AXES, axis=0, tiled=True)]
    ppermute x36 -> x41, starting transfers between devices: 54.5 us -> 85.1 us  [across(): return lax.ppermute(value, WEIGHT_AXES, torus_route(step))]
    ppermute x1, waiting for transfers between devices: 0.01 us -> 25.9 us  [gather_ctx(): other = lax.ppermute(block, 'ctx', [(0, 1), (1, 0)])]
    ppermute x36 -> x41, waiting for transfers between devices: 60.6 us -> 80.9 us  [across(): return lax.ppermute(value, WEIGHT_AXES, torus_route(step))]
    dot_general x12 -> x7, matrix products: 45.9 us -> 29.4 us  [dot_t(): lax.dot_general(a, b, (((1,), (1,)), ((), ())), preferred_element_type=jn...]
    convert_element_type x4 -> x1, other arithmetic: 17.3 us -> 1.05 us  [shards(): wide_two = feed_total.astype(jnp.float32)]
  transfers between devices with their start and end apart: 62 -> 67, of which waited for: 28 -> 26; matrix products, arithmetic and copies ran while one was open for 34% -> 20% of each run, Pallas kernels for 11% -> 18%
where the time goes in v3:
time: 563 us; the launch traced here: 553 us
  waiting for transfers between devices  136 us (24%)
  starting transfers between devices  118 us (21%)
  Pallas kernels  100 us (18%)
  matrix products  90.7 us (16%)
  other arithmetic  59.7 us (11%)
  local copies, waits for them, and re-layouts  32 us (6%)
  between operations  15.8 us (3%)
    ppermute x41, starting transfers between devices, across(): return lax.ppermute(value, WEIGHT_AXES, torus_route(step))  85.1 us
    ppermute x41, waiting for transfers between devices, across(): return lax.ppermute(value, WEIGHT_AXES, torus_route(step))  80.9 us
    pallas_call x4, Pallas kernels, call(): tall(kernel, (self.seqs, self.tiles), [specs[name] for name in ins], [spe...  35 us
    dot_general x8, matrix products, dot(): return jnp.dot(a, b, preferred_element_type=jnp.float32)  31.9 us
    pallas_call x1, Pallas kernels, backward(): tall(functools.partial(backward_kernel, self.pairs, last), self.grid, [*s...  30.5 us
    dot_general x5, matrix products, t_dot(): lax.dot_general(a, b, (((0,), (0,)), ((), ())), preferred_element_type=jn...  29.4 us
    dot_general x7, matrix products, dot_t(): lax.dot_general(a, b, (((1,), (1,)), ((), ())), preferred_element_type=jn...  29.4 us
    ppermute x1, waiting for transfers between devices, gather_ctx(): other = lax.ppermute(block, 'ctx', [(0, 1), (1, 0)])  25.9 us
  transfers between devices with their start and end apart: 67, of which 26 were waited for; matrix products, arithmetic and copies ran while one was open for 20% of the time, Pallas kernels for 18%

profile of v3, /device:TPU:0, one launch (start us, length us, event | category | flops | bytes accessed | tf_op | source)
XLA Modules:
  0.0 552.7 jit_solution(8075931268714328702)
XLA Ops:
  47.8 12.5 %collective-permute-start.3 = (bf16[2,2,64,512]{3,2,1,0:T(8,128)(2,1)S(1)}, bf16[2,2,64,512]{3,2,1,0:T(8,128)(2,1)S(1)}, u32[]{:S(2)}, u32[]{:S(2)}) collective-permute-start(bf16[2,2,64,512]{3,2,1,0:T(8,128)(2,1)S(1)} %pad_maximum_fusion.13), channel_id=1, source_target_pairs={{0,16},{2,18},{4,20},{6,22},{8,24},{10,26},{12,28},{14,30},{16,0},... | collective-permute-start | bytes 786440 | tf_op jit(solution)/shard_map/ppermute | solution.py:107
  62.0 8.3 %collective-permute-start.4 = (bf16[2,2,64,512]{3,2,1,0:T(8,128)(2,1)S(1)}, bf16[2,2,64,512]{3,2,1,0:T(8,128)(2,1)S(1)}, u32[]{:S(2)}, u32[]{:S(2)}) collective-permute-start(bf16[2,2,64,512]{3,2,1,0:T(8,128)(2,1)S(1)} %pad_maximum_fusion.13), channel_id=1, source_target_pairs={{0,24},{2,26},{4,28},{6,30},{8,0},{10,2},{12,4},{14,6},{16,8},{18,... | collective-permute-start | bytes 786440 | tf_op jit(solution)/shard_map/ppermute | solution.py:107
  73.4 18.6 %collective-permute-done.3 = bf16[2,2,64,512]{3,2,1,0:T(8,128)(2,1)S(1)} collective-permute-done((bf16[2,2,64,512]{3,2,1,0:T(8,128)(2,1)S(1)}, bf16[2,2,64,512]{3,2,1,0:T(8,128)(2,1)S(1)}, u32[]{:S(2)}, u32[]{:S(2)}) %collective-permute-start.3) | collective-permute-done | bytes 262176 | tf_op jit(solution)/shard_map/ppermute | solution.py:107
  99.2 25.9 %collective-permute-done.18 = bf16[2,512,128]{2,1,0:T(8,128)(2,1)S(1)} collective-permute-done((bf16[2,512,128]{2,1,0:T(8,128)(2,1)S(1)}, bf16[2,512,128]{2,1,0:T(8,128)(2,1)S(1)}, u32[]{:S(2)}, u32[]{:S(2)}) %collective-permute-start.18) | collective-permute-done | bytes 262176 | tf_op jit(solution)/shard_map/ppermute | solution.py:50
  135.6 7.7 %shard_map.313 = (bf16[2,128,768]{2,1,0:T(8,128)(2,1)S(1)}, f32[2,1,128]{2,1,0:T(1,128)}) custom-call(bf16[2,16,1024]{2,1,0:T(8,128)(2,1)S(1)} %collective-permute-done.10.edge_ref, bf16[1024,1024]{1,0:T(8,128)(2,1)S(1)} %convolution_convert_fusion.5.before_ref.block_ref, bf16[1024,1024]{1,0:T(8,128)(2,1)S(1)} %convolution_convert_fusion.5.before_ref.block_ref, ...), custom_call_target="tpu_custom_call" | custom-call | flops 201326592 | bytes 2359296 | tf_op jit(solution)/shard_map/pallas_call | solution.py:792
  151.4 12.2 %collective-permute-done.16.incoming_ref = bf16[2,128,768]{2,1,0:T(8,128)(2,1)S(1)} collective-permute-done((bf16[2,128,768]{2,1,0:T(8,128)(2,1)S(1)}, bf16[2,128,768]{2,1,0:T(8,128)(2,1)S(1)}, u32[]{:S(2)}, u32[]{:S(2)}) %collective-permute-start.16) | collective-permute-done | bytes 393248 | tf_op jit(solution)/shard_map/ppermute | solution.py:29
  163.6 17.2 %shard_map.314 = (f32[1024,768]{1,0:T(8,128)}, f32[1024,768]{1,0:T(8,128)}, f32[1024,1]{1,0:T(8,128)S(1)}, bf16[2,4,128,768]{3,2,1,0:T(8,128)(2,1)S(1)}, bf16[2,4,128,768]{3,2,1,0:T(8,128)(2,1)S(1)}) custom-call(bf16[2,16,1024]{2,1,0:T(8,128)(2,1)S(1)} %collective-permute-done.10.edge_ref, bf16[1024,1024]{1,0:T(8,128)(2,1)} %copy-done, ...), custom_call_target="tpu_custom_call" | custom-call | flops 805306368 | bytes 14155776 | tf_op jit(solution)/shard_map/pallas_call | solution.py:809
  181.9 14.6 %shard_map.316 = (bf16[1024,256]{1,0:T(8,128)(2,1)S(1)}, f32[2,8,512]{2,1,0:T(8,128)S(1)}) custom-call(s32[1]{0:T(128)} %bitcast.41.start_ref, bf16[1024,256]{1,0:T(8,128)(2,1)S(1)} %get-tuple-element.62.query_ref, bf16[2,1024,128]{2,1,0:T(8,128)(2,1)S(1)} %pad_maximum_fusion.11.pair_ref), custom_call_target="tpu_custom_call" | custom-call | flops 2147483648 | bytes 3145728 | tf_op jit(solution)/shard_map/pallas_call | solution.py:380
  203.5 6.2 %fusion.31 = f32[1024,1024]{1,0:T(8,128)} fusion(bf16[1024,1024]{1,0:T(8,128)(2,1)S(1)} %bitcast.363, bf16[1024,4096]{1,0:T(8,128)(2,1)} %all-gather.2.cloned.1.call-done), kind=kOutput, calls=%fused_computation.66 | convolution fusion | flops 2147483648 | bytes 8388608 | tf_op jit(solution)/shard_map/dot_general | solution.py:229
  219.1 7.1 %fusion.4 = (bf16[1024,1024]{0,1:T(8,128)(2,1)S(1)}, bf16[1024,1024]{0,1:T(8,128)(2,1)S(1)}, bf16[1024,1024]{0,1:T(8,128)(2,1)}) fusion(f32[1024,1024]{1,0:T(8,128)S(1)} %copy-done.47, f32[1024,1024]{0,1:T(8,128)S(1)} %fusion.26, bf16[1024,1024]{1,0:T(8,128)(2,1)S(1)} %multiply_convert_fusion.1, bf16[1024,4096]{1,0:T(8,128)(2,1)} %all-gather.2.cloned.1.call-done), kind=kOutput, calls=%fused_computation.8 | convolution fusion | flops 2163212288 | bytes 18874368 | tf_op jit(solution)/shard_map/dot_general | solution.py:229
  226.2 14.9 %convolution_convert_fusion.2 = bf16[1024,2048]{1,0:T(8,128)(2,1)S(1)} fusion(bf16[1024,1024]{1,0:T(8,128)(2,1)S(1)} %multiply_convert_fusion.1, bf16[1024,1024]{0,1:T(8,128)(2,1)S(1)} %get-tuple-element.185, bf16[1024,1024]{0,1:T(8,128)(2,1)S(1)} %get-tuple-element.184), kind=kOutput, calls=%fused_computation.39 | convolution fusion | flops 4305453056 | bytes 10485760 | tf_op jit(solution)/shard_map/dot_general | solution.py:237
  252.0 10.0 %fusion = f32[1024,1024]{1,0:T(8,128)} fusion(bf16[1024,2048]{0,1:T(8,128)(2,1)} %pad_maximum_fusion.1, bf16[1024,4096]{1,0:T(8,128)(2,1)} %all-gather.2.cloned.1.call-done), kind=kOutput, calls=%fused_computation.1 | convolution fusion | flops 4294967296 | bytes 12582912 | tf_op jit(solution)/shard_map/dot_general | solution.py:233
  274.9 5.1 multiply_reduce_fusion
  280.0 5.6 %fusion.101 = (bf16[1024,1024]{1,0:T(8,128)(2,1)S(1)}, f32[1024,1024]{1,0:T(8,128)}) fusion(f32[1024]{0:T(1024)S(1)} %broadcast_multiply_fusion.2, f32[1024,1024]{1,0:T(8,128)S(1)} %copy-done.11, f32[1024]{0:T(1024)S(1)} %get-tuple-element.243, f32[1024]{0:T(1024)S(1)} %get-tuple-element.176, f32[1024,1024]{1,0:T(8,128)} %fusion, ...), kind=kLoop, calls=%fused_computation.271 | loop fusion | flops 9437184 | bytes 20987904 | tf_op jit(solution)/shard_map/convert_element_type | solution.py:1059
  296.4 13.1 %collective-permute-start.43 = (f32[4,64]{1,0:T(4,128)S(1)}, f32[4,64]{1,0:T(4,128)S(1)}, u32[]{:S(2)}, u32[]{:S(2)}) collective-permute-start(f32[4,64]{1,0:T(4,128)S(1)} %get-tuple-element.237), channel_id=1, source_target_pairs={{0,24},{2,26},{4,28},{6,30},{8,0},{10,2},{12,4},{14,6},{16,8},{18,... | collective-permute-start | bytes 3080 | tf_op jit(solution)/shard_map/ppermute | solution.py:107
  309.5 6.1 %collective-permute-start.42 = (f32[4,64]{1,0:T(4,128)S(1)}, f32[4,64]{1,0:T(4,128)S(1)}, u32[]{:S(2)}, u32[]{:S(2)}) collective-permute-start(f32[4,64]{1,0:T(4,128)S(1)} %get-tuple-element.238), channel_id=1, source_target_pairs={{0,16},{2,18},{4,20},{6,22},{8,24},{10,26},{12,28},{14,30},{16,0},... | collective-permute-start | bytes 3080 | tf_op jit(solution)/shard_map/ppermute | solution.py:107
  318.2 18.2 %shard_map.317 = (bf16[1024,256]{1,0:T(8,128)(2,1)S(1)}, bf16[2,1024,128]{2,1,0:T(8,128)(2,1)S(1)}) custom-call(s32[1]{0:T(128)} %bitcast.41.start_ref, bf16[1024,256]{1,0:T(8,128)(2,1)S(1)} %copy-done.9, bf16[2,1024,128]{2,1,0:T(8,128)(2,1)S(1)} %copy-done.7, f32[2,8,512]{2,1,0:T(8,128)S(1)} %get-tuple-element.68.total_ref, ...), custom_call_target="tpu_custom_call" | custom-call | flops 5368709120 | bytes 3145728 | tf_op jit(solution)/shard_map/pallas_call | solution.py:380
  341.7 9.9 %shard_map.318 = (bf16[1024,768]{1,0:T(8,128)(2,1)S(1)}, bf16[1024,768]{1,0:T(8,128)(2,1)S(1)}, f32[8,768]{1,0:T(8,128)S(1)}, bf16[2,128,768]{2,1,0:T(8,128)(2,1)S(1)}) custom-call(bf16[2,16,1024]{2,1,0:T(8,128)(2,1)S(1)} %collective-permute-done.10.edge_ref, bf16[1024,1024]{1,0:T(8,128)(2,1)} %copy-done, bf16[1024,1024]{1,0:T(8,128)(2,1)} %copy-done, ...), custom_call_target="tpu_custom_call" | custom-call | flops 201326592 | bytes 15728640 | tf_op jit(solution)/shard_map/pallas_call | solution.py:828
  365.5 17.1 %collective-permute-done.23 = bf16[4,64,1024]{2,1,0:T(8,128)(2,1)S(1)} collective-permute-done((bf16[4,64,1024]{2,1,0:T(8,128)(2,1)S(1)}, bf16[4,64,1024]{2,1,0:T(8,128)(2,1)S(1)}, u32[]{:S(2)}, u32[]{:S(2)}) %collective-permute-start.23) | collective-permute-done | bytes 524320 | tf_op jit(solution)/shard_map/ppermute | solution.py:107
  385.1 30.5 %shard_map.320 = (bf16[1024,1024]{1,0:T(8,128)(2,1)}, bf16[1024,128]{1,0:T(8,128)(2,1)S(1)}, bf16[2,16,1024]{2,1,0:T(8,128)(2,1)S(1)}, f32[8,1024]{1,0:T(8,128)S...) custom-call(bf16[2,16,1024]{2,1,0:T(8,128)(2,1)S(1)} %collective-permute-done.10.edge_ref, bf16[1024,1024]{1,0:T(8,128)(2,1)} %copy-done, ...), custom_call_target="tpu_custom_call" | custom-call | flops 1811939328 | bytes 12582912 | tf_op jit(solution)/shard_map/pallas_call | solution.py:851
  444.8 5.2 convolution_convert_fusion
  458.0 5.7 %collective-permute-done.32 = bf16[4,2,64,512]{3,2,1,0:T(8,128)(2,1)S(1)} collective-permute-done((bf16[4,2,64,512]{3,2,1,0:T(8,128)(2,1)S(1)}, bf16[4,2,64,512]{3,2,1,0:T(8,128)(2,1)S(1)}, u32[]{:S(2)}, u32[]{:S(2)}) %collective-permute-start.32) | collective-permute-done | bytes 524320 | tf_op jit(solution)/shard_map/ppermute | solution.py:107
  482.9 9.3 %collective-permute-done.54 = bf16[4,2,64,640]{3,2,1,0:T(8,128)(2,1)S(1)} collective-permute-done((bf16[4,2,64,640]{3,2,1,0:T(8,128)(2,1)S(1)}, bf16[4,2,64,640]{3,2,1,0:T(8,128)(2,1)S(1)}, u32[]{:S(2)}, u32[]{:S(2)}) %collective-permute-start.54) | collective-permute-done | bytes 655392 | tf_op jit(solution)/shard_map/ppermute | solution.py:107
  534.1 6.9 %fusion.13 = f32[1024,1024]{1,0:T(8,128)} fusion(f32[1024,1024]{1,0:T(8,128)} %get-tuple-element.179, bf16[2,512,1024]{2,1,0:T(8,128)(2,1)S(1)} %copy-done.14, f32[1024]{0:T(1024)S(1)} %broadcast_multiply_fusion.1, f32[1024]{0:T(1024)S(1)} %multiply_multiply_fusion, f32[1024]{0:T(1024)S(1)} %get-tuple-element.177, f32[1024]{0:T(1024)S(1)} %bitcast.382, ...), kind=kLoop, calls=%fused_computation.24 | loop fusion | flops 8388608 | bytes 18890752 | tf_op jit(solution)/shard_map/add | solution.py:1129
  (410 shorter events, 249.2 us)
Async XLA Ops:
  7.2 191.1 %all-gather.2.cloned.1.call-start = ((), (), s32[]{:S(2)}) async-start(), calls=%async_computation.1 | async-start | bytes 8912896 | tf_op jit(solution)/shard_map/all_gather | solution.py:950
  26.2 515.5 %reduce-scatter.2.cloned.1.call-start = ((), (), s32[]{:S(2)}) async-start(), calls=%async_computation.2 | async-start | bytes 6684672 | tf_op jit(solution)/shard_map/reduce_scatter | solution.py:1055
  37.3 24.7 %collective-permute-start.13 = (bf16[2,64,768]{2,1,0:T(8,128)(2,1)S(1)}, bf16[2,64,768]{2,1,0:T(8,128)(2,1)S(1)}, u32[]{:S(2)}, u32[]{:S(2)}) collective-permute-start(bf16[2,64,768]{2,1,0:T(8,128)(2,1)S(1)} %pad_maximum_fusion.17), channel_id=1, source_target_pairs={{0,16},{2,18},{4,20},{6,22},{8,24},{10,26},{12,28},{14,30},{16,0},... | collective-permute-start | bytes 589832 | tf_op jit(solution)/shard_map/ppermute | solution.py:107
  39.6 30.8 %collective-permute-start.14 = (bf16[2,64,768]{2,1,0:T(8,128)(2,1)S(1)}, bf16[2,64,768]{2,1,0:T(8,128)(2,1)S(1)}, u32[]{:S(2)}, u32[]{:S(2)}) collective-permute-start(bf16[2,64,768]{2,1,0:T(8,128)(2,1)S(1)} %pad_maximum_fusion.17), channel_id=1, source_target_pairs={{0,24},{2,26},{4,28},{6,30},{8,0},{10,2},{12,4},{14,6},{16,8},{18,... | collective-permute-start | bytes 589832 | tf_op jit(solution)/shard_map/ppermute | solution.py:107
  40.1 52.9 %collective-permute-start.8 = (bf16[4,64,1024]{2,1,0:T(8,128)(2,1)}, bf16[4,64,1024]{2,1,0:T(8,128)(2,1)S(1)}, u32[]{:S(2)}, u32[]{:S(2)}) collective-permute-start(bf16[4,64,1024]{2,1,0:T(8,128)(2,1)} %bitcast_dynamic-update-slice_fusion.8), channel_id=1, source_target_pairs={{0,4},{2,6},{4,0},{6,2},{8,12},{10,14},{12,8},{14,10},{16,20},{18,... | collective-permute-start | bytes 1572872 | tf_op jit(solution)/shard_map/ppermute | solution.py:107
  41.6 31.8 %collective-permute-start.2 = (bf16[2,2,64,512]{3,2,1,0:T(8,128)(2,1)S(1)}, bf16[2,2,64,512]{3,2,1,0:T(8,128)(2,1)S(1)}, u32[]{:S(2)}, u32[]{:S(2)}) collective-permute-start(bf16[2,2,64,512]{3,2,1,0:T(8,128)(2,1)S(1)} %pad_maximum_fusion.13), channel_id=1, source_target_pairs={{0,8},{2,10},{4,12},{6,14},{8,16},{10,18},{12,20},{14,22},{16,24},... | collective-permute-start | bytes 786440 | tf_op jit(solution)/shard_map/ppermute | solution.py:107
  47.8 44.2 %collective-permute-start.3 = (bf16[2,2,64,512]{3,2,1,0:T(8,128)(2,1)S(1)}, bf16[2,2,64,512]{3,2,1,0:T(8,128)(2,1)S(1)}, u32[]{:S(2)}, u32[]{:S(2)}) collective-permute-start(bf16[2,2,64,512]{3,2,1,0:T(8,128)(2,1)S(1)} %pad_maximum_fusion.13), channel_id=1, source_target_pairs={{0,16},{2,18},{4,20},{6,22},{8,24},{10,26},{12,28},{14,30},{16,0},... | collective-permute-start | bytes 786440 | tf_op jit(solution)/shard_map/ppermute | solution.py:107
  62.0 30.0 %collective-permute-start.4 = (bf16[2,2,64,512]{3,2,1,0:T(8,128)(2,1)S(1)}, bf16[2,2,64,512]{3,2,1,0:T(8,128)(2,1)S(1)}, u32[]{:S(2)}, u32[]{:S(2)}) collective-permute-start(bf16[2,2,64,512]{3,2,1,0:T(8,128)(2,1)S(1)} %pad_maximum_fusion.13), channel_id=1, source_target_pairs={{0,24},{2,26},{4,28},{6,30},{8,0},{10,2},{12,4},{14,6},{16,8},{18,... | collective-permute-start | bytes 786440 | tf_op jit(solution)/shard_map/ppermute | solution.py:107
  70.4 54.8 %collective-permute-start.15 = (bf16[4,2,64,768]{3,2,1,0:T(8,128)(2,1)S(1)}, bf16[4,2,64,768]{3,2,1,0:T(8,128)(2,1)S(1)}, u32[]{:S(2)}, u32[]{:S(2)}) collective-permute-start(bf16[4,2,64,768]{3,2,1,0:T(8,128)(2,1)S(1)} %bitcast_dynamic-update-slice_fusion.4), channel_id=1, source_target_pairs={{0,4},{2,6},{4,0},{6,2},{8,12},{10,14},{12,8},{14,10},{16,20},{18,... | collective-permute-start | bytes 2359304 | tf_op jit(solution)/shard_map/ppermute | solution.py:107
  94.2 31.1 %collective-permute-start.9 = (bf16[4,2,64,1024]{3,2,1,0:T(8,128)(2,1)S(1)}, bf16[4,2,64,1024]{3,2,1,0:T(8,128)(2,1)S(1)}, u32[]{:S(2)}, u32[]{:S(2)}) collective-permute-start(bf16[4,2,64,1024]{3,2,1,0:T(8,128)(2,1)S(1)} %pad_maximum_fusion.8), channel_id=1, source_target_pairs={{0,2},{2,0},{4,6},{6,4},{8,10},{10,8},{12,14},{14,12},{16,18},{18,... | collective-permute-start | bytes 3145736 | tf_op jit(solution)/shard_map/ppermute | solution.py:107
  98.7 26.4 %collective-permute-start.18 = (bf16[2,512,128]{2,1,0:T(8,128)(2,1)S(1)}, bf16[2,512,128]{2,1,0:T(8,128)(2,1)S(1)}, u32[]{:S(2)}, u32[]{:S(2)}) collective-permute-start(bf16[2,512,128]{2,1,0:T(8,128)(2,1)S(1)} %bitcast.351), channel_id=1, source_target_pairs={{0,2},{2,0},{1,3},{3,1},{4,6},{6,4},{5,7},{7,5},{8,10},{10,8},{9,1... | collective-permute-start | bytes 786440 | tf_op jit(solution)/shard_map/ppermute | solution.py:50
  143.3 20.3 %collective-permute-start.16 = (bf16[2,128,768]{2,1,0:T(8,128)(2,1)S(1)}, bf16[2,128,768]{2,1,0:T(8,128)(2,1)S(1)}, u32[]{:S(2)}, u32[]{:S(2)}) collective-permute-start(bf16[2,128,768]{2,1,0:T(8,128)(2,1)S(1)} %get-tuple-element.59), channel_id=1, source_target_pairs={{0,2},{1,3},{4,6},{5,7},{8,10},{9,11},{12,14},{13,15},{16,18},{17,... | collective-permute-start | bytes 1179656 | tf_op jit(solution)/shard_map/ppermute | solution.py:29
  289.4 47.0 %collective-permute-start.22 = (bf16[4,2,64,1024]{3,2,0,1:T(8,128)(2,1)}, bf16[4,2,64,1024]{3,2,0,1:T(8,128)(2,1)}, u32[]{:S(2)}, u32[]{:S(2)}) collective-permute-start(bf16[4,2,64,1024]{3,2,0,1:T(8,128)(2,1)} %bitcast.347), channel_id=1, source_target_pairs={{0,4},{2,6},{4,0},{6,2},{8,12},{10,14},{12,8},{14,10},{16,20},{18,... | collective-permute-start | bytes 3145736 | tf_op jit(solution)/shard_map/ppermute | solution.py:107
  296.3 44.2 %collective-permute-start.24 = (f32[1024,1]{1,0:T(8,128)}, f32[1024,1]{1,0:T(8,128)}, u32[]{:S(2)}, u32[]{:S(2)}) collective-permute-start(f32[1024,1]{1,0:T(8,128)} %copy.110), channel_id=1, source_target_pairs={{0,1},{1,0},{2,3},{3,2},{4,5},{5,4},{6,7},{7,6},{8,9},{9,8},{10,11... | collective-permute-start | bytes 12296 | tf_op jit(solution)/shard_map/ppermute | solution.py:38
  296.4 44.0 %collective-permute-start.43 = (f32[4,64]{1,0:T(4,128)S(1)}, f32[4,64]{1,0:T(4,128)S(1)}, u32[]{:S(2)}, u32[]{:S(2)}) collective-permute-start(f32[4,64]{1,0:T(4,128)S(1)} %get-tuple-element.237), channel_id=1, source_target_pairs={{0,24},{2,26},{4,28},{6,30},{8,0},{10,2},{12,4},{14,6},{16,8},{18,... | collective-permute-start | bytes 3080 | tf_op jit(solution)/shard_map/ppermute | solution.py:107
  309.5 30.9 %collective-permute-start.42 = (f32[4,64]{1,0:T(4,128)S(1)}, f32[4,64]{1,0:T(4,128)S(1)}, u32[]{:S(2)}, u32[]{:S(2)}) collective-permute-start(f32[4,64]{1,0:T(4,128)S(1)} %get-tuple-element.238), channel_id=1, source_target_pairs={{0,16},{2,18},{4,20},{6,22},{8,24},{10,26},{12,28},{14,30},{16,0},... | collective-permute-start | bytes 3080 | tf_op jit(solution)/shard_map/ppermute | solution.py:107
  315.7 24.8 %collective-permute-start.41 = (f32[4,64]{1,0:T(4,128)S(1)}, f32[4,64]{1,0:T(4,128)S(1)}, u32[]{:S(2)}, u32[]{:S(2)}) collective-permute-start(f32[4,64]{1,0:T(4,128)S(1)} %get-tuple-element.236), channel_id=1, source_target_pairs={{0,8},{2,10},{4,12},{6,14},{8,16},{10,18},{12,20},{14,22},{16,24},... | collective-permute-start | bytes 3080 | tf_op jit(solution)/shard_map/ppermute | solution.py:107
  351.6 32.5 %collective-permute-start.30 = (bf16[2,128,768]{2,1,0:T(8,128)(2,1)S(1)}, bf16[2,128,768]{2,1,0:T(8,128)(2,1)S(1)}, u32[]{:S(2)}, u32[]{:S(2)}) collective-permute-start(bf16[2,128,768]{2,1,0:T(8,128)(2,1)S(1)} %get-tuple-element.79), channel_id=1, source_target_pairs={{2,0},{3,1},{6,4},{7,5},{10,8},{11,9},{14,12},{15,13},{18,16},{19,... | collective-permute-start | bytes 1179656 | tf_op jit(solution)/shard_map/ppermute | solution.py:29
  353.6 29.0 %collective-permute-start.23 = (bf16[4,64,1024]{2,1,0:T(8,128)(2,1)S(1)}, bf16[4,64,1024]{2,1,0:T(8,128)(2,1)S(1)}, u32[]{:S(2)}, u32[]{:S(2)}) collective-permute-start(bf16[4,64,1024]{2,1,0:T(8,128)(2,1)S(1)} %dynamic-slice_bitcast_fusion.3), channel_id=1, source_target_pairs={{0,2},{2,0},{4,6},{6,4},{8,10},{10,8},{12,14},{14,12},{16,18},{18,... | collective-permute-start | bytes 1572872 | tf_op jit(solution)/shard_map/ppermute | solution.py:107
  384.1 55.9 %collective-permute-start.26 = (bf16[4,2,64,1152]{3,2,0,1:T(8,128)(2,1)}, bf16[4,2,64,1152]{3,2,0,1:T(8,128)(2,1)}, u32[]{:S(2)}, u32[]{:S(2)}) collective-permute-start(bf16[4,2,64,1152]{3,2,0,1:T(8,128)(2,1)} %bitcast.346), channel_id=1, source_target_pairs={{0,2},{2,0},{4,6},{6,4},{8,10},{10,8},{12,14},{14,12},{16,18},{18,... | collective-permute-start | bytes 3538952 | tf_op jit(solution)/shard_map/ppermute | solution.py:107
  417.9 19.7 %collective-permute-start.29 = (bf16[64,1024]{1,0:T(8,128)(2,1)S(1)}, bf16[64,1024]{1,0:T(8,128)(2,1)S(1)}, u32[]{:S(2)}, u32[]{:S(2)}) collective-permute-start(bf16[64,1024]{1,0:T(8,128)(2,1)S(1)} %get-tuple-element.202), channel_id=1, source_target_pairs={{0,24},{2,26},{4,28},{6,30},{8,0},{10,2},{12,4},{14,6},{16,8},{18,... | collective-permute-start | bytes 393224 | tf_op jit(solution)/shard_map/ppermute | solution.py:107
  420.9 18.3 %collective-permute-start.28 = (bf16[64,1024]{1,0:T(8,128)(2,1)S(1)}, bf16[64,1024]{1,0:T(8,128)(2,1)S(1)}, u32[]{:S(2)}, u32[]{:S(2)}) collective-permute-start(bf16[64,1024]{1,0:T(8,128)(2,1)S(1)} %get-tuple-element.203), channel_id=1, source_target_pairs={{0,16},{2,18},{4,20},{6,22},{8,24},{10,26},{12,28},{14,30},{16,0},... | collective-permute-start | bytes 393224 | tf_op jit(solution)/shard_map/ppermute | solution.py:107
  433.4 36.6 %collective-permute-start.63 = (f32[48,128]{1,0:T(8,128)S(1)}, f32[48,128]{1,0:T(8,128)}, u32[]{:S(2)}, u32[]{:S(2)}) collective-permute-start(f32[48,128]{1,0:T(8,128)S(1)} %fusion.132), channel_id=1, source_target_pairs={{0,16},{4,20},{8,24},{12,28},{16,0},{20,4},{24,8},{28,12},{1,17},{... | collective-permute-start | bytes 73736 | tf_op jit(solution)/shard_map/ppermute | solution.py:38
  466.3 53.2 %collective-permute-start.34 = (f32[1024,1024]{1,0:T(8,128)}, f32[1024,1024]{1,0:T(8,128)}, u32[]{:S(2)}, u32[]{:S(2)}) collective-permute-start(f32[1024,1024]{1,0:T(8,128)} %add_add_fusion), channel_id=1, source_target_pairs={{0,1},{1,0},{2,3},{3,2},{4,5},{5,4},{6,7},{7,6},{8,9},{9,8},{10,11... | collective-permute-start | bytes 12582920 | tf_op jit(solution)/shard_map/ppermute | solution.py:38
  (92 other events, 858.9 us)
Sparse Core Ops, SparseCore 0:
  26.3 158.9 all-gather.1
  268.9 186.1 reduce-scatter.1

commit v4 on v3

--- a/solution.py
+++ b/solution.py
@@ -1046,7 +1046,8 @@
     both_grads = jnp.concatenate([gate_grad, up_grad], axis=1)
     feed_grads = jnp.concatenate(
         [
-            t_dot(normed_two, both_grads).astype(jnp.bfloat16),
+            t_dot(normed_two, gate_grad).astype(jnp.bfloat16),
+            t_dot(normed_two, up_grad).astype(jnp.bfloat16),
             t_dot(cotangent, act_low).astype(jnp.bfloat16),
         ],
         axis=1,

time: 563 us -> 565 us (level)
  matrix products: 90.7 us -> 80.2 us
  local copies, waits for them, and re-layouts: 32 us -> 41.3 us
    unnamed x103 -> x111, local copies, waits for them, and re-layouts: 8.58 us -> 20.1 us
    dot_general x5 -> x6, matrix products: 29.4 us -> 19.4 us  [t_dot(): lax.dot_general(a, b, (((0,), (0,)), ((), ())), preferred_element_type=jn...]
    concatenate x1, other arithmetic: 4.74 us -> 13.4 us  [shards(): jnp.concatenate([t_dot(normed_two, gate_grad).astype(jnp.bfloat16), t_dot...]
  transfers between devices with their start and end apart: 67 -> 67, of which waited for: 26 -> 29; matrix products, arithmetic and copies ran while one was open for 20% -> 22% of each run, Pallas kernels for 18% -> 18%
where the time goes in v4:
time: 565 us; the launch traced here: 555 us
  waiting for transfers between devices  135 us (24%)
  starting transfers between devices  118 us (21%)
  Pallas kernels  101 us (18%)
  matrix products  80.2 us (14%)
  other arithmetic  64.3 us (11%)
  local copies, waits for them, and re-layouts  41.3 us (7%)
  between operations  15.8 us (3%)
    ppermute x41, starting transfers between devices, across(): return lax.ppermute(value, WEIGHT_AXES, torus_route(step))  85.1 us
    ppermute x41, waiting for transfers between devices, across(): return lax.ppermute(value, WEIGHT_AXES, torus_route(step))  81.2 us
    pallas_call x4, Pallas kernels, call(): tall(kernel, (self.seqs, self.tiles), [specs[name] for name in ins], [spe...  35.6 us
    dot_general x8, matrix products, dot(): return jnp.dot(a, b, preferred_element_type=jnp.float32)  35 us
    pallas_call x1, Pallas kernels, backward(): tall(functools.partial(backward_kernel, self.pairs, last), self.grid, [*s...  30.5 us
    ppermute x1, waiting for transfers between devices, gather_ctx(): other = lax.ppermute(block, 'ctx', [(0, 1), (1, 0)])  25.8 us
    dot_general x7, matrix products, dot_t(): lax.dot_general(a, b, (((1,), (1,)), ((), ())), preferred_element_type=jn...  25.7 us
    unnamed x111, local copies, waits for them, and re-layouts  20.1 us
  transfers between devices with their start and end apart: 67, of which 29 were waited for; matrix products, arithmetic and copies ran while one was open for 22% of the time, Pallas kernels for 18%

profile of v4, /device:TPU:0, one launch (start us, length us, event | category | flops | bytes accessed | tf_op | source)
XLA Modules:
  0.0 555.4 jit_solution(10022874591356334300)
XLA Ops:
  47.3 12.7 %collective-permute-start.3 = (bf16[2,2,64,512]{3,2,1,0:T(8,128)(2,1)S(1)}, bf16[2,2,64,512]{3,2,1,0:T(8,128)(2,1)S(1)}, u32[]{:S(2)}, u32[]{:S(2)}) collective-permute-start(bf16[2,2,64,512]{3,2,1,0:T(8,128)(2,1)S(1)} %pad_maximum_fusion.13), channel_id=1, source_target_pairs={{0,16},{2,18},{4,20},{6,22},{8,24},{10,26},{12,28},{14,30},{16,0},... | collective-permute-start | bytes 786440 | tf_op jit(solution)/shard_map/ppermute | solution.py:107
  61.3 8.3 %collective-permute-start.4 = (bf16[2,2,64,512]{3,2,1,0:T(8,128)(2,1)S(1)}, bf16[2,2,64,512]{3,2,1,0:T(8,128)(2,1)S(1)}, u32[]{:S(2)}, u32[]{:S(2)}) collective-permute-start(bf16[2,2,64,512]{3,2,1,0:T(8,128)(2,1)S(1)} %pad_maximum_fusion.13), channel_id=1, source_target_pairs={{0,24},{2,26},{4,28},{6,30},{8,0},{10,2},{12,4},{14,6},{16,8},{18,... | collective-permute-start | bytes 786440 | tf_op jit(solution)/shard_map/ppermute | solution.py:107
  72.7 18.6 %collective-permute-done.3 = bf16[2,2,64,512]{3,2,1,0:T(8,128)(2,1)S(1)} collective-permute-done((bf16[2,2,64,512]{3,2,1,0:T(8,128)(2,1)S(1)}, bf16[2,2,64,512]{3,2,1,0:T(8,128)(2,1)S(1)}, u32[]{:S(2)}, u32[]{:S(2)}) %collective-permute-start.3) | collective-permute-done | bytes 262176 | tf_op jit(solution)/shard_map/ppermute | solution.py:107
  98.6 25.8 %collective-permute-done.18 = bf16[2,512,128]{2,1,0:T(8,128)(2,1)S(1)} collective-permute-done((bf16[2,512,128]{2,1,0:T(8,128)(2,1)S(1)}, bf16[2,512,128]{2,1,0:T(8,128)(2,1)S(1)}, u32[]{:S(2)}, u32[]{:S(2)}) %collective-permute-start.18) | collective-permute-done | bytes 262176 | tf_op jit(solution)/shard_map/ppermute | solution.py:50
  134.9 7.7 %shard_map.313 = (bf16[2,128,768]{2,1,0:T(8,128)(2,1)S(1)}, f32[2,1,128]{2,1,0:T(1,128)}) custom-call(bf16[2,16,1024]{2,1,0:T(8,128)(2,1)S(1)} %collective-permute-done.10.edge_ref, bf16[1024,1024]{1,0:T(8,128)(2,1)S(1)} %convolution_convert_fusion.6.before_ref.block_ref, bf16[1024,1024]{1,0:T(8,128)(2,1)S(1)} %convolution_convert_fusion.6.before_ref.block_ref, ...), custom_call_target="tpu_custom_call" | custom-call | flops 201326592 | bytes 2359296 | tf_op jit(solution)/shard_map/pallas_call | solution.py:792
  150.8 12.2 %collective-permute-done.16.incoming_ref = bf16[2,128,768]{2,1,0:T(8,128)(2,1)S(1)} collective-permute-done((bf16[2,128,768]{2,1,0:T(8,128)(2,1)S(1)}, bf16[2,128,768]{2,1,0:T(8,128)(2,1)S(1)}, u32[]{:S(2)}, u32[]{:S(2)}) %collective-permute-start.16) | collective-permute-done | bytes 393248 | tf_op jit(solution)/shard_map/ppermute | solution.py:29
  162.9 17.2 %shard_map.314 = (f32[1024,768]{1,0:T(8,128)}, f32[1024,768]{1,0:T(8,128)}, f32[1024,1]{1,0:T(8,128)S(1)}, bf16[2,4,128,768]{3,2,1,0:T(8,128)(2,1)S(1)}, bf16[2,4,128,768]{3,2,1,0:T(8,128)(2,1)S(1)}) custom-call(bf16[2,16,1024]{2,1,0:T(8,128)(2,1)S(1)} %collective-permute-done.10.edge_ref, bf16[1024,1024]{1,0:T(8,128)(2,1)} %copy-done, ...), custom_call_target="tpu_custom_call" | custom-call | flops 805306368 | bytes 14155776 | tf_op jit(solution)/shard_map/pallas_call | solution.py:809
  181.3 15.0 %shard_map.316 = (bf16[1024,256]{1,0:T(8,128)(2,1)S(1)}, f32[2,8,512]{2,1,0:T(8,128)S(1)}) custom-call(s32[1]{0:T(128)} %bitcast.41.start_ref, bf16[1024,256]{1,0:T(8,128)(2,1)S(1)} %get-tuple-element.62.query_ref, bf16[2,1024,128]{2,1,0:T(8,128)(2,1)S(1)} %pad_maximum_fusion.11.pair_ref), custom_call_target="tpu_custom_call" | custom-call | flops 2147483648 | bytes 3145728 | tf_op jit(solution)/shard_map/pallas_call | solution.py:380
  203.2 6.2 %fusion.31 = f32[1024,1024]{1,0:T(8,128)} fusion(bf16[1024,1024]{1,0:T(8,128)(2,1)S(1)} %bitcast.369, bf16[1024,4096]{1,0:T(8,128)(2,1)} %all-gather.2.cloned.1.call-done), kind=kOutput, calls=%fused_computation.67 | convolution fusion | flops 2147483648 | bytes 8388608 | tf_op jit(solution)/shard_map/dot_general | solution.py:229
  214.7 6.7 %fusion.26 = f32[1024,1024]{0,1:T(8,128)} fusion(bf16[1024,1024]{1,0:T(8,128)(2,1)S(1)} %multiply_convert_fusion.1, bf16[1024,4096]{1,0:T(8,128)(2,1)} %all-gather.2.cloned.1.call-done), kind=kOutput, calls=%fused_computation.51 | convolution fusion | flops 2147483648 | bytes 8388608 | tf_op jit(solution)/shard_map/dot_general | solution.py:229
  221.4 7.6 %fusion.4 = (bf16[1024,1024]{0,1:T(8,128)(2,1)S(1)}, bf16[1024,1024]{0,1:T(8,128)(2,1)S(1)}, bf16[1024,1024]{0,1:T(8,128)(2,1)}) fusion(f32[1024,1024]{1,0:T(8,128)} %fusion.31, f32[1024,1024]{0,1:T(8,128)} %fusion.26, bf16[1024,1024]{1,0:T(8,128)(2,1)S(1)} %multiply_convert_fusion.1, bf16[1024,4096]{1,0:T(8,128)(2,1)S(1)} %bitcast.403), kind=kOutput, calls=%fused_computation.8 | convolution fusion | flops 2163212288 | bytes 18874368 | tf_op jit(solution)/shard_map/dot_general | solution.py:229
  238.2 13.4 %pad_maximum_fusion = bf16[1024,3072]{0,1:T(8,128)(2,1)} fusion(bf16[1024,1024]{0,1:T(8,128)(2,1)S(1)} %convert_bitcast_fusion, bf16[1024,1024]{0,1:T(8,128)(2,1)S(1)} %convolution_convert_fusion.2, bf16[1024,1024]{0,1:T(8,128)(2,1)S(1)} %convolution_convert_fusion.3), kind=kLoop, calls=%fused_computation | loop fusion | flops 18874368 | bytes 12582912 | tf_op jit(solution)/shard_map/concatenate | solution.py:1047
  251.6 6.3 %fusion = f32[1024,1024]{1,0:T(8,128)} fusion(bf16[1024,2048]{0,1:T(8,128)(2,1)S(1)} %pad_maximum_fusion.1, bf16[1024,4096]{1,0:T(8,128)(2,1)S(1)} %bitcast.403), kind=kOutput, calls=%fused_computation.1 | convolution fusion | flops 4294967296 | bytes 12582912 | tf_op jit(solution)/shard_map/dot_general | solution.py:233
  264.6 8.7 %copy.123 = bf16[1024,3072]{1,0:T(8,128)(2,1)} copy(bf16[1024,3072]{0,1:T(8,128)(2,1)} %pad_maximum_fusion) | data formatting | bytes 12582912
  282.0 6.0 %fusion.101 = (bf16[1024,1024]{1,0:T(8,128)(2,1)S(1)}, f32[1024,1024]{1,0:T(8,128)}) fusion(f32[1024]{0:T(1024)S(1)} %broadcast_multiply_fusion.2, f32[1024,1024]{1,0:T(8,128)S(1)} %copy-done.11, f32[1024]{0:T(1024)S(1)} %get-tuple-element.243, f32[1024]{0:T(1024)S(1)} %get-tuple-element.176, f32[1024,1024]{1,0:T(8,128)} %fusion, ...), kind=kLoop, calls=%fused_computation.272 | loop fusion | flops 9437184 | bytes 20987904 | tf_op jit(solution)/shard_map/convert_element_type | solution.py:1060
  299.1 13.1 %collective-permute-start.43 = (f32[4,64]{1,0:T(4,128)S(1)}, f32[4,64]{1,0:T(4,128)S(1)}, u32[]{:S(2)}, u32[]{:S(2)}) collective-permute-start(f32[4,64]{1,0:T(4,128)S(1)} %get-tuple-element.237), channel_id=1, source_target_pairs={{0,24},{2,26},{4,28},{6,30},{8,0},{10,2},{12,4},{14,6},{16,8},{18,... | collective-permute-start | bytes 3080 | tf_op jit(solution)/shard_map/ppermute | solution.py:107
  312.2 5.4 collective-permute-start.42
  320.1 18.2 %shard_map.317 = (bf16[1024,256]{1,0:T(8,128)(2,1)S(1)}, bf16[2,1024,128]{2,1,0:T(8,128)(2,1)S(1)}) custom-call(s32[1]{0:T(128)} %bitcast.41.start_ref, bf16[1024,256]{1,0:T(8,128)(2,1)S(1)} %copy-done.9, bf16[2,1024,128]{2,1,0:T(8,128)(2,1)S(1)} %copy-done.7, f32[2,8,512]{2,1,0:T(8,128)S(1)} %get-tuple-element.68.total_ref, ...), custom_call_target="tpu_custom_call" | custom-call | flops 5368709120 | bytes 3145728 | tf_op jit(solution)/shard_map/pallas_call | solution.py:380
  344.2 9.9 %shard_map.318 = (bf16[1024,768]{1,0:T(8,128)(2,1)S(1)}, bf16[1024,768]{1,0:T(8,128)(2,1)S(1)}, f32[8,768]{1,0:T(8,128)S(1)}, bf16[2,128,768]{2,1,0:T(8,128)(2,1)S(1)}) custom-call(bf16[2,16,1024]{2,1,0:T(8,128)(2,1)S(1)} %collective-permute-done.10.edge_ref, bf16[1024,1024]{1,0:T(8,128)(2,1)} %copy-done, bf16[1024,1024]{1,0:T(8,128)(2,1)} %copy-done, ...), custom_call_target="tpu_custom_call" | custom-call | flops 201326592 | bytes 15728640 | tf_op jit(solution)/shard_map/pallas_call | solution.py:828
  367.7 17.4 %collective-permute-done.23 = bf16[4,64,1024]{2,1,0:T(8,128)(2,1)S(1)} collective-permute-done((bf16[4,64,1024]{2,1,0:T(8,128)(2,1)S(1)}, bf16[4,64,1024]{2,1,0:T(8,128)(2,1)S(1)}, u32[]{:S(2)}, u32[]{:S(2)}) %collective-permute-start.23) | collective-permute-done | bytes 524320 | tf_op jit(solution)/shard_map/ppermute | solution.py:107
  388.6 30.5 %shard_map.320 = (bf16[1024,1024]{1,0:T(8,128)(2,1)}, bf16[1024,128]{1,0:T(8,128)(2,1)S(1)}, bf16[2,16,1024]{2,1,0:T(8,128)(2,1)S(1)}, f32[8,1024]{1,0:T(8,128)S...) custom-call(bf16[2,16,1024]{2,1,0:T(8,128)(2,1)S(1)} %collective-permute-done.10.edge_ref, bf16[1024,1024]{1,0:T(8,128)(2,1)} %copy-done, ...), custom_call_target="tpu_custom_call" | custom-call | flops 1811939328 | bytes 12582912 | tf_op jit(solution)/shard_map/pallas_call | solution.py:851
  449.4 5.2 convolution_convert_fusion
  486.9 9.1 %collective-permute-done.54 = bf16[4,2,64,640]{3,2,1,0:T(8,128)(2,1)S(1)} collective-permute-done((bf16[4,2,64,640]{3,2,1,0:T(8,128)(2,1)S(1)}, bf16[4,2,64,640]{3,2,1,0:T(8,128)(2,1)S(1)}, u32[]{:S(2)}, u32[]{:S(2)}) %collective-permute-start.54) | collective-permute-done | bytes 655392 | tf_op jit(solution)/shard_map/ppermute | solution.py:107
  537.1 6.9 %fusion.13 = f32[1024,1024]{1,0:T(8,128)} fusion(f32[1024,1024]{1,0:T(8,128)} %get-tuple-element.179, bf16[2,512,1024]{2,1,0:T(8,128)(2,1)S(1)} %copy-done.14, f32[1024]{0:T(1024)S(1)} %broadcast_multiply_fusion.1, f32[1024]{0:T(1024)S(1)} %multiply_multiply_fusion, f32[1024]{0:T(1024)S(1)} %get-tuple-element.177, f32[1024]{0:T(1024)S(1)} %bitcast.388, ...), kind=kLoop, calls=%fused_computation.24 | loop fusion | flops 8388608 | bytes 18890752 | tf_op jit(solution)/shard_map/add | solution.py:1130
  (419 shorter events, 251.5 us)
Async XLA Ops:
  7.2 190.8 %all-gather.2.cloned.1.call-start = ((), (), s32[]{:S(2)}) async-start(), calls=%async_computation.1 | async-start | bytes 8912896 | tf_op jit(solution)/shard_map/all_gather | solution.py:950
  25.4 519.2 %reduce-scatter.4.cloned.1.call-start = ((), (), s32[]{:S(2)}) async-start(), calls=%async_computation.2 | async-start | bytes 6684672
  36.6 24.7 %collective-permute-start.13 = (bf16[2,64,768]{2,1,0:T(8,128)(2,1)S(1)}, bf16[2,64,768]{2,1,0:T(8,128)(2,1)S(1)}, u32[]{:S(2)}, u32[]{:S(2)}) collective-permute-start(bf16[2,64,768]{2,1,0:T(8,128)(2,1)S(1)} %pad_maximum_fusion.17), channel_id=1, source_target_pairs={{0,16},{2,18},{4,20},{6,22},{8,24},{10,26},{12,28},{14,30},{16,0},... | collective-permute-start | bytes 589832 | tf_op jit(solution)/shard_map/ppermute | solution.py:107
  38.9 30.7 %collective-permute-start.14 = (bf16[2,64,768]{2,1,0:T(8,128)(2,1)S(1)}, bf16[2,64,768]{2,1,0:T(8,128)(2,1)S(1)}, u32[]{:S(2)}, u32[]{:S(2)}) collective-permute-start(bf16[2,64,768]{2,1,0:T(8,128)(2,1)S(1)} %pad_maximum_fusion.17), channel_id=1, source_target_pairs={{0,24},{2,26},{4,28},{6,30},{8,0},{10,2},{12,4},{14,6},{16,8},{18,... | collective-permute-start | bytes 589832 | tf_op jit(solution)/shard_map/ppermute | solution.py:107
  39.5 52.9 %collective-permute-start.8 = (bf16[4,64,1024]{2,1,0:T(8,128)(2,1)}, bf16[4,64,1024]{2,1,0:T(8,128)(2,1)S(1)}, u32[]{:S(2)}, u32[]{:S(2)}) collective-permute-start(bf16[4,64,1024]{2,1,0:T(8,128)(2,1)} %bitcast_dynamic-update-slice_fusion.8), channel_id=1, source_target_pairs={{0,4},{2,6},{4,0},{6,2},{8,12},{10,14},{12,8},{14,10},{16,20},{18,... | collective-permute-start | bytes 1572872 | tf_op jit(solution)/shard_map/ppermute | solution.py:107
  40.8 31.9 %collective-permute-start.2 = (bf16[2,2,64,512]{3,2,1,0:T(8,128)(2,1)S(1)}, bf16[2,2,64,512]{3,2,1,0:T(8,128)(2,1)S(1)}, u32[]{:S(2)}, u32[]{:S(2)}) collective-permute-start(bf16[2,2,64,512]{3,2,1,0:T(8,128)(2,1)S(1)} %pad_maximum_fusion.13), channel_id=1, source_target_pairs={{0,8},{2,10},{4,12},{6,14},{8,16},{10,18},{12,20},{14,22},{16,24},... | collective-permute-start | bytes 786440 | tf_op jit(solution)/shard_map/ppermute | solution.py:107
  47.3 44.1 %collective-permute-start.3 = (bf16[2,2,64,512]{3,2,1,0:T(8,128)(2,1)S(1)}, bf16[2,2,64,512]{3,2,1,0:T(8,128)(2,1)S(1)}, u32[]{:S(2)}, u32[]{:S(2)}) collective-permute-start(bf16[2,2,64,512]{3,2,1,0:T(8,128)(2,1)S(1)} %pad_maximum_fusion.13), channel_id=1, source_target_pairs={{0,16},{2,18},{4,20},{6,22},{8,24},{10,26},{12,28},{14,30},{16,0},... | collective-permute-start | bytes 786440 | tf_op jit(solution)/shard_map/ppermute | solution.py:107
  61.3 30.0 %collective-permute-start.4 = (bf16[2,2,64,512]{3,2,1,0:T(8,128)(2,1)S(1)}, bf16[2,2,64,512]{3,2,1,0:T(8,128)(2,1)S(1)}, u32[]{:S(2)}, u32[]{:S(2)}) collective-permute-start(bf16[2,2,64,512]{3,2,1,0:T(8,128)(2,1)S(1)} %pad_maximum_fusion.13), channel_id=1, source_target_pairs={{0,24},{2,26},{4,28},{6,30},{8,0},{10,2},{12,4},{14,6},{16,8},{18,... | collective-permute-start | bytes 786440 | tf_op jit(solution)/shard_map/ppermute | solution.py:107
  69.7 54.8 %collective-permute-start.15 = (bf16[4,2,64,768]{3,2,1,0:T(8,128)(2,1)S(1)}, bf16[4,2,64,768]{3,2,1,0:T(8,128)(2,1)S(1)}, u32[]{:S(2)}, u32[]{:S(2)}) collective-permute-start(bf16[4,2,64,768]{3,2,1,0:T(8,128)(2,1)S(1)} %bitcast_dynamic-update-slice_fusion.4), channel_id=1, source_target_pairs={{0,4},{2,6},{4,0},{6,2},{8,12},{10,14},{12,8},{14,10},{16,20},{18,... | collective-permute-start | bytes 2359304 | tf_op jit(solution)/shard_map/ppermute | solution.py:107
  93.6 31.0 %collective-permute-start.9 = (bf16[4,2,64,1024]{3,2,1,0:T(8,128)(2,1)S(1)}, bf16[4,2,64,1024]{3,2,1,0:T(8,128)(2,1)S(1)}, u32[]{:S(2)}, u32[]{:S(2)}) collective-permute-start(bf16[4,2,64,1024]{3,2,1,0:T(8,128)(2,1)S(1)} %pad_maximum_fusion.8), channel_id=1, source_target_pairs={{0,2},{2,0},{4,6},{6,4},{8,10},{10,8},{12,14},{14,12},{16,18},{18,... | collective-permute-start | bytes 3145736 | tf_op jit(solution)/shard_map/ppermute | solution.py:107
  98.0 26.4 %collective-permute-start.18 = (bf16[2,512,128]{2,1,0:T(8,128)(2,1)S(1)}, bf16[2,512,128]{2,1,0:T(8,128)(2,1)S(1)}, u32[]{:S(2)}, u32[]{:S(2)}) collective-permute-start(bf16[2,512,128]{2,1,0:T(8,128)(2,1)S(1)} %bitcast.356), channel_id=1, source_target_pairs={{0,2},{2,0},{1,3},{3,1},{4,6},{6,4},{5,7},{7,5},{8,10},{10,8},{9,1... | collective-permute-start | bytes 786440 | tf_op jit(solution)/shard_map/ppermute | solution.py:50
  142.6 20.3 %collective-permute-start.16 = (bf16[2,128,768]{2,1,0:T(8,128)(2,1)S(1)}, bf16[2,128,768]{2,1,0:T(8,128)(2,1)S(1)}, u32[]{:S(2)}, u32[]{:S(2)}) collective-permute-start(bf16[2,128,768]{2,1,0:T(8,128)(2,1)S(1)} %get-tuple-element.59), channel_id=1, source_target_pairs={{0,2},{1,3},{4,6},{5,7},{8,10},{9,11},{12,14},{13,15},{16,18},{17,... | collective-permute-start | bytes 1179656 | tf_op jit(solution)/shard_map/ppermute | solution.py:29
  257.9 19.2 %collective-permute-start.21 = (f32[1024,1024]{1,0:T(8,128)}, f32[1024,1024]{1,0:T(8,128)}, u32[]{:S(2)}, u32[]{:S(2)}) collective-permute-start(f32[1024,1024]{1,0:T(8,128)} %fusion), channel_id=1, source_target_pairs={{0,1},{1,0},{2,3},{3,2},{4,5},{5,4},{6,7},{7,6},{8,9},{9,8},{10,11... | collective-permute-start | bytes 12582920 | tf_op jit(solution)/shard_map/ppermute | solution.py:38
  291.7 46.6 %collective-permute-start.22 = (bf16[4,2,64,1024]{3,2,0,1:T(8,128)(2,1)}, bf16[4,2,64,1024]{3,2,0,1:T(8,128)(2,1)}, u32[]{:S(2)}, u32[]{:S(2)}) collective-permute-start(bf16[4,2,64,1024]{3,2,0,1:T(8,128)(2,1)} %bitcast.352), channel_id=1, source_target_pairs={{0,4},{2,6},{4,0},{6,2},{8,12},{10,14},{12,8},{14,10},{16,20},{18,... | collective-permute-start | bytes 3145736 | tf_op jit(solution)/shard_map/ppermute | solution.py:107
  298.7 44.3 %collective-permute-start.24 = (f32[1024,1]{1,0:T(8,128)}, f32[1024,1]{1,0:T(8,128)}, u32[]{:S(2)}, u32[]{:S(2)}) collective-permute-start(f32[1024,1]{1,0:T(8,128)} %copy.112), channel_id=1, source_target_pairs={{0,1},{1,0},{2,3},{3,2},{4,5},{5,4},{6,7},{7,6},{8,9},{9,8},{10,11... | collective-permute-start | bytes 12296 | tf_op jit(solution)/shard_map/ppermute | solution.py:38
  299.1 43.8 %collective-permute-start.43 = (f32[4,64]{1,0:T(4,128)S(1)}, f32[4,64]{1,0:T(4,128)S(1)}, u32[]{:S(2)}, u32[]{:S(2)}) collective-permute-start(f32[4,64]{1,0:T(4,128)S(1)} %get-tuple-element.237), channel_id=1, source_target_pairs={{0,24},{2,26},{4,28},{6,30},{8,0},{10,2},{12,4},{14,6},{16,8},{18,... | collective-permute-start | bytes 3080 | tf_op jit(solution)/shard_map/ppermute | solution.py:107
  312.2 30.7 %collective-permute-start.42 = (f32[4,64]{1,0:T(4,128)S(1)}, f32[4,64]{1,0:T(4,128)S(1)}, u32[]{:S(2)}, u32[]{:S(2)}) collective-permute-start(f32[4,64]{1,0:T(4,128)S(1)} %get-tuple-element.238), channel_id=1, source_target_pairs={{0,16},{2,18},{4,20},{6,22},{8,24},{10,26},{12,28},{14,30},{16,0},... | collective-permute-start | bytes 3080 | tf_op jit(solution)/shard_map/ppermute | solution.py:107
  317.6 25.3 %collective-permute-start.41 = (f32[4,64]{1,0:T(4,128)S(1)}, f32[4,64]{1,0:T(4,128)S(1)}, u32[]{:S(2)}, u32[]{:S(2)}) collective-permute-start(f32[4,64]{1,0:T(4,128)S(1)} %get-tuple-element.236), channel_id=1, source_target_pairs={{0,8},{2,10},{4,12},{6,14},{8,16},{10,18},{12,20},{14,22},{16,24},... | collective-permute-start | bytes 3080 | tf_op jit(solution)/shard_map/ppermute | solution.py:107
  354.1 33.6 %collective-permute-start.30 = (bf16[2,128,768]{2,1,0:T(8,128)(2,1)S(1)}, bf16[2,128,768]{2,1,0:T(8,128)(2,1)S(1)}, u32[]{:S(2)}, u32[]{:S(2)}) collective-permute-start(bf16[2,128,768]{2,1,0:T(8,128)(2,1)S(1)} %get-tuple-element.79), channel_id=1, source_target_pairs={{2,0},{3,1},{6,4},{7,5},{10,8},{11,9},{14,12},{15,13},{18,16},{19,... | collective-permute-start | bytes 1179656 | tf_op jit(solution)/shard_map/ppermute | solution.py:29
  355.6 29.5 %collective-permute-start.23 = (bf16[4,64,1024]{2,1,0:T(8,128)(2,1)S(1)}, bf16[4,64,1024]{2,1,0:T(8,128)(2,1)S(1)}, u32[]{:S(2)}, u32[]{:S(2)}) collective-permute-start(bf16[4,64,1024]{2,1,0:T(8,128)(2,1)S(1)} %dynamic-slice_bitcast_fusion.3), channel_id=1, source_target_pairs={{0,2},{2,0},{4,6},{6,4},{8,10},{10,8},{12,14},{14,12},{16,18},{18,... | collective-permute-start | bytes 1572872 | tf_op jit(solution)/shard_map/ppermute | solution.py:107
  387.7 56.5 %collective-permute-start.26 = (bf16[4,2,64,1152]{3,2,0,1:T(8,128)(2,1)}, bf16[4,2,64,1152]{3,2,0,1:T(8,128)(2,1)}, u32[]{:S(2)}, u32[]{:S(2)}) collective-permute-start(bf16[4,2,64,1152]{3,2,0,1:T(8,128)(2,1)} %bitcast.351), channel_id=1, source_target_pairs={{0,2},{2,0},{4,6},{6,4},{8,10},{10,8},{12,14},{14,12},{16,18},{18,... | collective-permute-start | bytes 3538952 | tf_op jit(solution)/shard_map/ppermute | solution.py:107
  421.7 20.1 %collective-permute-start.29 = (bf16[64,1024]{1,0:T(8,128)(2,1)S(1)}, bf16[64,1024]{1,0:T(8,128)(2,1)S(1)}, u32[]{:S(2)}, u32[]{:S(2)}) collective-permute-start(bf16[64,1024]{1,0:T(8,128)(2,1)S(1)} %get-tuple-element.202), channel_id=1, source_target_pairs={{0,24},{2,26},{4,28},{6,30},{8,0},{10,2},{12,4},{14,6},{16,8},{18,... | collective-permute-start | bytes 393224 | tf_op jit(solution)/shard_map/ppermute | solution.py:107
  437.5 37.0 %collective-permute-start.63 = (f32[48,128]{1,0:T(8,128)S(1)}, f32[48,128]{1,0:T(8,128)S(1)}, u32[]{:S(2)}, u32[]{:S(2)}) collective-permute-start(f32[48,128]{1,0:T(8,128)S(1)} %fusion.135), channel_id=1, source_target_pairs={{0,16},{4,20},{8,24},{12,28},{16,0},{20,4},{24,8},{28,12},{1,17},{... | collective-permute-start | bytes 73736 | tf_op jit(solution)/shard_map/ppermute | solution.py:38
  470.8 51.7 %collective-permute-start.34 = (f32[1024,1024]{1,0:T(8,128)}, f32[1024,1024]{1,0:T(8,128)}, u32[]{:S(2)}, u32[]{:S(2)}) collective-permute-start(f32[1024,1024]{1,0:T(8,128)} %add_add_fusion), channel_id=1, source_target_pairs={{0,1},{1,0},{2,3},{3,2},{4,5},{5,4},{6,7},{7,6},{8,9},{9,8},{10,11... | collective-permute-start | bytes 12582920 | tf_op jit(solution)/shard_map/ppermute | solution.py:38
  (94 other events, 868.9 us)
Sparse Core Ops, SparseCore 0:
  25.6 158.9 all-gather.1
  273.4 186.1 reduce-scatter.3
